TPU v7x, 32 devices: a whole 2x2x4 slice. The times are simulated.
32 devices in a mesh: expert: 8 (over z, core), group: 4 (over y, x).
Axes of the slice: x: 2, y: 2, z: 4, core: 2. Of those that a mesh axis runs over, the one named last changes fastest.
Arguments:
- tokens_in: bfloat16 [4096, 2048], P(('expert', 'group')), may hold values from -6 to 6
- hidden_grad: bfloat16 [4096, 256], P(('expert', 'group')), may hold values from -3 to 3
- routing: int32 [4096], P(('expert', 'group')), may hold values from 0 to 7, as said below
- gate_up: bfloat16 [8, 2048, 512], P('expert'), may hold values from -0.125 to 0.125
Outputs:
- tokens_grad: bfloat16 [4096, 2048], P(('expert', 'group'))
- gate_up_grad: float32 [8, 2048, 512], P('expert', 'group')
Inputs may be any that keep to these rules, and one draw needn't show every extreme that they name: `routing`: the 128 rows of one device (block b of the rows, b = expert index * 4 + group index) name each expert at most 32 times. Blocks b and b + 2, for b % 4 < 2, together name each expert at most 3 * 32 // 2 times. In every draw both bounds are reached, and some expert receives 32 rows from every block of one group.
All inputs are finite; a program needn't handle non-finite values.
Results may differ from a plain program's by a relative error of at most 0.0049.
Values may be sent and summed in bfloat16 or wider, within the bound.
No kernel may reach another device: no remote copies, remote signals or barrier semaphores. Data moves between devices by JAX's collectives and lax.ppermute only.
A program may use at most 64 MiB of HBM per device.

v0:
```python
import jax
import jax.numpy as jnp
from jax import lax
from jax.sharding import PartitionSpec as P


def expert_backward(work_rows, weights, model_width):
    inputs = work_rows[:, :model_width]
    cotangent = work_rows[:, model_width:].astype(jnp.float32)
    projected = jnp.dot(inputs, weights, preferred_element_type=jnp.float32)
    hidden = weights.shape[1] // 2
    gate_pre = projected[:, :hidden]
    up_pre = projected[:, hidden:]
    sigmoid_gate = jax.nn.sigmoid(gate_pre)
    gate_grad = cotangent * up_pre * sigmoid_gate * (1.0 + gate_pre * (1.0 - sigmoid_gate))
    up_grad = cotangent * gate_pre * sigmoid_gate
    pre_grad = jnp.concatenate([gate_grad, up_grad], axis=1).astype(jnp.bfloat16)
    input_grad = lax.dot_general(
        pre_grad, weights, (((1,), (1,)), ((), ())), preferred_element_type=jnp.float32
    ).astype(jnp.bfloat16)
    return (inputs, pre_grad, input_grad)


def on_device(tokens_in, hidden_grad, routing, gate_up):
    experts = lax.axis_size("expert")
    row_count = routing.shape[0]
    capacity = 2 * row_count // experts
    slot_count = experts * capacity
    model_width = tokens_in.shape[1]
    weights = gate_up[0]
    one_hot = (routing[:, None] == jnp.arange(experts, dtype=jnp.int32)[None, :]).astype(jnp.int32)
    earlier = jnp.cumsum(one_hot, axis=0) - one_hot
    rank_in = jnp.sum(earlier * one_hot, axis=1)
    target = routing * capacity + rank_in
    joined = jnp.concatenate([tokens_in, hidden_grad], axis=1)
    outgoing = jnp.zeros((slot_count, joined.shape[1]), jnp.bfloat16).at[target].set(joined)
    arrived = lax.all_to_all(
        outgoing.reshape(experts, capacity, joined.shape[1]),
        "expert",
        split_axis=0,
        concat_axis=0,
        tiled=True,
    )
    slot_rows = arrived.reshape(slot_count, joined.shape[1])
    inputs, pre_grad, slot_grad = expert_backward(slot_rows, weights, model_width)
    arrived_grad = lax.all_to_all(
        slot_grad.reshape(experts, capacity, model_width),
        "expert",
        split_axis=0,
        concat_axis=0,
        tiled=True,
    )
    tokens_grad = jnp.take(
        arrived_grad.reshape(slot_count, model_width), target, axis=0, mode="clip"
    )
    weight_grad = lax.psum_scatter(
        lax.dot_general(
            inputs, pre_grad, (((0,), (0,)), ((), ())), preferred_element_type=jnp.float32
        ),
        "group",
        scatter_dimension=0,
        tiled=True,
    )
    return (tokens_grad, weight_grad[None])


def solution(mesh):
    return jax.shard_map(
        on_device,
        mesh=mesh,
        in_specs=(
            P(("expert", "group"), None),
            P(("expert", "group"), None),
            P(("expert", "group")),
            P("expert", None, None),
        ),
        out_specs=(P(("expert", "group"), None), P("expert", "group", None)),
        check_vma=False,
    )
```

profile of v0, /device:TPU:0, one launch (start us, length us, event | category | flops | bytes accessed | tf_op | source)
XLA Modules:
  0.0 109.8 jit_solution(7311571783881672310)
XLA Ops:
  7.2 0.0 copy-start
  7.2 0.0 reduce-scatter.2.cloned.1.call-start
  7.2 0.9 fusion.16
  8.1 0.2 reduce_window_sum.11
  8.3 0.8 select_reduce_fusion
  9.1 0.7 compare_select_fusion
  9.8 2.4 %scatter_custom_fusion = bf16[256,2304]{1,0:T(8,128)(2,1)S(1)} fusion(s32[128]{0:T(128)S(1)} %get-tuple-element.2, bf16[128,256]{1,0:T(8,128)(2,1)} %param.5, bf16[]{:T(256)} %constant.16, bf16[128,2048]{1,0:T(8,128)(2,1)} %param.4, bf16[]{:T(256)} %constant.5.clone.1), kind=kCustom, calls=%fused_computation.9 | custom fusion | flops 1179648 | bytes 1769476 | tf_op jit(solution)/shard_map/scatter | solution.py:36
  12.2 35.5 %all_to_all.10 = bf16[8,32,2304]{2,1,0:T(8,128)(2,1)S(1)} all-to-all(bf16[8,32,2304]{2,1,0:T(8,128)(2,1)S(1)} %bitcast.14), channel_id=1, replica_groups=mesh['expert'=8,'group'=4] {'expert'}, dimensions={0} | all-to-all | bytes 2359296 | tf_op jit(solution)/shard_map/all_to_all | solution.py:37
  47.7 0.0 copy-done
  47.7 0.7 fusion.1
  48.4 0.1 fusion.13
  48.6 2.7 %fusion.3 = f32[2048,512]{1,0:T(8,128)} fusion(bf16[256,2304]{1,0:T(8,128)(2,1)S(1)} %bitcast.13, bf16[256,256]{1,0:T(8,128)(2,1)S(1)} %get-tuple-element.5, bf16[256,256]{1,0:T(8,128)(2,1)S(1)} %get-tuple-element.4), kind=kOutput, calls=%fused_computation.6 | convolution fusion | flops 537395200 | bytes 5505024 | tf_op jit(solution)/shard_map/dot_general | solution.py:57
  51.2 0.0 reduce-scatter.2.cloned.1.call-update
  51.2 1.7 %convolution_convert_fusion = bf16[256,2048]{1,0:T(8,128)(2,1)} fusion(bf16[1,2048,512]{2,1,0:T(8,128)(2,1)S(1)} %copy-done, bf16[256,256]{1,0:T(8,128)(2,1)S(1)} %get-tuple-element.5, bf16[256,256]{1,0:T(8,128)(2,1)S(1)} %get-tuple-element.4), kind=kOutput, calls=%fused_computation.2 | convolution fusion | flops 537919488 | bytes 3407872 | tf_op jit(solution)/shard_map/dot_general | solution.py:18
  53.0 3.6 %all-to-all-start.1 = ((bf16[8,32,2048]{2,1,0:T(8,128)(2,1)}), bf16[8,32,2048]{2,1,0:T(8,128)(2,1)S(1)}, u32[]{:S(2)}, u32[]{:S(2)}) async-start(bf16[8,32,2048]{2,1,0:T(8,128)(2,1)} %bitcast.15), calls=%async_computation.1 | async-start | bytes 2097152 | tf_op jit(solution)/shard_map/all_to_all | solution.py:46
  56.5 26.5 %all-to-all-done.1 = bf16[8,32,2048]{2,1,0:T(8,128)(2,1)S(1)} async-done(((bf16[8,32,2048]{2,1,0:T(8,128)(2,1)}), bf16[8,32,2048]{2,1,0:T(8,128)(2,1)S(1)}, u32[]{:S(2)}, u32[]{:S(2)}) %all-to-all-start.1) | async-done | bytes 1048608 | tf_op jit(solution)/shard_map/all_to_all | solution.py:46
  83.0 1.7 %gather_fusion = bf16[128,2048]{1,0:T(8,128)(2,1)} fusion(bf16[256,2048]{1,0:T(8,128)(2,1)S(1)} %bitcast.10, s32[1024]{0:T(1024)S(1)} %pad_clamp_fusion), kind=kCustom, calls=%fused_computation | custom fusion | bytes 1049088 | tf_op jit(solution)/shard_map/jit(_take)/gather | solution.py:53
  84.7 18.2 %reduce-scatter.2.cloned.1.call-done = f32[512,512]{1,0:T(8,128)} async-done(((f32[2048,512]{1,0:T(8,128)}), f32[512,512]{1,0:T(8,128)}) %reduce-scatter.2.cloned.1.call-update) | async-done | bytes 1048592 | tf_op jit(solution)/shard_map/reduce_scatter | solution.py:56
  (1 shorter events, 0.0 us)
Async XLA Ops:
  7.2 40.5 %copy-start = (bf16[1,2048,512]{2,1,0:T(8,128)(2,1)S(1)}, bf16[1,2048,512]{2,1,0:T(8,128)(2,1)}, u32[]{:S(2)}) copy-start(bf16[1,2048,512]{2,1,0:T(8,128)(2,1)} %param.7) | copy-start | bytes 6291460
  7.2 95.7 %reduce-scatter.2.cloned.1.call-start = ((), (), s32[]{:S(2)}) async-start(), calls=%async_computation.3 | async-start | bytes 5242880 | tf_op jit(solution)/shard_map/reduce_scatter | solution.py:56
  53.0 30.1 %all-to-all-start.1 = ((bf16[8,32,2048]{2,1,0:T(8,128)(2,1)}), bf16[8,32,2048]{2,1,0:T(8,128)(2,1)S(1)}, u32[]{:S(2)}, u32[]{:S(2)}) async-start(bf16[8,32,2048]{2,1,0:T(8,128)(2,1)} %bitcast.15), calls=%async_computation.1 | async-start | bytes 2097152 | tf_op jit(solution)/shard_map/all_to_all | solution.py:46
Sparse Core Ops, SparseCore 0:
  51.4 51.5 reduce-scatter.1
where the time goes:
time: 110 us
  waiting for transfers between devices  44.7 us (41%)
  blocking collectives  35.5 us (32%)
  between operations  14.1 us (13%)
  other arithmetic  5.08 us (5%)
  matrix products  5.08 us (5%)
  starting transfers between devices  3.59 us (3%)
  local copies, waits for them, and re-layouts  1.73 us (2%)
    all_to_all x1, blocking collectives, on_device(): lax.all_to_all(outgoing.reshape(experts, capacity, joined.shape[1]), 'exp...  35.5 us
    all_to_all x1, waiting for transfers between devices, on_device(): lax.all_to_all(slot_grad.reshape(experts, capacity, model_width), 'expert...  26.5 us
    reduce_scatter x1, waiting for transfers between devices, on_device(): lax.psum_scatter(lax.dot_general(inputs, pre_grad, (((0,), (0,)), ((), ()...  18.2 us
    all_to_all x1, starting transfers between devices, on_device(): lax.all_to_all(slot_grad.reshape(experts, capacity, model_width), 'expert...  3.56 us
    dot_general x1, matrix products, on_device(): lax.dot_general(inputs, pre_grad, (((0,), (0,)), ((), ())), preferred_ele...  2.67 us
    scatter x1, other arithmetic, on_device(): jnp.zeros((slot_count, joined.shape[1]), jnp.bfloat16).at[target]  2.39 us
  transfers between devices with their start and end apart: 2, of which 2 were waited for; matrix products, arithmetic and copies ran while one was open for 3% of the time, Pallas kernels for 0%

commit v1 on v0

v1 whole, which is shorter than its diff:
```python
import functools

import jax
import jax.numpy as jnp
from jax import lax
from jax.experimental import pallas as pl
from jax.experimental.pallas import tpu as pltpu
from jax.sharding import PartitionSpec as P


BF16 = jnp.bfloat16
F32 = jnp.float32
VMEM = pl.BlockSpec(memory_space=pltpu.VMEM)
HBM = pl.BlockSpec(memory_space=pltpu.HBM)


def chunks(total, width):
    return [(at, min(width, total - at)) for at in range(0, total, width)]


def dot(a, b):
    return jnp.dot(a, b, preferred_element_type=F32)


def dot_t(a, b):
    return lax.dot_general(a, b, (((0,), (0,)), ((), ())), preferred_element_type=F32)


def dot_nt(a, b):
    return lax.dot_general(a, b, (((1,), (1,)), ((), ())), preferred_element_type=F32)


def stack(pieces, columns=slice(None)):
    if all(piece.shape[0] % 16 == 0 for piece in pieces):
        return jnp.concatenate([piece[:, columns] for piece in pieces], axis=0)
    return jnp.concatenate([piece[:, columns].astype(F32) for piece in pieces], axis=0).astype(BF16)


def unstack(value, pieces, columns):
    start = 0
    for piece in pieces:
        end = start + piece.shape[0]
        piece[:, columns] = value[start:end].astype(BF16)
        start = end


def ranks_of(block, experts):
    rows = block.shape[1]
    one_hot = block == lax.broadcasted_iota(jnp.int32, (experts, rows), 0)
    ones = jnp.where(one_hot, 1.0, 0.0)
    counts = dot(ones.astype(BF16), earlier(rows))
    return jnp.sum(counts * ones, axis=0, keepdims=True).astype(jnp.int32)


def earlier(rows):
    mask = lax.broadcasted_iota(jnp.int32, (rows, rows), 0) < lax.broadcasted_iota(
        jnp.int32, (rows, rows), 1
    )
    return jnp.where(mask, 1.0, 0.0).astype(BF16)


def one_hot_rows(target, count):
    return jnp.where(
        target == lax.broadcasted_iota(jnp.int32, (count, target.shape[1]), 0), 1.0, 0.0
    ).astype(BF16)


def load_inputs(routing_hbm, tokens_hbm, hidden_hbm, routing_ref, joined_ref, sems):
    width = tokens_hbm.shape[1]
    copies = [
        pltpu.make_async_copy(routing_hbm, routing_ref, sems.at[0]),
        pltpu.make_async_copy(tokens_hbm, joined_ref.at[:, :width], sems.at[1]),
        pltpu.make_async_copy(hidden_hbm, joined_ref.at[:, width:], sems.at[2]),
    ]
    for copy in copies:
        copy.start()
    return copies


def dispatch_kernel(experts, *refs):
    routing_hbm, tokens_hbm, hidden_hbm, select_ref, spill_ref, own_ref, *rest = refs
    near, low = rest[: experts // 2], rest[experts // 2 : experts]
    routing_ref, joined_ref, sems = rest[experts:]
    copies = load_inputs(routing_hbm, tokens_hbm, hidden_hbm, routing_ref, joined_ref, sems)
    rows, joined = joined_ref.shape
    half = experts // 2
    full, low_rows, up_rows = near[0].shape[0], low[0].shape[0], own_ref.shape[0] // half
    low_at = half * full
    own_at = low_at + half * low_rows
    spill_at = own_at + half * up_rows
    kept = low_rows + up_rows
    me = lax.axis_index("expert").astype(jnp.int32)
    copies[0].wait()
    block = routing_ref[...] ^ me
    rank = ranks_of(block, experts)
    far = block - half
    spilled = (far >= 0) & (rank >= kept)
    spilled_ones = jnp.broadcast_to(jnp.where(spilled, 1.0, 0.0), (8, rows)).astype(BF16)
    place = dot(spilled_ones, earlier(rows))[:1].astype(jnp.int32)
    target = jnp.where(
        far < 0,
        block * full + rank,
        jnp.where(
            rank < low_rows,
            low_at + far * low_rows + rank,
            jnp.where(
                spilled, spill_at + place, own_at + far * up_rows + (rank - low_rows)
            ),
        ),
    )
    select = one_hot_rows(target, select_ref.shape[0])
    select_ref[...] = select
    landing = jnp.where(spilled, far * up_rows + (up_rows - 1) - (rank - kept), -1)
    spill_ref[:, joined:] = dot_nt(
        select[spill_at:], one_hot_rows(landing, spill_ref.shape[1] - joined)
    ).astype(BF16)
    copies[1].wait()
    copies[2].wait()
    for at, size in chunks(joined, 256):
        columns = slice(at, at + size)
        placed = dot(select, joined_ref[:, columns])
        unstack(placed, [*near, *low, own_ref, spill_ref], columns)


def merge_kernel(own_ref, spill_ref, *piece_refs):
    slots, joined = own_ref.shape
    landing = spill_ref[:, joined:]
    for at, size in chunks(joined, 256):
        columns = slice(at, at + size)
        landed = dot_t(landing, spill_ref[:, columns])[:slots]
        unstack(landed + own_ref[:, columns].astype(F32), piece_refs, columns)


def split_kernel(spill_ref, *refs):
    *pieces, out_ref = refs
    slots = sum(piece.shape[0] for piece in pieces)
    joined = spill_ref.shape[1] - 128
    landing = spill_ref[:, joined:]
    for at, size in chunks(out_ref.shape[1], 512):
        columns = slice(at, at + size)
        value = stack(pieces, columns)
        pad = jnp.zeros((landing.shape[1] - slots, size), BF16)
        out_ref[:, columns] = dot(landing, jnp.concatenate([value, pad], axis=0)).astype(BF16)


def hidden_grads(inputs, cotangent, weights_ref):
    projected = dot(inputs, weights_ref[...])
    hidden = projected.shape[1] // 2
    gate_pre = projected[:, :hidden]
    up_pre = projected[:, hidden:]
    sigmoid_gate = jax.nn.sigmoid(gate_pre)
    gate_grad = cotangent * up_pre * sigmoid_gate * (1.0 + gate_pre * (1.0 - sigmoid_gate))
    up_grad = cotangent * gate_pre * sigmoid_gate
    return jnp.concatenate([gate_grad.astype(BF16), up_grad.astype(BF16)], axis=1)


def input_grads(pre_grad, weights_ref, pieces):
    for at, size in chunks(weights_ref.shape[0], 512):
        columns = slice(at, at + size)
        unstack(dot_nt(pre_grad, weights_ref[columns, :]), pieces, columns)


def near_kernel(count, *refs):
    pieces, (weights_ref, pre_ref), grads = refs[:count], refs[count : count + 2], refs[count + 2 :]
    width = weights_ref.shape[0]
    inputs = stack(pieces, slice(0, width))
    cotangent = stack(pieces, slice(width, None)).astype(F32)
    pre_ref[...] = hidden_grads(inputs, cotangent, weights_ref)
    input_grads(pre_ref[...], weights_ref, grads)


def far_kernel(groups, near_count, count, *refs):
    near = refs[:near_count]
    pieces = refs[near_count : near_count + count]
    near_pre_ref, weights_ref = refs[near_count + count : near_count + count + 2]
    rest = refs[near_count + count + 2 :]
    grads = rest[:count]
    send_a, keep_a, send_b, keep_b, inputs_ref, pre_ref = rest[count:]
    width, _ = weights_ref.shape
    split = near_pre_ref.shape[0]
    inputs_ref[:split, :] = stack(near, slice(0, width))
    pre_ref[:split, :] = near_pre_ref[...]
    low, up = pieces[: count // 2], pieces[count // 2 :]
    inputs = jnp.concatenate([stack(low, slice(0, width)), stack(up, slice(0, width))], axis=0)
    inputs_ref[split:, :] = inputs
    cotangent = jnp.concatenate(
        [stack(low, slice(width, None)), stack(up, slice(width, None))], axis=0
    ).astype(F32)
    pre_grad = hidden_grads(inputs_ref[split:, :], cotangent, weights_ref)
    pre_ref[split:, :] = pre_grad
    input_grads(pre_grad, weights_ref, grads)
    weight_terms(groups, inputs_ref, pre_ref, send_a, keep_a, send_b, keep_b)


def weight_terms(groups, inputs_ref, pre_ref, send_a, keep_a, send_b, keep_b):
    me = lax.axis_index("group").astype(jnp.int32)
    part = inputs_ref.shape[1] // groups
    hidden = pre_ref.shape[1] // 2
    pre_grad = pre_ref[...]
    for k in range(groups):
        columns = pl.ds(pl.multiple_of((me ^ k) * part, part), part)
        term = dot_t(inputs_ref[:, columns], pre_grad)
        if k % 2:
            send_a[k // 2] = term[:, :hidden].astype(BF16)
        else:
            keep_a[k // 2] = term[:, :hidden]
        if k >= groups // 2:
            send_b[k - groups // 2] = term[:, hidden:].astype(BF16)
        else:
            keep_b[k] = term[:, hidden:]


def combine_kernel(select_ref, *refs):
    *pieces, out_ref, stacked_ref = refs
    start = 0
    while pieces:
        rows = pieces[0].shape[0]
        run = pieces[: next((i for i, p in enumerate(pieces) if p.shape[0] != rows), len(pieces))]
        end = start + rows * len(run)
        stacked_ref[start:end, :] = stack(run)
        start, pieces = end, pieces[len(run) :]
    select = select_ref[...]
    for at, size in chunks(out_ref.shape[1], 512):
        out_ref[:, at : at + size] = dot_t(select, stacked_ref[:, at : at + size]).astype(BF16)


def call(kernel, out_shapes, scratch, flops, moved, args, specs=None, vmem=24 << 20):
    return pl.pallas_call(
        kernel,
        out_shape=out_shapes,
        in_specs=specs or [VMEM] * len(args),
        out_specs=jax.tree.map(lambda _: VMEM, out_shapes),
        scratch_shapes=scratch,
        compiler_params=pltpu.CompilerParams(vmem_limit_bytes=vmem),
        cost_estimate=pl.CostEstimate(flops=flops, bytes_accessed=moved, transcendentals=0),
    )(*args)


def shape(dims, kind=BF16):
    return jax.ShapeDtypeStruct(dims, kind)


def flip(value, axis, mask):
    size = lax.axis_size(axis)
    return lax.ppermute(value, axis, [(i, i ^ mask) for i in range(size)])


def sum_over_groups(send_a, keep_a, send_b, keep_b, groups):
    bits = groups.bit_length() - 1
    for step in range(bits):
        got_a = flip(send_a, "group", 1 << step).astype(F32)
        got_b = flip(send_b, "group", 1 << (bits - 1 - step)).astype(F32)
        if step == bits - 1:
            return jnp.concatenate([keep_a[0] + got_a[0], keep_b[0] + got_b[0]], axis=1)
        half = keep_a.shape[0] // 2
        send_a = (keep_a[1::2] + got_a[1::2]).astype(BF16)
        keep_a = keep_a[0::2] + got_a[0::2]
        send_b = (keep_b[half:] + got_b[half:]).astype(BF16)
        keep_b = keep_b[:half] + got_b[:half]


def term_shapes(groups, width, hidden):
    block = (groups // 2, width // groups, hidden)
    return [shape(block), shape(block, F32), shape(block), shape(block, F32)]


def paired(tokens_in, hidden_grad, routing, weights):
    experts = lax.axis_size("expert")
    groups = lax.axis_size("group")
    rows, width = tokens_in.shape
    hidden = hidden_grad.shape[1]
    joined = width + hidden
    half = experts // 2
    full, low_rows, up_rows = 2 * rows // experts, rows // experts, rows // (2 * experts)
    spill = rows // 4
    slots = half * (full + low_rows + up_rows) + spill
    lane = 128

    select, spilled, own, *pieces = call(
        functools.partial(dispatch_kernel, experts),
        [shape((slots, rows)), shape((spill, joined + lane)), shape((half * up_rows, joined))]
        + [shape((full, joined))] * half
        + [shape((low_rows, joined))] * half,
        [
            pltpu.VMEM((1, rows), jnp.int32),
            pltpu.VMEM((rows, joined), BF16),
            pltpu.SemaphoreType.DMA((3,)),
        ],
        2 * slots * rows * joined,
        2 * slots * joined,
        (routing.reshape(1, rows), tokens_in, hidden_grad),
        specs=[HBM] * 3,
        vmem=40 << 20,
    )
    near, low = pieces[:half], pieces[half:]
    landed = flip(spilled, "group", groups // 2)
    low = [flip(low[k], "expert", half + k) for k in range(half)]
    near = [near[0]] + [flip(near[k], "expert", k) for k in range(1, half)]
    up = call(
        merge_kernel,
        [shape((up_rows, joined))] * half,
        [],
        2 * spill * lane * joined,
        4 * half * up_rows * joined,
        (own, landed),
    )
    up = [flip(up[k], "expert", half + k) for k in range(half)]

    near_slots, far_slots = half * full, half * (low_rows + up_rows)
    near_pre, *near_grads = call(
        functools.partial(near_kernel, half),
        [shape((near_slots, 2 * hidden))] + [shape((full, width))] * half,
        [],
        8 * near_slots * width * hidden,
        4 * near_slots * joined,
        (*near, weights),
    )
    out = call(
        functools.partial(far_kernel, groups, half, 2 * half),
        [shape((low_rows, width))] * half
        + [shape((up_rows, width))] * half
        + term_shapes(groups, width, hidden),
        [
            pltpu.VMEM((near_slots + far_slots, width), BF16),
            pltpu.VMEM((near_slots + far_slots, 2 * hidden), BF16),
        ],
        12 * (near_slots + far_slots) * width * hidden,
        4 * (near_slots + far_slots) * joined,
        (*near, *low, *up, near_pre, weights),
        vmem=32 << 20,
    )
    low_grads, up_grads, terms = out[:half], out[half : 2 * half], out[2 * half :]
    near_grads = [near_grads[0]] + [flip(near_grads[k], "expert", k) for k in range(1, half)]
    up_grads = [flip(up_grads[k], "expert", half + k) for k in range(half)]
    low_grads = [flip(low_grads[k], "expert", half + k) for k in range(half)]
    spilled_grad = call(
        split_kernel,
        shape((spill, width)),
        [],
        2 * spill * lane * width,
        4 * half * up_rows * width,
        (landed, *up_grads),
    )
    spilled_grad = flip(spilled_grad, "group", groups // 2)
    weight_grad = sum_over_groups(*terms, groups)
    tokens_grad = call(
        combine_kernel,
        shape((rows, width)),
        [pltpu.VMEM((slots, width), BF16)],
        2 * slots * rows * width,
        2 * slots * width,
        (select, *near_grads, *low_grads, *up_grads, spilled_grad),
    )
    return tokens_grad, weight_grad


def whole_dispatch_kernel(experts, routing_hbm, tokens_hbm, hidden_hbm, select_ref, out_ref, *rest):
    routing_ref, joined_ref, sems = rest
    copies = load_inputs(routing_hbm, tokens_hbm, hidden_hbm, routing_ref, joined_ref, sems)
    copies[0].wait()
    block = routing_ref[...]
    slots = select_ref.shape[0]
    select = one_hot_rows(block * (slots // experts) + ranks_of(block, experts), slots)
    select_ref[...] = select
    copies[1].wait()
    copies[2].wait()
    for at, size in chunks(out_ref.shape[1], 256):
        columns = slice(at, at + size)
        out_ref[:, columns] = dot(select, joined_ref[:, columns]).astype(BF16)


def whole_expert_kernel(groups, rows_ref, weights_ref, grad_ref, *refs):
    *terms, inputs_ref, pre_ref = refs
    width = weights_ref.shape[0]
    inputs_ref[...] = rows_ref[:, :width]
    pre_ref[...] = hidden_grads(inputs_ref[...], rows_ref[:, width:].astype(F32), weights_ref)
    input_grads(pre_ref[...], weights_ref, [grad_ref])
    weight_terms(groups, inputs_ref, pre_ref, *terms)


def unpaired(tokens_in, hidden_grad, routing, weights):
    experts = lax.axis_size("expert")
    groups = lax.axis_size("group")
    rows, width = tokens_in.shape
    hidden = hidden_grad.shape[1]
    joined = width + hidden
    capacity = 2 * rows // experts
    slots = experts * capacity

    def exchange(value):
        block = value.reshape(experts, capacity, -1)
        moved = lax.all_to_all(block, "expert", split_axis=0, concat_axis=0, tiled=True)
        return moved.reshape(slots, -1)

    select, outgoing = call(
        functools.partial(whole_dispatch_kernel, experts),
        [shape((slots, rows)), shape((slots, joined))],
        [
            pltpu.VMEM((1, rows), jnp.int32),
            pltpu.VMEM((rows, joined), BF16),
            pltpu.SemaphoreType.DMA((3,)),
        ],
        2 * slots * rows * joined,
        2 * slots * joined,
        (routing.reshape(1, rows), tokens_in, hidden_grad),
        specs=[HBM] * 3,
    )
    grad, *terms = call(
        functools.partial(whole_expert_kernel, groups),
        [shape((slots, width))] + term_shapes(groups, width, hidden),
        [pltpu.VMEM((slots, width), BF16), pltpu.VMEM((slots, 2 * hidden), BF16)],
        12 * slots * width * hidden,
        4 * slots * joined,
        (exchange(outgoing), weights),
        vmem=32 << 20,
    )
    weight_grad = sum_over_groups(*terms, groups)
    tokens_grad = call(
        combine_kernel,
        shape((rows, width)),
        [pltpu.VMEM((slots, width), BF16)],
        2 * slots * rows * width,
        2 * slots * width,
        (select, exchange(grad)),
    )
    return tokens_grad, weight_grad


def can_pair(mesh, rows):
    experts, groups = mesh.shape["expert"], mesh.shape["group"]
    return groups % 2 == 0 and rows % (16 * experts) == 0 and experts <= 16


def on_device(pair, tokens_in, hidden_grad, routing, gate_up):
    run = paired if pair else unpaired
    tokens_grad, weight_grad = run(tokens_in, hidden_grad, routing, gate_up[0])
    return (tokens_grad, weight_grad[None])


def solution(mesh):
    devices = mesh.shape["expert"] * mesh.shape["group"]

    def whole(tokens_in, hidden_grad, routing, gate_up):
        pair = can_pair(mesh, routing.shape[0] // devices)
        return jax.shard_map(
            functools.partial(on_device, pair),
            mesh=mesh,
            in_specs=(
                P(("expert", "group"), None),
                P(("expert", "group"), None),
                P(("expert", "group")),
                P("expert", None, None),
            ),
            out_specs=(P(("expert", "group"), None), P("expert", "group", None)),
            check_vma=False,
        )(tokens_in, hidden_grad, routing, gate_up)

    return whole
```

time: 110 us -> 75.8 us (0.69)
  blocking collectives: 35.5 us -> 0 us
  starting transfers between devices: 3.59 us -> 33 us
  waiting for transfers between devices: 44.7 us -> 30.1 us
  between operations: 14.1 us -> 0.78 us
  Pallas kernels: 0 us -> 5.54 us
  matrix products: 5.08 us -> 0 us
  other arithmetic: 5.08 us -> 1.62 us
  local copies, waits for them, and re-layouts: 1.73 us -> 4.48 us
    all_to_all x1 -> x0, blocking collectives: 35.5 us -> none  [on_device(): lax.all_to_all(outgoing.reshape(experts, capacity, joined.shape[1]), 'exp...]
    ppermute x0 -> x28, starting transfers between devices: none -> 33 us  [flip(): return lax.ppermute(value, axis, [(i, i ^ mask) for i in range(size)])]
    ppermute x0 -> x28, waiting for transfers between devices: none -> 30.1 us  [flip(): return lax.ppermute(value, axis, [(i, i ^ mask) for i in range(size)])]
    all_to_all x1 -> x0, waiting for transfers between devices: 26.5 us -> none  [on_device(): lax.all_to_all(slot_grad.reshape(experts, capacity, model_width), 'expert...]
    reduce_scatter x1 -> x0, waiting for transfers between devices: 18.2 us -> none  [on_device(): lax.psum_scatter(lax.dot_general(inputs, pre_grad, (((0,), (0,)), ((), ()...]
    pallas_call x0 -> x6, Pallas kernels: none -> 5.54 us  [call(): pl.pallas_call(kernel, out_shape=out_shapes, in_specs=specs or [VMEM] * l...]
    dot_general x3 -> x0, matrix products: 5.08 us -> none  [the longest x1 2.67 us: on_device(): lax.dot_general(inputs, pre_grad, (((0,), (0,)), ((), ())), preferred_ele...]
    unnamed x2 -> x10, local copies, waits for them, and re-layouts: 0.01 us -> 4.48 us
  transfers between devices with their start and end apart: 2 -> 28, of which waited for: 2 -> 13; matrix products, arithmetic and copies ran while one was open for 3% -> 1% of each run, Pallas kernels for 0% -> 4%
where the time goes in v1:
time: 75.8 us; the launch traced here: 75.5 us
  starting transfers between devices  33 us (44%)
  waiting for transfers between devices  30.1 us (40%)
  Pallas kernels  5.54 us (7%)
  local copies, waits for them, and re-layouts  4.48 us (6%)
  other arithmetic  1.62 us (2%)
  between operations  0.78 us (1%)
    ppermute x28, starting transfers between devices, flip(): return lax.ppermute(value, axis, [(i, i ^ mask) for i in range(size)])  33 us
    ppermute x28, waiting for transfers between devices, flip(): return lax.ppermute(value, axis, [(i, i ^ mask) for i in range(size)])  30.1 us
    pallas_call x6, Pallas kernels, call(): pl.pallas_call(kernel, out_shape=out_shapes, in_specs=specs or [VMEM] * l...  5.54 us
    unnamed x10, local copies, waits for them, and re-layouts  4.48 us
  transfers between devices with their start and end apart: 28, of which 13 were waited for; matrix products, arithmetic and copies ran while one was open for 1% of the time, Pallas kernels for 4%

profile of v1, /device:TPU:0, one launch (start us, length us, event | category | flops | bytes accessed | tf_op | source)
XLA Modules:
  0.0 75.5 jit_solution(5556291195875812553)
XLA Ops:
  0.6 1.0 %copy-done.2 = bf16[128,2048]{1,0:T(8,128)(2,1)S(1)} copy-done((bf16[128,2048]{1,0:T(8,128)(2,1)S(1)}, bf16[128,2048]{1,0:T(8,128)(2,1)}, u32[]{:S(2)}) %copy-start.2) | copy-done | bytes 524312
  3.2 1.0 %shard_map.59 = (bf16[256,128]{1,0:T(8,128)(2,1)S(1)}, bf16[32,2432]{1,0:T(8,128)(2,1)S(1)}, bf16[32,2304]{1,0:T(8,128)(2,1)S(1)}, bf16[32,2304]{1,0:T(8,128)(2,...) custom-call(s32[1,128]{1,0:T(1,128)S(1)} %bitcast.10, ...), custom_call_target="tpu_custom_call" | custom-call | flops 150994944 | bytes 1179648 | tf_op jit(solution)/shard_map/pallas_call | solution.py:228
  4.1 4.1 %collective-permute-start.6 = (bf16[16,2304]{1,0:T(8,128)(2,1)S(1)}, bf16[16,2304]{1,0:T(8,128)(2,1)S(1)}, u32[]{:S(2)}, u32[]{:S(2)}) collective-permute-start(bf16[16,2304]{1,0:T(8,128)(2,1)S(1)} %get-tuple-element.43), channel_id=1, source_target_pairs={{0,16},{4,20},{8,24},{12,28},{16,0},{20,4},{24,8},{28,12},{1,17},{... | collective-permute-start | bytes 221192 | tf_op jit(solution)/shard_map/ppermute | solution.py:245
  8.3 1.5 %collective-permute-start.10 = (bf16[32,2432]{1,0:T(8,128)(2,1)S(1)}, bf16[32,2432]{1,0:T(8,128)(2,1)S(1)}, u32[]{:S(2)}, u32[]{:S(2)}) collective-permute-start(bf16[32,2432]{1,0:T(8,128)(2,1)S(1)} %get-tuple-element.48), channel_id=1, source_target_pairs={{0,2},{1,3},{2,0},{3,1},{4,6},{5,7},{6,4},{7,5},{8,10},{9,11},{10,... | collective-permute-start | bytes 466952 | tf_op jit(solution)/shard_map/ppermute | solution.py:245
  10.2 1.6 %collective-permute-start.1 = (bf16[32,2304]{1,0:T(8,128)(2,1)S(1)}, bf16[32,2304]{1,0:T(8,128)(2,1)S(1)}, u32[]{:S(2)}, u32[]{:S(2)}) collective-permute-start(bf16[32,2304]{1,0:T(8,128)(2,1)S(1)} %get-tuple-element.37), channel_id=1, source_target_pairs={{0,8},{4,12},{8,0},{12,4},{16,24},{20,28},{24,16},{28,20},{1,9},{5... | collective-permute-start | bytes 442376 | tf_op jit(solution)/shard_map/ppermute | solution.py:245
  12.2 4.2 %collective-permute-done.7.refs_5_ = bf16[16,2304]{1,0:T(8,128)(2,1)S(1)} collective-permute-done((bf16[16,2304]{1,0:T(8,128)(2,1)S(1)}, bf16[16,2304]{1,0:T(8,128)(2,1)S(1)}, u32[]{:S(2)}, u32[]{:S(2)}) %collective-permute-start.7) | collective-permute-done | bytes 73760 | tf_op jit(solution)/shard_map/ppermute | solution.py:245
  16.4 2.1 %collective-permute-start.8 = (bf16[16,2304]{1,0:T(8,128)(2,1)S(1)}, bf16[16,2304]{1,0:T(8,128)(2,1)S(1)}, u32[]{:S(2)}, u32[]{:S(2)}) collective-permute-start(bf16[16,2304]{1,0:T(8,128)(2,1)S(1)} %get-tuple-element.45), channel_id=1, source_target_pairs={{0,24},{4,28},{8,16},{12,20},{16,8},{20,12},{24,0},{28,4},{1,25},{... | collective-permute-start | bytes 221192 | tf_op jit(solution)/shard_map/ppermute | solution.py:245
  18.9 5.1 %collective-permute-done.8.refs_6_ = bf16[16,2304]{1,0:T(8,128)(2,1)S(1)} collective-permute-done((bf16[16,2304]{1,0:T(8,128)(2,1)S(1)}, bf16[16,2304]{1,0:T(8,128)(2,1)S(1)}, u32[]{:S(2)}, u32[]{:S(2)}) %collective-permute-start.8) | collective-permute-done | bytes 73760 | tf_op jit(solution)/shard_map/ppermute | solution.py:245
  24.1 1.7 %collective-permute-start.12 = (bf16[8,2304]{1,0:T(8,128)(2,1)S(1)}, bf16[8,2304]{1,0:T(8,128)(2,1)S(1)}, u32[]{:S(2)}, u32[]{:S(2)}) collective-permute-start(bf16[8,2304]{1,0:T(8,128)(2,1)S(1)} %get-tuple-element.50), channel_id=1, source_target_pairs={{0,20},{4,16},{8,28},{12,24},{16,4},{20,0},{24,12},{28,8},{1,21},{... | collective-permute-start | bytes 110600 | tf_op jit(solution)/shard_map/ppermute | solution.py:245
  26.1 4.2 %collective-permute-start.14 = (bf16[8,2304]{1,0:T(8,128)(2,1)S(1)}, bf16[8,2304]{1,0:T(8,128)(2,1)S(1)}, u32[]{:S(2)}, u32[]{:S(2)}) collective-permute-start(bf16[8,2304]{1,0:T(8,128)(2,1)S(1)} %get-tuple-element.52), channel_id=1, source_target_pairs={{0,28},{4,24},{8,20},{12,16},{16,12},{20,8},{24,4},{28,0},{1,29},{... | collective-permute-start | bytes 110600 | tf_op jit(solution)/shard_map/ppermute | solution.py:245
  30.3 1.6 %copy-done = bf16[1,2048,512]{2,1,0:T(8,128)(2,1)S(1)} copy-done((bf16[1,2048,512]{2,1,0:T(8,128)(2,1)S(1)}, bf16[1,2048,512]{2,1,0:T(8,128)(2,1)}, u32[]{:S(2)}) %copy-start) | copy-done | bytes 2097176
  31.9 1.2 %shard_map.60 = (bf16[128,512]{1,0:T(8,128)(2,1)S(1)}, bf16[32,2048]{1,0:T(8,128)(2,1)S(1)}, bf16[32,2048]{1,0:T(8,128)(2,1)S(1)}, bf16[32,2048]{1,0:T(8,128)(2,1)S(1)}, bf16[32,2048]{1,0:T(8,128)(2,1)S(1)}) custom-call(bf16[32,2304]{1,0:T(8,128)(2,1)S(1)} %get-tuple-element.35.refs_0_, bf16[32,2304]{1,0:T(8,128)(2,1)S(1)} %collective-permute-done.refs_1_, ...), custom_call_target="tpu_custom_call" | custom-call | flops 536870912 | bytes 1179648 | tf_op jit(solution)/shard_map/pallas_call | solution.py:228
  33.4 1.8 %shard_map.62 = (bf16[16,2048]{1,0:T(8,128)(2,1)S(1)}, bf16[16,2048]{1,0:T(8,128)(2,1)S(1)}, bf16[16,2048]{1,0:T(8,128)(2,1)S(1)}, bf16[16,2048]{1,0:T(8,128)(2,...) custom-call(bf16[32,2304]{1,0:T(8,128)(2,1)S(1)} %get-tuple-element., ...), custom_call_target="tpu_custom_call" | custom-call | flops 1409286144 | bytes 2064384 | tf_op jit(solution)/shard_map/pallas_call | solution.py:228
  35.2 1.6 %collective-permute-start.24 = (bf16[2,512,256]{2,1,0:T(8,128)(2,1)S(1)}, bf16[2,512,256]{2,1,0:T(8,128)(2,1)S(1)}, u32[]{:S(2)}, u32[]{:S(2)}) collective-permute-start(bf16[2,512,256]{2,1,0:T(8,128)(2,1)S(1)} %get-tuple-element.63), channel_id=1, source_target_pairs={{0,1},{1,0},{2,3},{3,2},{4,5},{5,4},{6,7},{7,6},{8,9},{9,8},{10,11... | collective-permute-start | bytes 1572872 | tf_op jit(solution)/shard_map/ppermute | solution.py:245
  37.5 2.3 %collective-permute-start.20 = (bf16[8,2048]{1,0:T(8,128)(2,1)S(1)}, bf16[8,2048]{1,0:T(8,128)(2,1)S(1)}, u32[]{:S(2)}, u32[]{:S(2)}) collective-permute-start(bf16[8,2048]{1,0:T(8,128)(2,1)S(1)} %get-tuple-element.59), channel_id=1, source_target_pairs={{0,20},{4,16},{8,28},{12,24},{16,4},{20,0},{24,12},{28,8},{1,21},{... | collective-permute-start | bytes 98312 | tf_op jit(solution)/shard_map/ppermute | solution.py:245
  39.8 1.4 %collective-permute-start.21 = (bf16[8,2048]{1,0:T(8,128)(2,1)S(1)}, bf16[8,2048]{1,0:T(8,128)(2,1)S(1)}, u32[]{:S(2)}, u32[]{:S(2)}) collective-permute-start(bf16[8,2048]{1,0:T(8,128)(2,1)S(1)} %get-tuple-element.60), channel_id=1, source_target_pairs={{0,24},{4,28},{8,16},{12,20},{16,8},{20,12},{24,0},{28,4},{1,25},{... | collective-permute-start | bytes 98312 | tf_op jit(solution)/shard_map/ppermute | solution.py:245
  41.2 1.3 %collective-permute-done.19.refs_0_.refs_8_ = bf16[8,2048]{1,0:T(8,128)(2,1)S(1)} collective-permute-done((bf16[8,2048]{1,0:T(8,128)(2,1)S(1)}, bf16[8,2048]{1,0:T(8,128)(2,1)S(1)}, u32[]{:S(2)}, u32[]{:S(2)}) %collective-permute-start.19) | collective-permute-done | bytes 32800 | tf_op jit(solution)/shard_map/ppermute | solution.py:245
  43.2 1.1 %collective-permute-start.15 = (bf16[16,2048]{1,0:T(8,128)(2,1)S(1)}, bf16[16,2048]{1,0:T(8,128)(2,1)S(1)}, u32[]{:S(2)}, u32[]{:S(2)}) collective-permute-start(bf16[16,2048]{1,0:T(8,128)(2,1)S(1)} %get-tuple-element.54), channel_id=1, source_target_pairs={{0,16},{4,20},{8,24},{12,28},{16,0},{20,4},{24,8},{28,12},{1,17},{... | collective-permute-start | bytes 196616 | tf_op jit(solution)/shard_map/ppermute | solution.py:245
  44.3 1.2 %collective-permute-done.21.refs_2_.refs_10_ = bf16[8,2048]{1,0:T(8,128)(2,1)S(1)} collective-permute-done((bf16[8,2048]{1,0:T(8,128)(2,1)S(1)}, bf16[8,2048]{1,0:T(8,128)(2,1)S(1)}, u32[]{:S(2)}, u32[]{:S(2)}) %collective-permute-start.21) | collective-permute-done | bytes 32800 | tf_op jit(solution)/shard_map/ppermute | solution.py:245
  45.5 1.6 %collective-permute-start.16 = (bf16[16,2048]{1,0:T(8,128)(2,1)S(1)}, bf16[16,2048]{1,0:T(8,128)(2,1)S(1)}, u32[]{:S(2)}, u32[]{:S(2)}) collective-permute-start(bf16[16,2048]{1,0:T(8,128)(2,1)S(1)} %get-tuple-element.55), channel_id=1, source_target_pairs={{0,20},{4,16},{8,28},{12,24},{16,4},{20,0},{24,12},{28,8},{1,21},{... | collective-permute-start | bytes 196616 | tf_op jit(solution)/shard_map/ppermute | solution.py:245
  47.9 2.1 %collective-permute-start.17 = (bf16[16,2048]{1,0:T(8,128)(2,1)S(1)}, bf16[16,2048]{1,0:T(8,128)(2,1)S(1)}, u32[]{:S(2)}, u32[]{:S(2)}) collective-permute-start(bf16[16,2048]{1,0:T(8,128)(2,1)S(1)} %get-tuple-element.56), channel_id=1, source_target_pairs={{0,24},{4,28},{8,16},{12,20},{16,8},{20,12},{24,0},{28,4},{1,25},{... | collective-permute-start | bytes 196616 | tf_op jit(solution)/shard_map/ppermute | solution.py:245
  50.0 1.2 %collective-permute-start.18 = (bf16[16,2048]{1,0:T(8,128)(2,1)S(1)}, bf16[16,2048]{1,0:T(8,128)(2,1)S(1)}, u32[]{:S(2)}, u32[]{:S(2)}) collective-permute-start(bf16[16,2048]{1,0:T(8,128)(2,1)S(1)} %get-tuple-element.57), channel_id=1, source_target_pairs={{0,28},{4,24},{8,20},{12,16},{16,12},{20,8},{24,4},{28,0},{1,29},{... | collective-permute-start | bytes 196616 | tf_op jit(solution)/shard_map/ppermute | solution.py:245
  52.2 4.2 %collective-permute-done.16.refs_5_ = bf16[16,2048]{1,0:T(8,128)(2,1)S(1)} collective-permute-done((bf16[16,2048]{1,0:T(8,128)(2,1)S(1)}, bf16[16,2048]{1,0:T(8,128)(2,1)S(1)}, u32[]{:S(2)}, u32[]{:S(2)}) %collective-permute-start.16) | collective-permute-done | bytes 65568 | tf_op jit(solution)/shard_map/ppermute | solution.py:245
  56.4 1.6 %collective-permute-start.5 = (bf16[32,2048]{1,0:T(8,128)(2,1)S(1)}, bf16[32,2048]{1,0:T(8,128)(2,1)S(1)}, u32[]{:S(2)}, u32[]{:S(2)}) collective-permute-start(bf16[32,2048]{1,0:T(8,128)(2,1)S(1)} %get-tuple-element.42), channel_id=1, source_target_pairs={{0,12},{4,8},{8,4},{12,0},{16,28},{20,24},{24,20},{28,16},{1,13},{... | collective-permute-start | bytes 393224 | tf_op jit(solution)/shard_map/ppermute | solution.py:245
  58.0 1.0 %collective-permute-start.23 = (bf16[32,2048]{1,0:T(8,128)(2,1)S(1)}, bf16[32,2048]{1,0:T(8,128)(2,1)S(1)}, u32[]{:S(2)}, u32[]{:S(2)}) collective-permute-start(bf16[32,2048]{1,0:T(8,128)(2,1)S(1)} %shard_map.63), channel_id=1, source_target_pairs={{0,2},{1,3},{2,0},{3,1},{4,6},{5,7},{6,4},{7,5},{8,10},{9,11},{10,... | collective-permute-start | bytes 393224 | tf_op jit(solution)/shard_map/ppermute | solution.py:245
  59.1 1.1 %collective-permute-start.25 = (bf16[1,512,256]{2,1,0:T(8,128)(2,1)S(1)}, bf16[1,512,256]{2,1,0:T(8,128)(2,1)S(1)}, u32[]{:S(2)}, u32[]{:S(2)}) collective-permute-start(bf16[1,512,256]{2,1,0:T(8,128)(2,1)S(1)} %fusion.3), channel_id=1, source_target_pairs={{0,2},{1,3},{2,0},{3,1},{4,6},{5,7},{6,4},{7,5},{8,10},{9,11},{10,... | collective-permute-start | bytes 786440 | tf_op jit(solution)/shard_map/ppermute | solution.py:245
  60.2 2.6 %collective-permute-done.4.refs_2_ = bf16[32,2048]{1,0:T(8,128)(2,1)S(1)} collective-permute-done((bf16[32,2048]{1,0:T(8,128)(2,1)S(1)}, bf16[32,2048]{1,0:T(8,128)(2,1)S(1)}, u32[]{:S(2)}, u32[]{:S(2)}) %collective-permute-start.4) | collective-permute-done | bytes 131104 | tf_op jit(solution)/shard_map/ppermute | solution.py:245
  62.8 0.9 %collective-permute-done.5.refs_3_ = bf16[32,2048]{1,0:T(8,128)(2,1)S(1)} collective-permute-done((bf16[32,2048]{1,0:T(8,128)(2,1)S(1)}, bf16[32,2048]{1,0:T(8,128)(2,1)S(1)}, u32[]{:S(2)}, u32[]{:S(2)}) %collective-permute-start.5) | collective-permute-done | bytes 131104 | tf_op jit(solution)/shard_map/ppermute | solution.py:245
  64.4 1.1 %shard_map.64 = bf16[128,2048]{1,0:T(8,128)(2,1)} custom-call(bf16[256,128]{1,0:T(8,128)(2,1)S(1)} %get-tuple-element.34.select_ref, bf16[32,2048]{1,0:T(8,128)(2,1)S(1)} %get-tuple-element.39.refs_0_, bf16[32,2048]{1,0:T(8,128)(2,1)S(1)} %collective-permute-done.3.refs_1_, bf16[32,2048]{1,0:T(8,128)(2,1)S(1)} %collective-permute-done.4.refs_2_, ...), custom_call_target="tpu_custom_call" | custom-call | flops 134217728 | bytes 1048576 | tf_op jit(solution)/shard_map/pallas_call | solution.py:228
  66.2 3.3 %collective-permute-done.25 = bf16[1,512,256]{2,1,0:T(8,128)(2,1)S(1)} collective-permute-done((bf16[1,512,256]{2,1,0:T(8,128)(2,1)S(1)}, bf16[1,512,256]{2,1,0:T(8,128)(2,1)S(1)}, u32[]{:S(2)}, u32[]{:S(2)}) %collective-permute-start.25) | collective-permute-done | bytes 262176 | tf_op jit(solution)/shard_map/ppermute | solution.py:245
  69.7 4.6 %collective-permute-done.27 = bf16[1,512,256]{2,1,0:T(8,128)(2,1)S(1)} collective-permute-done((bf16[1,512,256]{2,1,0:T(8,128)(2,1)S(1)}, bf16[1,512,256]{2,1,0:T(8,128)(2,1)S(1)}, u32[]{:S(2)}, u32[]{:S(2)}) %collective-permute-start.27) | collective-permute-done | bytes 262176 | tf_op jit(solution)/shard_map/ppermute | solution.py:245
  74.4 1.1 %maximum_bitcast_fusion = f32[1,512,512]{2,1,0:T(8,128)} fusion(f32[512,256]{1,0:T(8,128)S(1)} %fusion.2, f32[512,256]{1,0:T(8,128)S(1)} %fusion.5), kind=kLoop, calls=%fused_computation | loop fusion | flops 262144 | bytes 2097152 | tf_op jit(solution)/shard_map/broadcast_in_dim | solution.py:437
  (47 shorter events, 8.4 us)
Async XLA Ops:
  0.6 1.0 %copy-start.2 = (bf16[128,2048]{1,0:T(8,128)(2,1)S(1)}, bf16[128,2048]{1,0:T(8,128)(2,1)}, u32[]{:S(2)}) copy-start(bf16[128,2048]{1,0:T(8,128)(2,1)} %refs_1_.1) | copy-start | bytes 1572868
  1.7 0.8 %copy-start.3 = (bf16[128,256]{1,0:T(8,128)(2,1)S(1)}, bf16[128,256]{1,0:T(8,128)(2,1)}, u32[]{:S(2)}) copy-start(bf16[128,256]{1,0:T(8,128)(2,1)} %refs_2_.1) | copy-start | bytes 196612
  4.1 8.0 %collective-permute-start.6 = (bf16[16,2304]{1,0:T(8,128)(2,1)S(1)}, bf16[16,2304]{1,0:T(8,128)(2,1)S(1)}, u32[]{:S(2)}, u32[]{:S(2)}) collective-permute-start(bf16[16,2304]{1,0:T(8,128)(2,1)S(1)} %get-tuple-element.43), channel_id=1, source_target_pairs={{0,16},{4,20},{8,24},{12,28},{16,0},{20,4},{24,8},{28,12},{1,17},{... | collective-permute-start | bytes 221192 | tf_op jit(solution)/shard_map/ppermute | solution.py:245
  8.3 10.3 %collective-permute-start.10 = (bf16[32,2432]{1,0:T(8,128)(2,1)S(1)}, bf16[32,2432]{1,0:T(8,128)(2,1)S(1)}, u32[]{:S(2)}, u32[]{:S(2)}) collective-permute-start(bf16[32,2432]{1,0:T(8,128)(2,1)S(1)} %get-tuple-element.48), channel_id=1, source_target_pairs={{0,2},{1,3},{2,0},{3,1},{4,6},{5,7},{6,4},{7,5},{8,10},{9,11},{10,... | collective-permute-start | bytes 466952 | tf_op jit(solution)/shard_map/ppermute | solution.py:245
  9.8 6.6 %collective-permute-start.7 = (bf16[16,2304]{1,0:T(8,128)(2,1)S(1)}, bf16[16,2304]{1,0:T(8,128)(2,1)S(1)}, u32[]{:S(2)}, u32[]{:S(2)}) collective-permute-start(bf16[16,2304]{1,0:T(8,128)(2,1)S(1)} %get-tuple-element.44), channel_id=1, source_target_pairs={{0,20},{4,16},{8,28},{12,24},{16,4},{20,0},{24,12},{28,8},{1,21},{... | collective-permute-start | bytes 221192 | tf_op jit(solution)/shard_map/ppermute | solution.py:245
  9.8 14.3 %collective-permute-start = (bf16[32,2304]{1,0:T(8,128)(2,1)S(1)}, bf16[32,2304]{1,0:T(8,128)(2,1)S(1)}, u32[]{:S(2)}, u32[]{:S(2)}) collective-permute-start(bf16[32,2304]{1,0:T(8,128)(2,1)S(1)} %get-tuple-element.36), channel_id=1, source_target_pairs={{0,4},{4,0},{8,12},{12,8},{16,20},{20,16},{24,28},{28,24},{1,5},{5... | collective-permute-start | bytes 442376 | tf_op jit(solution)/shard_map/ppermute | solution.py:245
  10.2 15.6 %collective-permute-start.1 = (bf16[32,2304]{1,0:T(8,128)(2,1)S(1)}, bf16[32,2304]{1,0:T(8,128)(2,1)S(1)}, u32[]{:S(2)}, u32[]{:S(2)}) collective-permute-start(bf16[32,2304]{1,0:T(8,128)(2,1)S(1)} %get-tuple-element.37), channel_id=1, source_target_pairs={{0,8},{4,12},{8,0},{12,4},{16,24},{20,28},{24,16},{28,20},{1,9},{5... | collective-permute-start | bytes 442376 | tf_op jit(solution)/shard_map/ppermute | solution.py:245
  12.2 13.9 %collective-permute-start.2 = (bf16[32,2304]{1,0:T(8,128)(2,1)S(1)}, bf16[32,2304]{1,0:T(8,128)(2,1)S(1)}, u32[]{:S(2)}, u32[]{:S(2)}) collective-permute-start(bf16[32,2304]{1,0:T(8,128)(2,1)S(1)} %get-tuple-element.38), channel_id=1, source_target_pairs={{0,12},{4,8},{8,4},{12,0},{16,28},{20,24},{24,20},{28,16},{1,13},{... | collective-permute-start | bytes 442376 | tf_op jit(solution)/shard_map/ppermute | solution.py:245
  16.4 7.6 %collective-permute-start.8 = (bf16[16,2304]{1,0:T(8,128)(2,1)S(1)}, bf16[16,2304]{1,0:T(8,128)(2,1)S(1)}, u32[]{:S(2)}, u32[]{:S(2)}) collective-permute-start(bf16[16,2304]{1,0:T(8,128)(2,1)S(1)} %get-tuple-element.45), channel_id=1, source_target_pairs={{0,24},{4,28},{8,16},{12,20},{16,8},{20,12},{24,0},{28,4},{1,25},{... | collective-permute-start | bytes 221192 | tf_op jit(solution)/shard_map/ppermute | solution.py:245
  18.6 14.5 %collective-permute-start.9 = (bf16[16,2304]{1,0:T(8,128)(2,1)S(1)}, bf16[16,2304]{1,0:T(8,128)(2,1)S(1)}, u32[]{:S(2)}, u32[]{:S(2)}) collective-permute-start(bf16[16,2304]{1,0:T(8,128)(2,1)S(1)} %get-tuple-element.46), channel_id=1, source_target_pairs={{0,28},{4,24},{8,20},{12,16},{16,12},{20,8},{24,4},{28,0},{1,29},{... | collective-permute-start | bytes 221192 | tf_op jit(solution)/shard_map/ppermute | solution.py:245
  24.1 9.0 %collective-permute-start.11 = (bf16[8,2304]{1,0:T(8,128)(2,1)S(1)}, bf16[8,2304]{1,0:T(8,128)(2,1)S(1)}, u32[]{:S(2)}, u32[]{:S(2)}) collective-permute-start(bf16[8,2304]{1,0:T(8,128)(2,1)S(1)} %get-tuple-element.49), channel_id=1, source_target_pairs={{0,16},{4,20},{8,24},{12,28},{16,0},{20,4},{24,8},{28,12},{1,17},{... | collective-permute-start | bytes 110600 | tf_op jit(solution)/shard_map/ppermute | solution.py:245
  24.1 9.0 %collective-permute-start.12 = (bf16[8,2304]{1,0:T(8,128)(2,1)S(1)}, bf16[8,2304]{1,0:T(8,128)(2,1)S(1)}, u32[]{:S(2)}, u32[]{:S(2)}) collective-permute-start(bf16[8,2304]{1,0:T(8,128)(2,1)S(1)} %get-tuple-element.50), channel_id=1, source_target_pairs={{0,20},{4,16},{8,28},{12,24},{16,4},{20,0},{24,12},{28,8},{1,21},{... | collective-permute-start | bytes 110600 | tf_op jit(solution)/shard_map/ppermute | solution.py:245
  25.8 7.3 %collective-permute-start.13 = (bf16[8,2304]{1,0:T(8,128)(2,1)S(1)}, bf16[8,2304]{1,0:T(8,128)(2,1)S(1)}, u32[]{:S(2)}, u32[]{:S(2)}) collective-permute-start(bf16[8,2304]{1,0:T(8,128)(2,1)S(1)} %get-tuple-element.51), channel_id=1, source_target_pairs={{0,24},{4,28},{8,16},{12,20},{16,8},{20,12},{24,0},{28,4},{1,25},{... | collective-permute-start | bytes 110600 | tf_op jit(solution)/shard_map/ppermute | solution.py:245
  26.1 7.0 %collective-permute-start.14 = (bf16[8,2304]{1,0:T(8,128)(2,1)S(1)}, bf16[8,2304]{1,0:T(8,128)(2,1)S(1)}, u32[]{:S(2)}, u32[]{:S(2)}) collective-permute-start(bf16[8,2304]{1,0:T(8,128)(2,1)S(1)} %get-tuple-element.52), channel_id=1, source_target_pairs={{0,28},{4,24},{8,20},{12,16},{16,12},{20,8},{24,4},{28,0},{1,29},{... | collective-permute-start | bytes 110600 | tf_op jit(solution)/shard_map/ppermute | solution.py:245
  30.3 1.6 %copy-start = (bf16[1,2048,512]{2,1,0:T(8,128)(2,1)S(1)}, bf16[1,2048,512]{2,1,0:T(8,128)(2,1)}, u32[]{:S(2)}) copy-start(bf16[1,2048,512]{2,1,0:T(8,128)(2,1)} %param.7) | copy-start | bytes 6291460
  31.9 1.6 %copy-start.1 = (bf16[1,2048,512]{2,1,0:T(8,128)(2,1)S(1)}, bf16[1,2048,512]{2,1,0:T(8,128)(2,1)}, u32[]{:S(2)}) copy-start(bf16[1,2048,512]{2,1,0:T(8,128)(2,1)} %param.7) | copy-start | bytes 6291460
  35.2 14.8 %collective-permute-start.24 = (bf16[2,512,256]{2,1,0:T(8,128)(2,1)S(1)}, bf16[2,512,256]{2,1,0:T(8,128)(2,1)S(1)}, u32[]{:S(2)}, u32[]{:S(2)}) collective-permute-start(bf16[2,512,256]{2,1,0:T(8,128)(2,1)S(1)} %get-tuple-element.63), channel_id=1, source_target_pairs={{0,1},{1,0},{2,3},{3,2},{4,5},{5,4},{6,7},{7,6},{8,9},{9,8},{10,11... | collective-permute-start | bytes 1572872 | tf_op jit(solution)/shard_map/ppermute | solution.py:245
  36.8 28.7 %collective-permute-start.26 = (bf16[2,512,256]{2,1,0:T(8,128)(2,1)S(1)}, bf16[2,512,256]{2,1,0:T(8,128)(2,1)S(1)}, u32[]{:S(2)}, u32[]{:S(2)}) collective-permute-start(bf16[2,512,256]{2,1,0:T(8,128)(2,1)S(1)} %get-tuple-element.65), channel_id=1, source_target_pairs={{0,2},{1,3},{2,0},{3,1},{4,6},{5,7},{6,4},{7,5},{8,10},{9,11},{10,... | collective-permute-start | bytes 1572872 | tf_op jit(solution)/shard_map/ppermute | solution.py:245
  37.0 5.4 %collective-permute-start.19 = (bf16[8,2048]{1,0:T(8,128)(2,1)S(1)}, bf16[8,2048]{1,0:T(8,128)(2,1)S(1)}, u32[]{:S(2)}, u32[]{:S(2)}) collective-permute-start(bf16[8,2048]{1,0:T(8,128)(2,1)S(1)} %get-tuple-element.58), channel_id=1, source_target_pairs={{0,16},{4,20},{8,24},{12,28},{16,0},{20,4},{24,8},{28,12},{1,17},{... | collective-permute-start | bytes 98312 | tf_op jit(solution)/shard_map/ppermute | solution.py:245
  37.5 5.7 %collective-permute-start.20 = (bf16[8,2048]{1,0:T(8,128)(2,1)S(1)}, bf16[8,2048]{1,0:T(8,128)(2,1)S(1)}, u32[]{:S(2)}, u32[]{:S(2)}) collective-permute-start(bf16[8,2048]{1,0:T(8,128)(2,1)S(1)} %get-tuple-element.59), channel_id=1, source_target_pairs={{0,20},{4,16},{8,28},{12,24},{16,4},{20,0},{24,12},{28,8},{1,21},{... | collective-permute-start | bytes 98312 | tf_op jit(solution)/shard_map/ppermute | solution.py:245
  39.8 5.7 %collective-permute-start.21 = (bf16[8,2048]{1,0:T(8,128)(2,1)S(1)}, bf16[8,2048]{1,0:T(8,128)(2,1)S(1)}, u32[]{:S(2)}, u32[]{:S(2)}) collective-permute-start(bf16[8,2048]{1,0:T(8,128)(2,1)S(1)} %get-tuple-element.60), channel_id=1, source_target_pairs={{0,24},{4,28},{8,16},{12,20},{16,8},{20,12},{24,0},{28,4},{1,25},{... | collective-permute-start | bytes 98312 | tf_op jit(solution)/shard_map/ppermute | solution.py:245
  42.4 5.5 %collective-permute-start.22 = (bf16[8,2048]{1,0:T(8,128)(2,1)S(1)}, bf16[8,2048]{1,0:T(8,128)(2,1)S(1)}, u32[]{:S(2)}, u32[]{:S(2)}) collective-permute-start(bf16[8,2048]{1,0:T(8,128)(2,1)S(1)} %get-tuple-element.61), channel_id=1, source_target_pairs={{0,28},{4,24},{8,20},{12,16},{16,12},{20,8},{24,4},{28,0},{1,29},{... | collective-permute-start | bytes 98312 | tf_op jit(solution)/shard_map/ppermute | solution.py:245
  43.2 8.9 %collective-permute-start.15 = (bf16[16,2048]{1,0:T(8,128)(2,1)S(1)}, bf16[16,2048]{1,0:T(8,128)(2,1)S(1)}, u32[]{:S(2)}, u32[]{:S(2)}) collective-permute-start(bf16[16,2048]{1,0:T(8,128)(2,1)S(1)} %get-tuple-element.54), channel_id=1, source_target_pairs={{0,16},{4,20},{8,24},{12,28},{16,0},{20,4},{24,8},{28,12},{1,17},{... | collective-permute-start | bytes 196616 | tf_op jit(solution)/shard_map/ppermute | solution.py:245
  45.5 10.9 %collective-permute-start.16 = (bf16[16,2048]{1,0:T(8,128)(2,1)S(1)}, bf16[16,2048]{1,0:T(8,128)(2,1)S(1)}, u32[]{:S(2)}, u32[]{:S(2)}) collective-permute-start(bf16[16,2048]{1,0:T(8,128)(2,1)S(1)} %get-tuple-element.55), channel_id=1, source_target_pairs={{0,20},{4,16},{8,28},{12,24},{16,4},{20,0},{24,12},{28,8},{1,21},{... | collective-permute-start | bytes 196616 | tf_op jit(solution)/shard_map/ppermute | solution.py:245
  47.9 8.5 %collective-permute-start.17 = (bf16[16,2048]{1,0:T(8,128)(2,1)S(1)}, bf16[16,2048]{1,0:T(8,128)(2,1)S(1)}, u32[]{:S(2)}, u32[]{:S(2)}) collective-permute-start(bf16[16,2048]{1,0:T(8,128)(2,1)S(1)} %get-tuple-element.56), channel_id=1, source_target_pairs={{0,24},{4,28},{8,16},{12,20},{16,8},{20,12},{24,0},{28,4},{1,25},{... | collective-permute-start | bytes 196616 | tf_op jit(solution)/shard_map/ppermute | solution.py:245
  50.0 8.0 %collective-permute-start.18 = (bf16[16,2048]{1,0:T(8,128)(2,1)S(1)}, bf16[16,2048]{1,0:T(8,128)(2,1)S(1)}, u32[]{:S(2)}, u32[]{:S(2)}) collective-permute-start(bf16[16,2048]{1,0:T(8,128)(2,1)S(1)} %get-tuple-element.57), channel_id=1, source_target_pairs={{0,28},{4,24},{8,20},{12,16},{16,12},{20,8},{24,4},{28,0},{1,29},{... | collective-permute-start | bytes 196616 | tf_op jit(solution)/shard_map/ppermute | solution.py:245
  52.1 7.0 %collective-permute-start.3 = (bf16[32,2048]{1,0:T(8,128)(2,1)S(1)}, bf16[32,2048]{1,0:T(8,128)(2,1)S(1)}, u32[]{:S(2)}, u32[]{:S(2)}) collective-permute-start(bf16[32,2048]{1,0:T(8,128)(2,1)S(1)} %get-tuple-element.40), channel_id=1, source_target_pairs={{0,4},{4,0},{8,12},{12,8},{16,20},{20,16},{24,28},{28,24},{1,5},{5... | collective-permute-start | bytes 393224 | tf_op jit(solution)/shard_map/ppermute | solution.py:245
  56.4 6.4 %collective-permute-start.4 = (bf16[32,2048]{1,0:T(8,128)(2,1)S(1)}, bf16[32,2048]{1,0:T(8,128)(2,1)S(1)}, u32[]{:S(2)}, u32[]{:S(2)}) collective-permute-start(bf16[32,2048]{1,0:T(8,128)(2,1)S(1)} %get-tuple-element.41), channel_id=1, source_target_pairs={{0,8},{4,12},{8,0},{12,4},{16,24},{20,28},{24,16},{28,20},{1,9},{5... | collective-permute-start | bytes 393224 | tf_op jit(solution)/shard_map/ppermute | solution.py:245
  56.4 7.3 %collective-permute-start.5 = (bf16[32,2048]{1,0:T(8,128)(2,1)S(1)}, bf16[32,2048]{1,0:T(8,128)(2,1)S(1)}, u32[]{:S(2)}, u32[]{:S(2)}) collective-permute-start(bf16[32,2048]{1,0:T(8,128)(2,1)S(1)} %get-tuple-element.42), channel_id=1, source_target_pairs={{0,12},{4,8},{8,4},{12,0},{16,28},{20,24},{24,20},{28,16},{1,13},{... | collective-permute-start | bytes 393224 | tf_op jit(solution)/shard_map/ppermute | solution.py:245
  58.0 6.4 %collective-permute-start.23 = (bf16[32,2048]{1,0:T(8,128)(2,1)S(1)}, bf16[32,2048]{1,0:T(8,128)(2,1)S(1)}, u32[]{:S(2)}, u32[]{:S(2)}) collective-permute-start(bf16[32,2048]{1,0:T(8,128)(2,1)S(1)} %shard_map.63), channel_id=1, source_target_pairs={{0,2},{1,3},{2,0},{3,1},{4,6},{5,7},{6,4},{7,5},{8,10},{9,11},{10,... | collective-permute-start | bytes 393224 | tf_op jit(solution)/shard_map/ppermute | solution.py:245
  59.1 10.5 %collective-permute-start.25 = (bf16[1,512,256]{2,1,0:T(8,128)(2,1)S(1)}, bf16[1,512,256]{2,1,0:T(8,128)(2,1)S(1)}, u32[]{:S(2)}, u32[]{:S(2)}) collective-permute-start(bf16[1,512,256]{2,1,0:T(8,128)(2,1)S(1)} %fusion.3), channel_id=1, source_target_pairs={{0,2},{1,3},{2,0},{3,1},{4,6},{5,7},{6,4},{7,5},{8,10},{9,11},{10,... | collective-permute-start | bytes 786440 | tf_op jit(solution)/shard_map/ppermute | solution.py:245
  65.6 8.7 %collective-permute-start.27 = (bf16[1,512,256]{2,1,0:T(8,128)(2,1)S(1)}, bf16[1,512,256]{2,1,0:T(8,128)(2,1)S(1)}, u32[]{:S(2)}, u32[]{:S(2)}) collective-permute-start(bf16[1,512,256]{2,1,0:T(8,128)(2,1)S(1)} %fusion), channel_id=1, source_target_pairs={{0,1},{1,0},{2,3},{3,2},{4,5},{5,4},{6,7},{7,6},{8,9},{9,8},{10,11... | collective-permute-start | bytes 786440 | tf_op jit(solution)/shard_map/ppermute | solution.py:245
  (1 other events, 0.7 us)

commit v2 on v1

--- a/solution.py
+++ b/solution.py
@@ -160,6 +160,12 @@
         unstack(dot_nt(pre_grad, weights_ref[columns, :]), pieces, columns)
 
 
+def load_kernel(source, target, sem):
+    copy = pltpu.make_async_copy(source, target, sem)
+    copy.start()
+    copy.wait()
+
+
 def near_kernel(count, *refs):
     pieces, (weights_ref, pre_ref), grads = refs[:count], refs[count : count + 2], refs[count + 2 :]
     width = weights_ref.shape[0]
@@ -225,6 +231,11 @@
 
 
 def call(kernel, out_shapes, scratch, flops, moved, args, specs=None, vmem=24 << 20):
+    if specs is not None:
+        args = [
+            pltpu.with_memory_space_constraint(arg, pltpu.HBM) if spec is HBM else arg
+            for arg, spec in zip(args, specs)
+        ]
     return pl.pallas_call(
         kernel,
         out_shape=out_shapes,
@@ -290,7 +301,6 @@
         2 * slots * joined,
         (routing.reshape(1, rows), tokens_in, hidden_grad),
         specs=[HBM] * 3,
-        vmem=40 << 20,
     )
     near, low = pieces[:half], pieces[half:]
     landed = flip(spilled, "group", groups // 2)
@@ -306,6 +316,15 @@
     )
     up = [flip(up[k], "expert", half + k) for k in range(half)]
 
+    weights = call(
+        load_kernel,
+        shape(weights.shape),
+        [pltpu.SemaphoreType.DMA],
+        0,
+        weights.size * 2,
+        (weights,),
+        specs=[HBM],
+    )
     near_slots, far_slots = half * full, half * (low_rows + up_rows)
     near_pre, *near_grads = call(
         functools.partial(near_kernel, half),

time: 75.8 us -> 73.5 us (0.970)
  local copies, waits for them, and re-layouts: 4.48 us -> 0 us
  Pallas kernels: 5.54 us -> 7.76 us
    unnamed x10 -> x0, local copies, waits for them, and re-layouts: 4.48 us -> none
    pallas_call x6 -> x7, Pallas kernels: 5.54 us -> 7.76 us  [call(): pl.pallas_call(kernel, out_shape=out_shapes, in_specs=specs or [VMEM] * l...]
  transfers between devices with their start and end apart: 28 -> 28, of which waited for: 13 -> 15; matrix products, arithmetic and copies ran while one was open for 1% -> 1% of each run, Pallas kernels for 4% -> 6%
where the time goes in v2:
time: 73.5 us; the launch traced here: 73.3 us
  starting transfers between devices  33.6 us (46%)
  waiting for transfers between devices  29.5 us (40%)
  Pallas kernels  7.76 us (11%)
  other arithmetic  1.65 us (2%)
  between operations  0.76 us (1%)
    ppermute x28, starting transfers between devices, flip(): return lax.ppermute(value, axis, [(i, i ^ mask) for i in range(size)])  33.6 us
    ppermute x28, waiting for transfers between devices, flip(): return lax.ppermute(value, axis, [(i, i ^ mask) for i in range(size)])  29.5 us
    pallas_call x7, Pallas kernels, call(): pl.pallas_call(kernel, out_shape=out_shapes, in_specs=specs or [VMEM] * l...  7.76 us
  transfers between devices with their start and end apart: 28, of which 15 were waited for; matrix products, arithmetic and copies ran while one was open for 1% of the time, Pallas kernels for 6%

profile of v2, /device:TPU:0, one launch (start us, length us, event | category | flops | bytes accessed | tf_op | source)
XLA Modules:
  0.0 73.3 jit_solution(16457550156242910314)
XLA Ops:
  0.6 1.6 %shard_map.59 = (bf16[256,128]{1,0:T(8,128)(2,1)S(1)}, bf16[32,2432]{1,0:T(8,128)(2,1)S(1)}, bf16[32,2304]{1,0:T(8,128)(2,1)S(1)}, bf16[32,2304]{1,0:T(8,128)(2,...) custom-call(s32[1,128]{1,0:T(1,128)} %bitcast.9, ...), custom_call_target="tpu_custom_call" | custom-call | flops 150994944 | bytes 1179648 | tf_op jit(solution)/shard_map/pallas_call | solution.py:239
  2.2 4.1 %collective-permute-start.6 = (bf16[16,2304]{1,0:T(8,128)(2,1)S(1)}, bf16[16,2304]{1,0:T(8,128)(2,1)S(1)}, u32[]{:S(2)}, u32[]{:S(2)}) collective-permute-start(bf16[16,2304]{1,0:T(8,128)(2,1)S(1)} %get-tuple-element.43), channel_id=1, source_target_pairs={{0,16},{4,20},{8,24},{12,28},{16,0},{20,4},{24,8},{28,12},{1,17},{... | collective-permute-start | bytes 221192 | tf_op jit(solution)/shard_map/ppermute | solution.py:256
  6.3 1.5 %collective-permute-start.10 = (bf16[32,2432]{1,0:T(8,128)(2,1)S(1)}, bf16[32,2432]{1,0:T(8,128)(2,1)S(1)}, u32[]{:S(2)}, u32[]{:S(2)}) collective-permute-start(bf16[32,2432]{1,0:T(8,128)(2,1)S(1)} %get-tuple-element.48), channel_id=1, source_target_pairs={{0,2},{1,3},{2,0},{3,1},{4,6},{5,7},{6,4},{7,5},{8,10},{9,11},{10,... | collective-permute-start | bytes 466952 | tf_op jit(solution)/shard_map/ppermute | solution.py:256
  8.3 1.6 %collective-permute-start.1 = (bf16[32,2304]{1,0:T(8,128)(2,1)S(1)}, bf16[32,2304]{1,0:T(8,128)(2,1)S(1)}, u32[]{:S(2)}, u32[]{:S(2)}) collective-permute-start(bf16[32,2304]{1,0:T(8,128)(2,1)S(1)} %get-tuple-element.37), channel_id=1, source_target_pairs={{0,8},{4,12},{8,0},{12,4},{16,24},{20,28},{24,16},{28,20},{1,9},{5... | collective-permute-start | bytes 442376 | tf_op jit(solution)/shard_map/ppermute | solution.py:256
  10.3 4.2 %collective-permute-done.7.refs_5_ = bf16[16,2304]{1,0:T(8,128)(2,1)S(1)} collective-permute-done((bf16[16,2304]{1,0:T(8,128)(2,1)S(1)}, bf16[16,2304]{1,0:T(8,128)(2,1)S(1)}, u32[]{:S(2)}, u32[]{:S(2)}) %collective-permute-start.7) | collective-permute-done | bytes 73760 | tf_op jit(solution)/shard_map/ppermute | solution.py:256
  14.5 2.1 %collective-permute-start.8 = (bf16[16,2304]{1,0:T(8,128)(2,1)S(1)}, bf16[16,2304]{1,0:T(8,128)(2,1)S(1)}, u32[]{:S(2)}, u32[]{:S(2)}) collective-permute-start(bf16[16,2304]{1,0:T(8,128)(2,1)S(1)} %get-tuple-element.45), channel_id=1, source_target_pairs={{0,24},{4,28},{8,16},{12,20},{16,8},{20,12},{24,0},{28,4},{1,25},{... | collective-permute-start | bytes 221192 | tf_op jit(solution)/shard_map/ppermute | solution.py:256
  16.7 1.6 %shard_map.60.refs_4_.refs_13_ = bf16[2048,512]{1,0:T(8,128)(2,1)S(1)} custom-call(bf16[2048,512]{1,0:T(8,128)(2,1)} %bitcast.8), custom_call_target="tpu_custom_call" | custom-call | bytes 2097152 | tf_op jit(solution)/shard_map/pallas_call | solution.py:239
  18.6 3.5 %collective-permute-done.8.refs_6_ = bf16[16,2304]{1,0:T(8,128)(2,1)S(1)} collective-permute-done((bf16[16,2304]{1,0:T(8,128)(2,1)S(1)}, bf16[16,2304]{1,0:T(8,128)(2,1)S(1)}, u32[]{:S(2)}, u32[]{:S(2)}) %collective-permute-start.8) | collective-permute-done | bytes 73760 | tf_op jit(solution)/shard_map/ppermute | solution.py:256
  22.1 1.7 %collective-permute-start.12 = (bf16[8,2304]{1,0:T(8,128)(2,1)S(1)}, bf16[8,2304]{1,0:T(8,128)(2,1)S(1)}, u32[]{:S(2)}, u32[]{:S(2)}) collective-permute-start(bf16[8,2304]{1,0:T(8,128)(2,1)S(1)} %get-tuple-element.50), channel_id=1, source_target_pairs={{0,20},{4,16},{8,28},{12,24},{16,4},{20,0},{24,12},{28,8},{1,21},{... | collective-permute-start | bytes 110600 | tf_op jit(solution)/shard_map/ppermute | solution.py:256
  24.9 3.5 %collective-permute-start.14 = (bf16[8,2304]{1,0:T(8,128)(2,1)S(1)}, bf16[8,2304]{1,0:T(8,128)(2,1)S(1)}, u32[]{:S(2)}, u32[]{:S(2)}) collective-permute-start(bf16[8,2304]{1,0:T(8,128)(2,1)S(1)} %get-tuple-element.52), channel_id=1, source_target_pairs={{0,28},{4,24},{8,20},{12,16},{16,12},{20,8},{24,4},{28,0},{1,29},{... | collective-permute-start | bytes 110600 | tf_op jit(solution)/shard_map/ppermute | solution.py:256
  28.3 1.2 %shard_map.61 = (bf16[128,512]{1,0:T(8,128)(2,1)S(1)}, bf16[32,2048]{1,0:T(8,128)(2,1)S(1)}, bf16[32,2048]{1,0:T(8,128)(2,1)S(1)}, bf16[32,2048]{1,0:T(8,128)(2,1)S(1)}, bf16[32,2048]{1,0:T(8,128)(2,1)S(1)}) custom-call(bf16[32,2304]{1,0:T(8,128)(2,1)S(1)} %get-tuple-element.35.refs_0_, bf16[32,2304]{1,0:T(8,128)(2,1)S(1)} %collective-permute-done.refs_1_, ...), custom_call_target="tpu_custom_call" | custom-call | flops 536870912 | bytes 1179648 | tf_op jit(solution)/shard_map/pallas_call | solution.py:239
  30.5 1.8 %shard_map.63 = (bf16[16,2048]{1,0:T(8,128)(2,1)S(1)}, bf16[16,2048]{1,0:T(8,128)(2,1)S(1)}, bf16[16,2048]{1,0:T(8,128)(2,1)S(1)}, bf16[16,2048]{1,0:T(8,128)(2,...) custom-call(bf16[32,2304]{1,0:T(8,128)(2,1)S(1)} %get-tuple-element., ...), custom_call_target="tpu_custom_call" | custom-call | flops 1409286144 | bytes 2064384 | tf_op jit(solution)/shard_map/pallas_call | solution.py:239
  32.3 1.5 %collective-permute-start.24 = (bf16[2,512,256]{2,1,0:T(8,128)(2,1)S(1)}, bf16[2,512,256]{2,1,0:T(8,128)(2,1)S(1)}, u32[]{:S(2)}, u32[]{:S(2)}) collective-permute-start(bf16[2,512,256]{2,1,0:T(8,128)(2,1)S(1)} %get-tuple-element.63), channel_id=1, source_target_pairs={{0,1},{1,0},{2,3},{3,2},{4,5},{5,4},{6,7},{7,6},{8,9},{9,8},{10,11... | collective-permute-start | bytes 1572872 | tf_op jit(solution)/shard_map/ppermute | solution.py:256
  33.9 1.2 %collective-permute-start.26 = (bf16[2,512,256]{2,1,0:T(8,128)(2,1)S(1)}, bf16[2,512,256]{2,1,0:T(8,128)(2,1)S(1)}, u32[]{:S(2)}, u32[]{:S(2)}) collective-permute-start(bf16[2,512,256]{2,1,0:T(8,128)(2,1)S(1)} %get-tuple-element.65), channel_id=1, source_target_pairs={{0,2},{1,3},{2,0},{3,1},{4,6},{5,7},{6,4},{7,5},{8,10},{9,11},{10,... | collective-permute-start | bytes 1572872 | tf_op jit(solution)/shard_map/ppermute | solution.py:256
  35.6 2.3 %collective-permute-start.20 = (bf16[8,2048]{1,0:T(8,128)(2,1)S(1)}, bf16[8,2048]{1,0:T(8,128)(2,1)S(1)}, u32[]{:S(2)}, u32[]{:S(2)}) collective-permute-start(bf16[8,2048]{1,0:T(8,128)(2,1)S(1)} %get-tuple-element.59), channel_id=1, source_target_pairs={{0,20},{4,16},{8,28},{12,24},{16,4},{20,0},{24,12},{28,8},{1,21},{... | collective-permute-start | bytes 98312 | tf_op jit(solution)/shard_map/ppermute | solution.py:256
  37.9 1.4 %collective-permute-start.21 = (bf16[8,2048]{1,0:T(8,128)(2,1)S(1)}, bf16[8,2048]{1,0:T(8,128)(2,1)S(1)}, u32[]{:S(2)}, u32[]{:S(2)}) collective-permute-start(bf16[8,2048]{1,0:T(8,128)(2,1)S(1)} %get-tuple-element.60), channel_id=1, source_target_pairs={{0,24},{4,28},{8,16},{12,20},{16,8},{20,12},{24,0},{28,4},{1,25},{... | collective-permute-start | bytes 98312 | tf_op jit(solution)/shard_map/ppermute | solution.py:256
  39.2 1.3 %collective-permute-done.19.refs_0_.refs_8_ = bf16[8,2048]{1,0:T(8,128)(2,1)S(1)} collective-permute-done((bf16[8,2048]{1,0:T(8,128)(2,1)S(1)}, bf16[8,2048]{1,0:T(8,128)(2,1)S(1)}, u32[]{:S(2)}, u32[]{:S(2)}) %collective-permute-start.19) | collective-permute-done | bytes 32800 | tf_op jit(solution)/shard_map/ppermute | solution.py:256
  41.2 1.1 %collective-permute-start.15 = (bf16[16,2048]{1,0:T(8,128)(2,1)S(1)}, bf16[16,2048]{1,0:T(8,128)(2,1)S(1)}, u32[]{:S(2)}, u32[]{:S(2)}) collective-permute-start(bf16[16,2048]{1,0:T(8,128)(2,1)S(1)} %get-tuple-element.54), channel_id=1, source_target_pairs={{0,16},{4,20},{8,24},{12,28},{16,0},{20,4},{24,8},{28,12},{1,17},{... | collective-permute-start | bytes 196616 | tf_op jit(solution)/shard_map/ppermute | solution.py:256
  42.3 1.3 %collective-permute-done.21.refs_2_.refs_10_ = bf16[8,2048]{1,0:T(8,128)(2,1)S(1)} collective-permute-done((bf16[8,2048]{1,0:T(8,128)(2,1)S(1)}, bf16[8,2048]{1,0:T(8,128)(2,1)S(1)}, u32[]{:S(2)}, u32[]{:S(2)}) %collective-permute-start.21) | collective-permute-done | bytes 32800 | tf_op jit(solution)/shard_map/ppermute | solution.py:256
  44.4 1.3 %collective-permute-done.22.refs_3_.refs_11_ = bf16[8,2048]{1,0:T(8,128)(2,1)S(1)} collective-permute-done((bf16[8,2048]{1,0:T(8,128)(2,1)S(1)}, bf16[8,2048]{1,0:T(8,128)(2,1)S(1)}, u32[]{:S(2)}, u32[]{:S(2)}) %collective-permute-start.22) | collective-permute-done | bytes 32800 | tf_op jit(solution)/shard_map/ppermute | solution.py:256
  45.6 1.7 %collective-permute-start.17 = (bf16[16,2048]{1,0:T(8,128)(2,1)S(1)}, bf16[16,2048]{1,0:T(8,128)(2,1)S(1)}, u32[]{:S(2)}, u32[]{:S(2)}) collective-permute-start(bf16[16,2048]{1,0:T(8,128)(2,1)S(1)} %get-tuple-element.56), channel_id=1, source_target_pairs={{0,24},{4,28},{8,16},{12,20},{16,8},{20,12},{24,0},{28,4},{1,25},{... | collective-permute-start | bytes 196616 | tf_op jit(solution)/shard_map/ppermute | solution.py:256
  47.3 2.0 %collective-permute-start.18 = (bf16[16,2048]{1,0:T(8,128)(2,1)S(1)}, bf16[16,2048]{1,0:T(8,128)(2,1)S(1)}, u32[]{:S(2)}, u32[]{:S(2)}) collective-permute-start(bf16[16,2048]{1,0:T(8,128)(2,1)S(1)} %get-tuple-element.57), channel_id=1, source_target_pairs={{0,28},{4,24},{8,20},{12,16},{16,12},{20,8},{24,4},{28,0},{1,29},{... | collective-permute-start | bytes 196616 | tf_op jit(solution)/shard_map/ppermute | solution.py:256
  49.5 1.0 %collective-permute-done.15.refs_4_ = bf16[16,2048]{1,0:T(8,128)(2,1)S(1)} collective-permute-done((bf16[16,2048]{1,0:T(8,128)(2,1)S(1)}, bf16[16,2048]{1,0:T(8,128)(2,1)S(1)}, u32[]{:S(2)}, u32[]{:S(2)}) %collective-permute-start.15) | collective-permute-done | bytes 65568 | tf_op jit(solution)/shard_map/ppermute | solution.py:256
  50.7 3.4 %collective-permute-done.16.refs_5_ = bf16[16,2048]{1,0:T(8,128)(2,1)S(1)} collective-permute-done((bf16[16,2048]{1,0:T(8,128)(2,1)S(1)}, bf16[16,2048]{1,0:T(8,128)(2,1)S(1)}, u32[]{:S(2)}, u32[]{:S(2)}) %collective-permute-start.16) | collective-permute-done | bytes 65568 | tf_op jit(solution)/shard_map/ppermute | solution.py:256
  54.1 1.7 %collective-permute-start.5 = (bf16[32,2048]{1,0:T(8,128)(2,1)S(1)}, bf16[32,2048]{1,0:T(8,128)(2,1)S(1)}, u32[]{:S(2)}, u32[]{:S(2)}) collective-permute-start(bf16[32,2048]{1,0:T(8,128)(2,1)S(1)} %get-tuple-element.42), channel_id=1, source_target_pairs={{0,12},{4,8},{8,4},{12,0},{16,28},{20,24},{24,20},{28,16},{1,13},{... | collective-permute-start | bytes 393224 | tf_op jit(solution)/shard_map/ppermute | solution.py:256
  56.7 1.3 %collective-permute-start.25 = (bf16[1,512,256]{2,1,0:T(8,128)(2,1)S(1)}, bf16[1,512,256]{2,1,0:T(8,128)(2,1)S(1)}, u32[]{:S(2)}, u32[]{:S(2)}) collective-permute-start(bf16[1,512,256]{2,1,0:T(8,128)(2,1)S(1)} %fusion.3), channel_id=1, source_target_pairs={{0,2},{1,3},{2,0},{3,1},{4,6},{5,7},{6,4},{7,5},{8,10},{9,11},{10,... | collective-permute-start | bytes 786440 | tf_op jit(solution)/shard_map/ppermute | solution.py:256
  58.0 2.5 %collective-permute-done.4.refs_2_ = bf16[32,2048]{1,0:T(8,128)(2,1)S(1)} collective-permute-done((bf16[32,2048]{1,0:T(8,128)(2,1)S(1)}, bf16[32,2048]{1,0:T(8,128)(2,1)S(1)}, u32[]{:S(2)}, u32[]{:S(2)}) %collective-permute-start.4) | collective-permute-done | bytes 131104 | tf_op jit(solution)/shard_map/ppermute | solution.py:256
  60.4 1.1 %collective-permute-done.5.refs_3_ = bf16[32,2048]{1,0:T(8,128)(2,1)S(1)} collective-permute-done((bf16[32,2048]{1,0:T(8,128)(2,1)S(1)}, bf16[32,2048]{1,0:T(8,128)(2,1)S(1)}, u32[]{:S(2)}, u32[]{:S(2)}) %collective-permute-start.5) | collective-permute-done | bytes 131104 | tf_op jit(solution)/shard_map/ppermute | solution.py:256
  62.1 1.1 %shard_map.65 = bf16[128,2048]{1,0:T(8,128)(2,1)} custom-call(bf16[256,128]{1,0:T(8,128)(2,1)S(1)} %get-tuple-element.34.select_ref, bf16[32,2048]{1,0:T(8,128)(2,1)S(1)} %get-tuple-element.39.refs_0_, bf16[32,2048]{1,0:T(8,128)(2,1)S(1)} %collective-permute-done.3.refs_1_, bf16[32,2048]{1,0:T(8,128)(2,1)S(1)} %collective-permute-done.4.refs_2_, ...), custom_call_target="tpu_custom_call" | custom-call | flops 134217728 | bytes 1048576 | tf_op jit(solution)/shard_map/pallas_call | solution.py:239
  64.0 3.2 %collective-permute-done.25 = bf16[1,512,256]{2,1,0:T(8,128)(2,1)S(1)} collective-permute-done((bf16[1,512,256]{2,1,0:T(8,128)(2,1)S(1)}, bf16[1,512,256]{2,1,0:T(8,128)(2,1)S(1)}, u32[]{:S(2)}, u32[]{:S(2)}) %collective-permute-start.25) | collective-permute-done | bytes 262176 | tf_op jit(solution)/shard_map/ppermute | solution.py:256
  67.3 4.8 %collective-permute-done.27 = bf16[1,512,256]{2,1,0:T(8,128)(2,1)S(1)} collective-permute-done((bf16[1,512,256]{2,1,0:T(8,128)(2,1)S(1)}, bf16[1,512,256]{2,1,0:T(8,128)(2,1)S(1)}, u32[]{:S(2)}, u32[]{:S(2)}) %collective-permute-start.27) | collective-permute-done | bytes 262176 | tf_op jit(solution)/shard_map/ppermute | solution.py:256
  72.2 1.1 %maximum_bitcast_fusion = f32[1,512,512]{2,1,0:T(8,128)} fusion(f32[512,256]{1,0:T(8,128)S(1)} %fusion.2, f32[512,256]{1,0:T(8,128)S(1)} %fusion.5), kind=kLoop, calls=%fused_computation | loop fusion | flops 262144 | bytes 2097152 | tf_op jit(solution)/shard_map/broadcast_in_dim | solution.py:456
  (38 shorter events, 8.0 us)
Async XLA Ops:
  2.2 8.0 %collective-permute-start.6 = (bf16[16,2304]{1,0:T(8,128)(2,1)S(1)}, bf16[16,2304]{1,0:T(8,128)(2,1)S(1)}, u32[]{:S(2)}, u32[]{:S(2)}) collective-permute-start(bf16[16,2304]{1,0:T(8,128)(2,1)S(1)} %get-tuple-element.43), channel_id=1, source_target_pairs={{0,16},{4,20},{8,24},{12,28},{16,0},{20,4},{24,8},{28,12},{1,17},{... | collective-permute-start | bytes 221192 | tf_op jit(solution)/shard_map/ppermute | solution.py:256
  6.3 10.3 %collective-permute-start.10 = (bf16[32,2432]{1,0:T(8,128)(2,1)S(1)}, bf16[32,2432]{1,0:T(8,128)(2,1)S(1)}, u32[]{:S(2)}, u32[]{:S(2)}) collective-permute-start(bf16[32,2432]{1,0:T(8,128)(2,1)S(1)} %get-tuple-element.48), channel_id=1, source_target_pairs={{0,2},{1,3},{2,0},{3,1},{4,6},{5,7},{6,4},{7,5},{8,10},{9,11},{10,... | collective-permute-start | bytes 466952 | tf_op jit(solution)/shard_map/ppermute | solution.py:256
  7.9 6.6 %collective-permute-start.7 = (bf16[16,2304]{1,0:T(8,128)(2,1)S(1)}, bf16[16,2304]{1,0:T(8,128)(2,1)S(1)}, u32[]{:S(2)}, u32[]{:S(2)}) collective-permute-start(bf16[16,2304]{1,0:T(8,128)(2,1)S(1)} %get-tuple-element.44), channel_id=1, source_target_pairs={{0,20},{4,16},{8,28},{12,24},{16,4},{20,0},{24,12},{28,8},{1,21},{... | collective-permute-start | bytes 221192 | tf_op jit(solution)/shard_map/ppermute | solution.py:256
  7.9 14.3 %collective-permute-start = (bf16[32,2304]{1,0:T(8,128)(2,1)S(1)}, bf16[32,2304]{1,0:T(8,128)(2,1)S(1)}, u32[]{:S(2)}, u32[]{:S(2)}) collective-permute-start(bf16[32,2304]{1,0:T(8,128)(2,1)S(1)} %get-tuple-element.36), channel_id=1, source_target_pairs={{0,4},{4,0},{8,12},{12,8},{16,20},{20,16},{24,28},{28,24},{1,5},{5... | collective-permute-start | bytes 442376 | tf_op jit(solution)/shard_map/ppermute | solution.py:256
  8.3 15.6 %collective-permute-start.1 = (bf16[32,2304]{1,0:T(8,128)(2,1)S(1)}, bf16[32,2304]{1,0:T(8,128)(2,1)S(1)}, u32[]{:S(2)}, u32[]{:S(2)}) collective-permute-start(bf16[32,2304]{1,0:T(8,128)(2,1)S(1)} %get-tuple-element.37), channel_id=1, source_target_pairs={{0,8},{4,12},{8,0},{12,4},{16,24},{20,28},{24,16},{28,20},{1,9},{5... | collective-permute-start | bytes 442376 | tf_op jit(solution)/shard_map/ppermute | solution.py:256
  10.3 14.6 %collective-permute-start.2 = (bf16[32,2304]{1,0:T(8,128)(2,1)S(1)}, bf16[32,2304]{1,0:T(8,128)(2,1)S(1)}, u32[]{:S(2)}, u32[]{:S(2)}) collective-permute-start(bf16[32,2304]{1,0:T(8,128)(2,1)S(1)} %get-tuple-element.38), channel_id=1, source_target_pairs={{0,12},{4,8},{8,4},{12,0},{16,28},{20,24},{24,20},{28,16},{1,13},{... | collective-permute-start | bytes 442376 | tf_op jit(solution)/shard_map/ppermute | solution.py:256
  14.5 7.6 %collective-permute-start.8 = (bf16[16,2304]{1,0:T(8,128)(2,1)S(1)}, bf16[16,2304]{1,0:T(8,128)(2,1)S(1)}, u32[]{:S(2)}, u32[]{:S(2)}) collective-permute-start(bf16[16,2304]{1,0:T(8,128)(2,1)S(1)} %get-tuple-element.45), channel_id=1, source_target_pairs={{0,24},{4,28},{8,16},{12,20},{16,8},{20,12},{24,0},{28,4},{1,25},{... | collective-permute-start | bytes 221192 | tf_op jit(solution)/shard_map/ppermute | solution.py:256
  16.6 12.9 %collective-permute-start.9 = (bf16[16,2304]{1,0:T(8,128)(2,1)S(1)}, bf16[16,2304]{1,0:T(8,128)(2,1)S(1)}, u32[]{:S(2)}, u32[]{:S(2)}) collective-permute-start(bf16[16,2304]{1,0:T(8,128)(2,1)S(1)} %get-tuple-element.46), channel_id=1, source_target_pairs={{0,28},{4,24},{8,20},{12,16},{16,12},{20,8},{24,4},{28,0},{1,29},{... | collective-permute-start | bytes 221192 | tf_op jit(solution)/shard_map/ppermute | solution.py:256
  22.1 7.4 %collective-permute-start.11 = (bf16[8,2304]{1,0:T(8,128)(2,1)S(1)}, bf16[8,2304]{1,0:T(8,128)(2,1)S(1)}, u32[]{:S(2)}, u32[]{:S(2)}) collective-permute-start(bf16[8,2304]{1,0:T(8,128)(2,1)S(1)} %get-tuple-element.49), channel_id=1, source_target_pairs={{0,16},{4,20},{8,24},{12,28},{16,0},{20,4},{24,8},{28,12},{1,17},{... | collective-permute-start | bytes 110600 | tf_op jit(solution)/shard_map/ppermute | solution.py:256
  22.1 7.4 %collective-permute-start.12 = (bf16[8,2304]{1,0:T(8,128)(2,1)S(1)}, bf16[8,2304]{1,0:T(8,128)(2,1)S(1)}, u32[]{:S(2)}, u32[]{:S(2)}) collective-permute-start(bf16[8,2304]{1,0:T(8,128)(2,1)S(1)} %get-tuple-element.50), channel_id=1, source_target_pairs={{0,20},{4,16},{8,28},{12,24},{16,4},{20,0},{24,12},{28,8},{1,21},{... | collective-permute-start | bytes 110600 | tf_op jit(solution)/shard_map/ppermute | solution.py:256
  23.9 5.9 %collective-permute-start.13 = (bf16[8,2304]{1,0:T(8,128)(2,1)S(1)}, bf16[8,2304]{1,0:T(8,128)(2,1)S(1)}, u32[]{:S(2)}, u32[]{:S(2)}) collective-permute-start(bf16[8,2304]{1,0:T(8,128)(2,1)S(1)} %get-tuple-element.51), channel_id=1, source_target_pairs={{0,24},{4,28},{8,16},{12,20},{16,8},{20,12},{24,0},{28,4},{1,25},{... | collective-permute-start | bytes 110600 | tf_op jit(solution)/shard_map/ppermute | solution.py:256
  24.9 5.7 %collective-permute-start.14 = (bf16[8,2304]{1,0:T(8,128)(2,1)S(1)}, bf16[8,2304]{1,0:T(8,128)(2,1)S(1)}, u32[]{:S(2)}, u32[]{:S(2)}) collective-permute-start(bf16[8,2304]{1,0:T(8,128)(2,1)S(1)} %get-tuple-element.52), channel_id=1, source_target_pairs={{0,28},{4,24},{8,20},{12,16},{16,12},{20,8},{24,4},{28,0},{1,29},{... | collective-permute-start | bytes 110600 | tf_op jit(solution)/shard_map/ppermute | solution.py:256
  32.3 15.0 %collective-permute-start.24 = (bf16[2,512,256]{2,1,0:T(8,128)(2,1)S(1)}, bf16[2,512,256]{2,1,0:T(8,128)(2,1)S(1)}, u32[]{:S(2)}, u32[]{:S(2)}) collective-permute-start(bf16[2,512,256]{2,1,0:T(8,128)(2,1)S(1)} %get-tuple-element.63), channel_id=1, source_target_pairs={{0,1},{1,0},{2,3},{3,2},{4,5},{5,4},{6,7},{7,6},{8,9},{9,8},{10,11... | collective-permute-start | bytes 1572872 | tf_op jit(solution)/shard_map/ppermute | solution.py:256
  33.9 29.4 %collective-permute-start.26 = (bf16[2,512,256]{2,1,0:T(8,128)(2,1)S(1)}, bf16[2,512,256]{2,1,0:T(8,128)(2,1)S(1)}, u32[]{:S(2)}, u32[]{:S(2)}) collective-permute-start(bf16[2,512,256]{2,1,0:T(8,128)(2,1)S(1)} %get-tuple-element.65), channel_id=1, source_target_pairs={{0,2},{1,3},{2,0},{3,1},{4,6},{5,7},{6,4},{7,5},{8,10},{9,11},{10,... | collective-permute-start | bytes 1572872 | tf_op jit(solution)/shard_map/ppermute | solution.py:256
  35.0 5.5 %collective-permute-start.19 = (bf16[8,2048]{1,0:T(8,128)(2,1)S(1)}, bf16[8,2048]{1,0:T(8,128)(2,1)S(1)}, u32[]{:S(2)}, u32[]{:S(2)}) collective-permute-start(bf16[8,2048]{1,0:T(8,128)(2,1)S(1)} %get-tuple-element.58), channel_id=1, source_target_pairs={{0,16},{4,20},{8,24},{12,28},{16,0},{20,4},{24,8},{28,12},{1,17},{... | collective-permute-start | bytes 98312 | tf_op jit(solution)/shard_map/ppermute | solution.py:256
  35.6 5.7 %collective-permute-start.20 = (bf16[8,2048]{1,0:T(8,128)(2,1)S(1)}, bf16[8,2048]{1,0:T(8,128)(2,1)S(1)}, u32[]{:S(2)}, u32[]{:S(2)}) collective-permute-start(bf16[8,2048]{1,0:T(8,128)(2,1)S(1)} %get-tuple-element.59), channel_id=1, source_target_pairs={{0,20},{4,16},{8,28},{12,24},{16,4},{20,0},{24,12},{28,8},{1,21},{... | collective-permute-start | bytes 98312 | tf_op jit(solution)/shard_map/ppermute | solution.py:256
  37.9 5.7 %collective-permute-start.21 = (bf16[8,2048]{1,0:T(8,128)(2,1)S(1)}, bf16[8,2048]{1,0:T(8,128)(2,1)S(1)}, u32[]{:S(2)}, u32[]{:S(2)}) collective-permute-start(bf16[8,2048]{1,0:T(8,128)(2,1)S(1)} %get-tuple-element.60), channel_id=1, source_target_pairs={{0,24},{4,28},{8,16},{12,20},{16,8},{20,12},{24,0},{28,4},{1,25},{... | collective-permute-start | bytes 98312 | tf_op jit(solution)/shard_map/ppermute | solution.py:256
  40.5 5.1 %collective-permute-start.22 = (bf16[8,2048]{1,0:T(8,128)(2,1)S(1)}, bf16[8,2048]{1,0:T(8,128)(2,1)S(1)}, u32[]{:S(2)}, u32[]{:S(2)}) collective-permute-start(bf16[8,2048]{1,0:T(8,128)(2,1)S(1)} %get-tuple-element.61), channel_id=1, source_target_pairs={{0,28},{4,24},{8,20},{12,16},{16,12},{20,8},{24,4},{28,0},{1,29},{... | collective-permute-start | bytes 98312 | tf_op jit(solution)/shard_map/ppermute | solution.py:256
  41.2 9.3 %collective-permute-start.15 = (bf16[16,2048]{1,0:T(8,128)(2,1)S(1)}, bf16[16,2048]{1,0:T(8,128)(2,1)S(1)}, u32[]{:S(2)}, u32[]{:S(2)}) collective-permute-start(bf16[16,2048]{1,0:T(8,128)(2,1)S(1)} %get-tuple-element.54), channel_id=1, source_target_pairs={{0,16},{4,20},{8,24},{12,28},{16,0},{20,4},{24,8},{28,12},{1,17},{... | collective-permute-start | bytes 196616 | tf_op jit(solution)/shard_map/ppermute | solution.py:256
  43.6 10.5 %collective-permute-start.16 = (bf16[16,2048]{1,0:T(8,128)(2,1)S(1)}, bf16[16,2048]{1,0:T(8,128)(2,1)S(1)}, u32[]{:S(2)}, u32[]{:S(2)}) collective-permute-start(bf16[16,2048]{1,0:T(8,128)(2,1)S(1)} %get-tuple-element.55), channel_id=1, source_target_pairs={{0,20},{4,16},{8,28},{12,24},{16,4},{20,0},{24,12},{28,8},{1,21},{... | collective-permute-start | bytes 196616 | tf_op jit(solution)/shard_map/ppermute | solution.py:256
  45.6 8.4 %collective-permute-start.17 = (bf16[16,2048]{1,0:T(8,128)(2,1)S(1)}, bf16[16,2048]{1,0:T(8,128)(2,1)S(1)}, u32[]{:S(2)}, u32[]{:S(2)}) collective-permute-start(bf16[16,2048]{1,0:T(8,128)(2,1)S(1)} %get-tuple-element.56), channel_id=1, source_target_pairs={{0,24},{4,28},{8,16},{12,20},{16,8},{20,12},{24,0},{28,4},{1,25},{... | collective-permute-start | bytes 196616 | tf_op jit(solution)/shard_map/ppermute | solution.py:256
  47.3 8.5 %collective-permute-start.18 = (bf16[16,2048]{1,0:T(8,128)(2,1)S(1)}, bf16[16,2048]{1,0:T(8,128)(2,1)S(1)}, u32[]{:S(2)}, u32[]{:S(2)}) collective-permute-start(bf16[16,2048]{1,0:T(8,128)(2,1)S(1)} %get-tuple-element.57), channel_id=1, source_target_pairs={{0,28},{4,24},{8,20},{12,16},{16,12},{20,8},{24,4},{28,0},{1,29},{... | collective-permute-start | bytes 196616 | tf_op jit(solution)/shard_map/ppermute | solution.py:256
  50.6 6.1 %collective-permute-start.3 = (bf16[32,2048]{1,0:T(8,128)(2,1)S(1)}, bf16[32,2048]{1,0:T(8,128)(2,1)S(1)}, u32[]{:S(2)}, u32[]{:S(2)}) collective-permute-start(bf16[32,2048]{1,0:T(8,128)(2,1)S(1)} %get-tuple-element.40), channel_id=1, source_target_pairs={{0,4},{4,0},{8,12},{12,8},{16,20},{20,16},{24,28},{28,24},{1,5},{5... | collective-permute-start | bytes 393224 | tf_op jit(solution)/shard_map/ppermute | solution.py:256
  54.1 6.4 %collective-permute-start.4 = (bf16[32,2048]{1,0:T(8,128)(2,1)S(1)}, bf16[32,2048]{1,0:T(8,128)(2,1)S(1)}, u32[]{:S(2)}, u32[]{:S(2)}) collective-permute-start(bf16[32,2048]{1,0:T(8,128)(2,1)S(1)} %get-tuple-element.41), channel_id=1, source_target_pairs={{0,8},{4,12},{8,0},{12,4},{16,24},{20,28},{24,16},{28,20},{1,9},{5... | collective-permute-start | bytes 393224 | tf_op jit(solution)/shard_map/ppermute | solution.py:256
  54.1 7.5 %collective-permute-start.5 = (bf16[32,2048]{1,0:T(8,128)(2,1)S(1)}, bf16[32,2048]{1,0:T(8,128)(2,1)S(1)}, u32[]{:S(2)}, u32[]{:S(2)}) collective-permute-start(bf16[32,2048]{1,0:T(8,128)(2,1)S(1)} %get-tuple-element.42), channel_id=1, source_target_pairs={{0,12},{4,8},{8,4},{12,0},{16,28},{20,24},{24,20},{28,16},{1,13},{... | collective-permute-start | bytes 393224 | tf_op jit(solution)/shard_map/ppermute | solution.py:256
  55.8 6.4 %collective-permute-start.23 = (bf16[32,2048]{1,0:T(8,128)(2,1)S(1)}, bf16[32,2048]{1,0:T(8,128)(2,1)S(1)}, u32[]{:S(2)}, u32[]{:S(2)}) collective-permute-start(bf16[32,2048]{1,0:T(8,128)(2,1)S(1)} %shard_map.64), channel_id=1, source_target_pairs={{0,2},{1,3},{2,0},{3,1},{4,6},{5,7},{6,4},{7,5},{8,10},{9,11},{10,... | collective-permute-start | bytes 393224 | tf_op jit(solution)/shard_map/ppermute | solution.py:256
  56.7 10.5 %collective-permute-start.25 = (bf16[1,512,256]{2,1,0:T(8,128)(2,1)S(1)}, bf16[1,512,256]{2,1,0:T(8,128)(2,1)S(1)}, u32[]{:S(2)}, u32[]{:S(2)}) collective-permute-start(bf16[1,512,256]{2,1,0:T(8,128)(2,1)S(1)} %fusion.3), channel_id=1, source_target_pairs={{0,2},{1,3},{2,0},{3,1},{4,6},{5,7},{6,4},{7,5},{8,10},{9,11},{10,... | collective-permute-start | bytes 786440 | tf_op jit(solution)/shard_map/ppermute | solution.py:256
  63.4 8.7 %collective-permute-start.27 = (bf16[1,512,256]{2,1,0:T(8,128)(2,1)S(1)}, bf16[1,512,256]{2,1,0:T(8,128)(2,1)S(1)}, u32[]{:S(2)}, u32[]{:S(2)}) collective-permute-start(bf16[1,512,256]{2,1,0:T(8,128)(2,1)S(1)} %fusion), channel_id=1, source_target_pairs={{0,1},{1,0},{2,3},{3,2},{4,5},{5,4},{6,7},{7,6},{8,9},{9,8},{10,11... | collective-permute-start | bytes 786440 | tf_op jit(solution)/shard_map/ppermute | solution.py:256

commit v3 on v2

--- a/solution.py
+++ b/solution.py
@@ -10,6 +10,8 @@
 
 BF16 = jnp.bfloat16
 F32 = jnp.float32
+LATE = ("up0", "up1", "up2", "up3")
+PARTS = 1
 VMEM = pl.BlockSpec(memory_space=pltpu.VMEM)
 HBM = pl.BlockSpec(memory_space=pltpu.HBM)
 
@@ -166,39 +168,41 @@
     copy.wait()
 
 
-def near_kernel(count, *refs):
-    pieces, (weights_ref, pre_ref), grads = refs[:count], refs[count : count + 2], refs[count + 2 :]
+def rows_grads(pieces, weights_ref, inputs_ref, pre_ref, grads):
     width = weights_ref.shape[0]
-    inputs = stack(pieces, slice(0, width))
-    cotangent = stack(pieces, slice(width, None)).astype(F32)
-    pre_ref[...] = hidden_grads(inputs, cotangent, weights_ref)
+    start = 0
+    for run in runs(pieces):
+        end = start + sum(piece.shape[0] for piece in run)
+        inputs_ref[start:end, :] = stack(run, slice(0, width))
+        start = end
+    cotangent = jnp.concatenate(
+        [stack(run, slice(width, None)).astype(F32) for run in runs(pieces)], axis=0
+    )
+    pre_ref[...] = hidden_grads(inputs_ref[...], cotangent, weights_ref)
     input_grads(pre_ref[...], weights_ref, grads)
 
 
-def far_kernel(groups, near_count, count, *refs):
-    near = refs[:near_count]
-    pieces = refs[near_count : near_count + count]
-    near_pre_ref, weights_ref = refs[near_count + count : near_count + count + 2]
-    rest = refs[near_count + count + 2 :]
-    grads = rest[:count]
-    send_a, keep_a, send_b, keep_b, inputs_ref, pre_ref = rest[count:]
-    width, _ = weights_ref.shape
-    split = near_pre_ref.shape[0]
-    inputs_ref[:split, :] = stack(near, slice(0, width))
-    pre_ref[:split, :] = near_pre_ref[...]
-    low, up = pieces[: count // 2], pieces[count // 2 :]
-    inputs = jnp.concatenate([stack(low, slice(0, width)), stack(up, slice(0, width))], axis=0)
-    inputs_ref[split:, :] = inputs
-    cotangent = jnp.concatenate(
-        [stack(low, slice(width, None)), stack(up, slice(width, None))], axis=0
-    ).astype(F32)
-    pre_grad = hidden_grads(inputs_ref[split:, :], cotangent, weights_ref)
-    pre_ref[split:, :] = pre_grad
-    input_grads(pre_grad, weights_ref, grads)
-    weight_terms(groups, inputs_ref, pre_ref, send_a, keep_a, send_b, keep_b)
-
-
-def weight_terms(groups, inputs_ref, pre_ref, send_a, keep_a, send_b, keep_b):
+def early_kernel(count, *refs):
+    pieces, (weights_ref, inputs_ref, pre_ref), grads = (
+        refs[:count],
+        refs[count : count + 3],
+        refs[count + 3 :],
+    )
+    rows_grads(pieces, weights_ref, inputs_ref, pre_ref, grads)
+
+
+def late_kernel(groups, parts, count, *refs):
+    early_inputs_ref, early_pre_ref, weights_ref = refs[:3]
+    pieces, rest = refs[3 : count + 3], refs[count + 3 :]
+    grads, terms, (inputs_ref, pre_ref) = rest[:count], rest[count:-2], rest[-2:]
+    split = early_pre_ref.shape[0]
+    inputs_ref[:split, :] = early_inputs_ref[...]
+    pre_ref[:split, :] = early_pre_ref[...]
+    rows_grads(pieces, weights_ref, inputs_ref.at[split:, :], pre_ref.at[split:, :], grads)
+    weight_terms(groups, parts, inputs_ref, pre_ref, terms)
+
+
+def weight_terms(groups, parts, inputs_ref, pre_ref, terms):
     me = lax.axis_index("group").astype(jnp.int32)
     part = inputs_ref.shape[1] // groups
     hidden = pre_ref.shape[1] // 2
@@ -206,28 +210,50 @@
     for k in range(groups):
         columns = pl.ds(pl.multiple_of((me ^ k) * part, part), part)
         term = dot_t(inputs_ref[:, columns], pre_grad)
-        if k % 2:
-            send_a[k // 2] = term[:, :hidden].astype(BF16)
+        for chunk in range(parts):
+            send_a, keep_a, send_b, keep_b = terms[4 * chunk : 4 * chunk + 4]
+            size = part // parts
+            rows = slice(chunk * size, (chunk + 1) * size)
+            if k % 2:
+                send_a[k // 2] = term[rows, :hidden].astype(BF16)
+            else:
+                keep_a[k // 2] = term[rows, :hidden]
+            if k >= groups // 2:
+                send_b[k - groups // 2] = term[rows, hidden:].astype(BF16)
+            else:
+                keep_b[k] = term[rows, hidden:]
+
+
+def runs(pieces):
+    found = []
+    for piece in pieces:
+        if found and found[-1][0].shape[0] == piece.shape[0]:
+            found[-1].append(piece)
         else:
-            keep_a[k // 2] = term[:, :hidden]
-        if k >= groups // 2:
-            send_b[k - groups // 2] = term[:, hidden:].astype(BF16)
-        else:
-            keep_b[k] = term[:, hidden:]
+            found.append([piece])
+    return found
 
 
 def combine_kernel(select_ref, *refs):
     *pieces, out_ref, stacked_ref = refs
     start = 0
-    while pieces:
-        rows = pieces[0].shape[0]
-        run = pieces[: next((i for i, p in enumerate(pieces) if p.shape[0] != rows), len(pieces))]
-        end = start + rows * len(run)
+    for run in runs(pieces):
+        end = start + sum(piece.shape[0] for piece in run)
         stacked_ref[start:end, :] = stack(run)
-        start, pieces = end, pieces[len(run) :]
+        start = end
     select = select_ref[...]
     for at, size in chunks(out_ref.shape[1], 512):
         out_ref[:, at : at + size] = dot_t(select, stacked_ref[:, at : at + size]).astype(BF16)
+
+
+def finish_kernel(parts, *refs):
+    *terms, out_ref = refs
+    size, hidden = out_ref.shape[0] // parts, out_ref.shape[1] // 2
+    for chunk in range(parts):
+        keep_a, got_a, keep_b, got_b = terms[4 * chunk : 4 * chunk + 4]
+        rows = slice(chunk * size, (chunk + 1) * size)
+        out_ref[rows, :hidden] = keep_a[0] + got_a[0].astype(F32)
+        out_ref[rows, hidden:] = keep_b[0] + got_b[0].astype(F32)
 
 
 def call(kernel, out_shapes, scratch, flops, moved, args, specs=None, vmem=24 << 20):
@@ -256,23 +282,37 @@
     return lax.ppermute(value, axis, [(i, i ^ mask) for i in range(size)])
 
 
-def sum_over_groups(send_a, keep_a, send_b, keep_b, groups):
+def sum_over_groups(terms, groups, parts):
     bits = groups.bit_length() - 1
-    for step in range(bits):
-        got_a = flip(send_a, "group", 1 << step).astype(F32)
-        got_b = flip(send_b, "group", 1 << (bits - 1 - step)).astype(F32)
-        if step == bits - 1:
-            return jnp.concatenate([keep_a[0] + got_a[0], keep_b[0] + got_b[0]], axis=1)
-        half = keep_a.shape[0] // 2
-        send_a = (keep_a[1::2] + got_a[1::2]).astype(BF16)
-        keep_a = keep_a[0::2] + got_a[0::2]
-        send_b = (keep_b[half:] + got_b[half:]).astype(BF16)
-        keep_b = keep_b[:half] + got_b[:half]
-
-
-def term_shapes(groups, width, hidden):
-    block = (groups // 2, width // groups, hidden)
-    return [shape(block), shape(block, F32), shape(block), shape(block, F32)]
+    last = []
+    for chunk in range(parts):
+        send_a, keep_a, send_b, keep_b = terms[4 * chunk : 4 * chunk + 4]
+        for step in range(bits):
+            got_a = flip(send_a, "group", 1 << step)
+            got_b = flip(send_b, "group", 1 << (bits - 1 - step))
+            if step == bits - 1:
+                last += [keep_a, got_a, keep_b, got_b]
+                break
+            got_a, got_b = got_a.astype(F32), got_b.astype(F32)
+            half = keep_a.shape[0] // 2
+            send_a = (keep_a[1::2] + got_a[1::2]).astype(BF16)
+            keep_a = keep_a[0::2] + got_a[0::2]
+            send_b = (keep_b[half:] + got_b[half:]).astype(BF16)
+            keep_b = keep_b[:half] + got_b[:half]
+    rows, columns = parts * last[0].shape[1], 2 * last[0].shape[2]
+    return call(
+        functools.partial(finish_kernel, parts),
+        shape((rows, columns), F32),
+        [],
+        2 * rows * columns,
+        10 * rows * columns,
+        last,
+    )
+
+
+def term_shapes(groups, width, hidden, parts):
+    block = (groups // 2, width // groups // parts, hidden)
+    return [shape(block), shape(block, F32), shape(block), shape(block, F32)] * parts
 
 
 def paired(tokens_in, hidden_grad, routing, weights):
@@ -325,50 +365,58 @@
         (weights,),
         specs=[HBM],
     )
-    near_slots, far_slots = half * full, half * (low_rows + up_rows)
-    near_pre, *near_grads = call(
-        functools.partial(near_kernel, half),
-        [shape((near_slots, 2 * hidden))] + [shape((full, width))] * half,
+    names = [f"near{k}" for k in range(half)]
+    names += [f"low{k}" for k in range(half)] + [f"up{k}" for k in range(half)]
+    arrived = dict(zip(names, [*near, *low, *up]))
+    late = [name for name in names if name in LATE]
+    early = [name for name in names if name not in LATE]
+    early_rows = sum(arrived[name].shape[0] for name in early)
+    all_rows = half * (full + low_rows + up_rows)
+
+    def grad_shapes(of):
+        return [shape((arrived[name].shape[0], width)) for name in of]
+
+    early_inputs, early_pre, *early_grads = call(
+        functools.partial(early_kernel, len(early)),
+        [shape((early_rows, width)), shape((early_rows, 2 * hidden))] + grad_shapes(early),
         [],
-        8 * near_slots * width * hidden,
-        4 * near_slots * joined,
-        (*near, weights),
+        8 * early_rows * width * hidden,
+        4 * early_rows * joined,
+        (*(arrived[name] for name in early), weights),
     )
     out = call(
-        functools.partial(far_kernel, groups, half, 2 * half),
-        [shape((low_rows, width))] * half
-        + [shape((up_rows, width))] * half
-        + term_shapes(groups, width, hidden),
-        [
-            pltpu.VMEM((near_slots + far_slots, width), BF16),
-            pltpu.VMEM((near_slots + far_slots, 2 * hidden), BF16),
-        ],
-        12 * (near_slots + far_slots) * width * hidden,
-        4 * (near_slots + far_slots) * joined,
-        (*near, *low, *up, near_pre, weights),
+        functools.partial(late_kernel, groups, PARTS, len(late)),
+        grad_shapes(late) + term_shapes(groups, width, hidden, PARTS),
+        [pltpu.VMEM((all_rows, width), BF16), pltpu.VMEM((all_rows, 2 * hidden), BF16)],
+        4 * (all_rows + 2 * (all_rows - early_rows)) * width * hidden,
+        4 * all_rows * joined,
+        (early_inputs, early_pre, weights, *(arrived[name] for name in late)),
         vmem=32 << 20,
     )
-    low_grads, up_grads, terms = out[:half], out[half : 2 * half], out[2 * half :]
-    near_grads = [near_grads[0]] + [flip(near_grads[k], "expert", k) for k in range(1, half)]
-    up_grads = [flip(up_grads[k], "expert", half + k) for k in range(half)]
-    low_grads = [flip(low_grads[k], "expert", half + k) for k in range(half)]
+    terms = out[len(late) :]
+    grads = dict(zip(early + late, [*early_grads, *out[: len(late)]]))
+    for k in range(half):
+        if k:
+            grads[f"near{k}"] = flip(grads[f"near{k}"], "expert", k)
+        for name in (f"low{k}", f"up{k}"):
+            grads[name] = flip(grads[name], "expert", half + k)
     spilled_grad = call(
         split_kernel,
         shape((spill, width)),
         [],
         2 * spill * lane * width,
         4 * half * up_rows * width,
-        (landed, *up_grads),
+        (landed, *(grads[f"up{k}"] for k in range(half))),
     )
     spilled_grad = flip(spilled_grad, "group", groups // 2)
-    weight_grad = sum_over_groups(*terms, groups)
+    weight_grad = sum_over_groups(terms, groups, PARTS)
     tokens_grad = call(
         combine_kernel,
         shape((rows, width)),
         [pltpu.VMEM((slots, width), BF16)],
         2 * slots * rows * width,
         2 * slots * width,
-        (select, *near_grads, *low_grads, *up_grads, spilled_grad),
+        (select, *(grads[name] for name in names), spilled_grad),
     )
     return tokens_grad, weight_grad
 
@@ -390,11 +438,8 @@
 
 def whole_expert_kernel(groups, rows_ref, weights_ref, grad_ref, *refs):
     *terms, inputs_ref, pre_ref = refs
-    width = weights_ref.shape[0]
-    inputs_ref[...] = rows_ref[:, :width]
-    pre_ref[...] = hidden_grads(inputs_ref[...], rows_ref[:, width:].astype(F32), weights_ref)
-    input_grads(pre_ref[...], weights_ref, [grad_ref])
-    weight_terms(groups, inputs_ref, pre_ref, *terms)
+    rows_grads([rows_ref], weights_ref, inputs_ref, pre_ref, [grad_ref])
+    weight_terms(groups, 1, inputs_ref, pre_ref, terms)
 
 
 def unpaired(tokens_in, hidden_grad, routing, weights):
@@ -426,14 +471,14 @@
     )
     grad, *terms = call(
         functools.partial(whole_expert_kernel, groups),
-        [shape((slots, width))] + term_shapes(groups, width, hidden),
+        [shape((slots, width))] + term_shapes(groups, width, hidden, 1),
         [pltpu.VMEM((slots, width), BF16), pltpu.VMEM((slots, 2 * hidden), BF16)],
         12 * slots * width * hidden,
         4 * slots * joined,
         (exchange(outgoing), weights),
         vmem=32 << 20,
     )
-    weight_grad = sum_over_groups(*terms, groups)
+    weight_grad = sum_over_groups(terms, groups, 1)
     tokens_grad = call(
         combine_kernel,
         shape((rows, width)),

time: 73.5 us -> 75.4 us (1.026)
  waiting for transfers between devices: 29.5 us -> 32.6 us
  Pallas kernels: 7.76 us -> 8.98 us
  starting transfers between devices: 33.6 us -> 32.4 us
  other arithmetic: 1.65 us -> 0.56 us
    ppermute x28, waiting for transfers between devices: 29.5 us -> 32.6 us  [flip(): return lax.ppermute(value, axis, [(i, i ^ mask) for i in range(size)])]
    ppermute x28, starting transfers between devices: 33.6 us -> 32.4 us  [flip(): return lax.ppermute(value, axis, [(i, i ^ mask) for i in range(size)])]
    pallas_call x7 -> x8, Pallas kernels: 7.76 us -> 8.98 us  [call(): pl.pallas_call(kernel, out_shape=out_shapes, in_specs=specs or [VMEM] * l...]
    broadcast_in_dim x1 -> x0, other arithmetic: 1.13 us -> none  [on_device(): return (tokens_grad, weight_grad[None])]
  transfers between devices with their start and end apart: 28 -> 28, of which waited for: 15 -> 14; matrix products, arithmetic and copies ran while one was open for 1% -> 1% of each run, Pallas kernels for 6% -> 6%
where the time goes in v3:
time: 75.4 us; the launch traced here: 75.2 us
  waiting for transfers between devices  32.6 us (43%)
  starting transfers between devices  32.4 us (43%)
  Pallas kernels  8.98 us (12%)
    ppermute x28, waiting for transfers between devices, flip(): return lax.ppermute(value, axis, [(i, i ^ mask) for i in range(size)])  32.6 us
    ppermute x28, starting transfers between devices, flip(): return lax.ppermute(value, axis, [(i, i ^ mask) for i in range(size)])  32.4 us
    pallas_call x8, Pallas kernels, call(): pl.pallas_call(kernel, out_shape=out_shapes, in_specs=specs or [VMEM] * l...  8.98 us
  transfers between devices with their start and end apart: 28, of which 14 were waited for; matrix products, arithmetic and copies ran while one was open for 1% of the time, Pallas kernels for 6%

profile of v3, /device:TPU:0, one launch (start us, length us, event | category | flops | bytes accessed | tf_op | source)
XLA Modules:
  0.0 75.2 jit_solution(12731835847253538340)
XLA Ops:
  0.6 1.6 %shard_map.59 = (bf16[256,128]{1,0:T(8,128)(2,1)S(1)}, bf16[32,2432]{1,0:T(8,128)(2,1)S(1)}, bf16[32,2304]{1,0:T(8,128)(2,1)S(1)}, bf16[32,2304]{1,0:T(8,128)(2,...) custom-call(s32[1,128]{1,0:T(1,128)} %bitcast.5, ...), custom_call_target="tpu_custom_call" | custom-call | flops 150994944 | bytes 1179648 | tf_op jit(solution)/shard_map/pallas_call | solution.py:265
  2.2 3.1 %collective-permute-start.14 = (bf16[32,2432]{1,0:T(8,128)(2,1)S(1)}, bf16[32,2432]{1,0:T(8,128)(2,1)S(1)}, u32[]{:S(2)}, u32[]{:S(2)}) collective-permute-start(bf16[32,2432]{1,0:T(8,128)(2,1)S(1)} %get-tuple-element.55), channel_id=1, source_target_pairs={{0,2},{1,3},{2,0},{3,1},{4,6},{5,7},{6,4},{7,5},{8,10},{9,11},{10,... | collective-permute-start | bytes 466952 | tf_op jit(solution)/shard_map/ppermute | solution.py:282
  5.3 2.6 %collective-permute-start.3 = (bf16[16,2304]{1,0:T(8,128)(2,1)S(1)}, bf16[16,2304]{1,0:T(8,128)(2,1)S(1)}, u32[]{:S(2)}, u32[]{:S(2)}) collective-permute-start(bf16[16,2304]{1,0:T(8,128)(2,1)S(1)} %get-tuple-element.40), channel_id=1, source_target_pairs={{0,16},{4,20},{8,24},{12,28},{16,0},{20,4},{24,8},{28,12},{1,17},{... | collective-permute-start | bytes 221192 | tf_op jit(solution)/shard_map/ppermute | solution.py:282
  8.3 1.6 %collective-permute-start.1 = (bf16[32,2304]{1,0:T(8,128)(2,1)S(1)}, bf16[32,2304]{1,0:T(8,128)(2,1)S(1)}, u32[]{:S(2)}, u32[]{:S(2)}) collective-permute-start(bf16[32,2304]{1,0:T(8,128)(2,1)S(1)} %get-tuple-element.38), channel_id=1, source_target_pairs={{0,8},{4,12},{8,0},{12,4},{16,24},{20,28},{24,16},{28,20},{1,9},{5... | collective-permute-start | bytes 442376 | tf_op jit(solution)/shard_map/ppermute | solution.py:282
  9.9 1.9 %collective-permute-done.3.refs_4_ = bf16[16,2304]{1,0:T(8,128)(2,1)S(1)} collective-permute-done((bf16[16,2304]{1,0:T(8,128)(2,1)S(1)}, bf16[16,2304]{1,0:T(8,128)(2,1)S(1)}, u32[]{:S(2)}, u32[]{:S(2)}) %collective-permute-start.3) | collective-permute-done | bytes 73760 | tf_op jit(solution)/shard_map/ppermute | solution.py:282
  12.4 2.6 %collective-permute-done.4.refs_5_ = bf16[16,2304]{1,0:T(8,128)(2,1)S(1)} collective-permute-done((bf16[16,2304]{1,0:T(8,128)(2,1)S(1)}, bf16[16,2304]{1,0:T(8,128)(2,1)S(1)}, u32[]{:S(2)}, u32[]{:S(2)}) %collective-permute-start.4) | collective-permute-done | bytes 73760 | tf_op jit(solution)/shard_map/ppermute | solution.py:282
  15.0 2.9 %collective-permute-start.5 = (bf16[16,2304]{1,0:T(8,128)(2,1)S(1)}, bf16[16,2304]{1,0:T(8,128)(2,1)S(1)}, u32[]{:S(2)}, u32[]{:S(2)}) collective-permute-start(bf16[16,2304]{1,0:T(8,128)(2,1)S(1)} %get-tuple-element.42), channel_id=1, source_target_pairs={{0,24},{4,28},{8,16},{12,20},{16,8},{20,12},{24,0},{28,4},{1,25},{... | collective-permute-start | bytes 221192 | tf_op jit(solution)/shard_map/ppermute | solution.py:282
  18.1 1.6 %shard_map.60.refs_8_.refs_2_ = bf16[2048,512]{1,0:T(8,128)(2,1)S(1)} custom-call(bf16[2048,512]{1,0:T(8,128)(2,1)} %bitcast.3), custom_call_target="tpu_custom_call" | custom-call | bytes 2097152 | tf_op jit(solution)/shard_map/pallas_call | solution.py:265
  20.0 1.8 %collective-permute-done.5.refs_6_ = bf16[16,2304]{1,0:T(8,128)(2,1)S(1)} collective-permute-done((bf16[16,2304]{1,0:T(8,128)(2,1)S(1)}, bf16[16,2304]{1,0:T(8,128)(2,1)S(1)}, u32[]{:S(2)}, u32[]{:S(2)}) %collective-permute-start.5) | collective-permute-done | bytes 73760 | tf_op jit(solution)/shard_map/ppermute | solution.py:282
  21.9 2.4 %collective-permute-done.6.refs_7_ = bf16[16,2304]{1,0:T(8,128)(2,1)S(1)} collective-permute-done((bf16[16,2304]{1,0:T(8,128)(2,1)S(1)}, bf16[16,2304]{1,0:T(8,128)(2,1)S(1)}, u32[]{:S(2)}, u32[]{:S(2)}) %collective-permute-start.6) | collective-permute-done | bytes 73760 | tf_op jit(solution)/shard_map/ppermute | solution.py:282
  24.2 1.2 %collective-permute-start.16 = (bf16[8,2304]{1,0:T(8,128)(2,1)S(1)}, bf16[8,2304]{1,0:T(8,128)(2,1)S(1)}, u32[]{:S(2)}, u32[]{:S(2)}) collective-permute-start(bf16[8,2304]{1,0:T(8,128)(2,1)S(1)} %get-tuple-element.57), channel_id=1, source_target_pairs={{0,20},{4,16},{8,28},{12,24},{16,4},{20,0},{24,12},{28,8},{1,21},{... | collective-permute-start | bytes 110600 | tf_op jit(solution)/shard_map/ppermute | solution.py:282
  25.4 2.0 %collective-permute-start.17 = (bf16[8,2304]{1,0:T(8,128)(2,1)S(1)}, bf16[8,2304]{1,0:T(8,128)(2,1)S(1)}, u32[]{:S(2)}, u32[]{:S(2)}) collective-permute-start(bf16[8,2304]{1,0:T(8,128)(2,1)S(1)} %get-tuple-element.58), channel_id=1, source_target_pairs={{0,24},{4,28},{8,16},{12,20},{16,8},{20,12},{24,0},{28,4},{1,25},{... | collective-permute-start | bytes 110600 | tf_op jit(solution)/shard_map/ppermute | solution.py:282
  27.4 2.0 %collective-permute-start.18 = (bf16[8,2304]{1,0:T(8,128)(2,1)S(1)}, bf16[8,2304]{1,0:T(8,128)(2,1)S(1)}, u32[]{:S(2)}, u32[]{:S(2)}) collective-permute-start(bf16[8,2304]{1,0:T(8,128)(2,1)S(1)} %get-tuple-element.59), channel_id=1, source_target_pairs={{0,28},{4,24},{8,20},{12,16},{16,12},{20,8},{24,4},{28,0},{1,29},{... | collective-permute-start | bytes 110600 | tf_op jit(solution)/shard_map/ppermute | solution.py:282
  29.4 1.3 %shard_map.61 = (bf16[192,2048]{1,0:T(8,128)(2,1)S(1)}, bf16[192,512]{1,0:T(8,128)(2,1)S(1)}, bf16[32,2048]{1,0:T(8,128)(2,1)S(1)}, bf16[32,2048]{1,0:T(8,128)(2...) custom-call(bf16[32,2304]{1,0:T(8,128)(2,1)S(1)} %get-tuple-element., ...), custom_call_target="tpu_custom_call" | custom-call | flops 805306368 | bytes 1769472 | tf_op jit(solution)/shard_map/pallas_call | solution.py:265
  31.5 1.3 %collective-permute-done.18.refs_6_ = bf16[8,2304]{1,0:T(8,128)(2,1)S(1)} collective-permute-done((bf16[8,2304]{1,0:T(8,128)(2,1)S(1)}, bf16[8,2304]{1,0:T(8,128)(2,1)S(1)}, u32[]{:S(2)}, u32[]{:S(2)}) %collective-permute-start.18) | collective-permute-done | bytes 36896 | tf_op jit(solution)/shard_map/ppermute | solution.py:282
  32.8 1.8 %shard_map.63 = (bf16[8,2048]{1,0:T(8,128)(2,1)S(1)}, bf16[8,2048]{1,0:T(8,128)(2,1)S(1)}, bf16[8,2048]{1,0:T(8,128)(2,1)S(1)}, bf16[8,2048]{1,0:T(8,128)(2,1)S(...) custom-call(bf16[192,2048]{1,0:T(8,128)(2,1)S(1)} %get-tuple-element, ...), custom_call_target="tpu_custom_call" | custom-call | flops 603979776 | bytes 2064384 | tf_op jit(solution)/shard_map/pallas_call | solution.py:265
  34.6 1.6 %collective-permute-start.24 = (bf16[2,512,256]{2,1,0:T(8,128)(2,1)S(1)}, bf16[2,512,256]{2,1,0:T(8,128)(2,1)S(1)}, u32[]{:S(2)}, u32[]{:S(2)}) collective-permute-start(bf16[2,512,256]{2,1,0:T(8,128)(2,1)S(1)} %get-tuple-element.65), channel_id=1, source_target_pairs={{0,1},{1,0},{2,3},{3,2},{4,5},{5,4},{6,7},{7,6},{8,9},{9,8},{10,11... | collective-permute-start | bytes 1572872 | tf_op jit(solution)/shard_map/ppermute | solution.py:282
  36.7 1.8 %collective-permute-start.11 = (bf16[16,2048]{1,0:T(8,128)(2,1)S(1)}, bf16[16,2048]{1,0:T(8,128)(2,1)S(1)}, u32[]{:S(2)}, u32[]{:S(2)}) collective-permute-start(bf16[16,2048]{1,0:T(8,128)(2,1)S(1)} %get-tuple-element.49), channel_id=1, source_target_pairs={{0,20},{4,16},{8,28},{12,24},{16,4},{20,0},{24,12},{28,8},{1,21},{... | collective-permute-start | bytes 196616 | tf_op jit(solution)/shard_map/ppermute | solution.py:282
  38.5 1.2 %collective-permute-start.7 = (bf16[32,2048]{1,0:T(8,128)(2,1)S(1)}, bf16[32,2048]{1,0:T(8,128)(2,1)S(1)}, u32[]{:S(2)}, u32[]{:S(2)}) collective-permute-start(bf16[32,2048]{1,0:T(8,128)(2,1)S(1)} %get-tuple-element.45), channel_id=1, source_target_pairs={{0,4},{4,0},{8,12},{12,8},{16,20},{20,16},{24,28},{28,24},{1,5},{5... | collective-permute-start | bytes 393224 | tf_op jit(solution)/shard_map/ppermute | solution.py:282
  39.7 8.9 %collective-permute-done.24 = bf16[2,512,256]{2,1,0:T(8,128)(2,1)S(1)} collective-permute-done((bf16[2,512,256]{2,1,0:T(8,128)(2,1)S(1)}, bf16[2,512,256]{2,1,0:T(8,128)(2,1)S(1)}, u32[]{:S(2)}, u32[]{:S(2)}) %collective-permute-start.24) | collective-permute-done | bytes 524320 | tf_op jit(solution)/shard_map/ppermute | solution.py:282
  50.8 1.0 %collective-permute-start.25 = (bf16[1,512,256]{2,1,0:T(8,128)(2,1)S(1)}, bf16[1,512,256]{2,1,0:T(8,128)(2,1)S(1)}, u32[]{:S(2)}, u32[]{:S(2)}) collective-permute-start(bf16[1,512,256]{2,1,0:T(8,128)(2,1)S(1)} %get-tuple-element.70), channel_id=1, source_target_pairs={{0,2},{1,3},{2,0},{3,1},{4,6},{5,7},{6,4},{7,5},{8,10},{9,11},{10,... | collective-permute-start | bytes 786440 | tf_op jit(solution)/shard_map/ppermute | solution.py:282
  53.5 2.0 %collective-permute-start.21 = (bf16[8,2048]{1,0:T(8,128)(2,1)S(1)}, bf16[8,2048]{1,0:T(8,128)(2,1)S(1)}, u32[]{:S(2)}, u32[]{:S(2)}) collective-permute-start(bf16[8,2048]{1,0:T(8,128)(2,1)S(1)} %get-tuple-element.62), channel_id=1, source_target_pairs={{0,24},{4,28},{8,16},{12,20},{16,8},{20,12},{24,0},{28,4},{1,25},{... | collective-permute-start | bytes 98312 | tf_op jit(solution)/shard_map/ppermute | solution.py:282
  55.5 1.5 %collective-permute-start.22 = (bf16[8,2048]{1,0:T(8,128)(2,1)S(1)}, bf16[8,2048]{1,0:T(8,128)(2,1)S(1)}, u32[]{:S(2)}, u32[]{:S(2)}) collective-permute-start(bf16[8,2048]{1,0:T(8,128)(2,1)S(1)} %get-tuple-element.63), channel_id=1, source_target_pairs={{0,28},{4,24},{8,20},{12,16},{16,12},{20,8},{24,4},{28,0},{1,29},{... | collective-permute-start | bytes 98312 | tf_op jit(solution)/shard_map/ppermute | solution.py:282
  57.0 2.2 %collective-permute-done.21.refs_2_.refs_10_ = bf16[8,2048]{1,0:T(8,128)(2,1)S(1)} collective-permute-done((bf16[8,2048]{1,0:T(8,128)(2,1)S(1)}, bf16[8,2048]{1,0:T(8,128)(2,1)S(1)}, u32[]{:S(2)}, u32[]{:S(2)}) %collective-permute-start.21) | collective-permute-done | bytes 32800 | tf_op jit(solution)/shard_map/ppermute | solution.py:282
  59.2 2.0 %collective-permute-start.12 = (bf16[16,2048]{1,0:T(8,128)(2,1)S(1)}, bf16[16,2048]{1,0:T(8,128)(2,1)S(1)}, u32[]{:S(2)}, u32[]{:S(2)}) collective-permute-start(bf16[16,2048]{1,0:T(8,128)(2,1)S(1)} %get-tuple-element.50), channel_id=1, source_target_pairs={{0,24},{4,28},{8,16},{12,20},{16,8},{20,12},{24,0},{28,4},{1,25},{... | collective-permute-start | bytes 196616 | tf_op jit(solution)/shard_map/ppermute | solution.py:282
  62.4 2.9 %collective-permute-done.12.refs_6_ = bf16[16,2048]{1,0:T(8,128)(2,1)S(1)} collective-permute-done((bf16[16,2048]{1,0:T(8,128)(2,1)S(1)}, bf16[16,2048]{1,0:T(8,128)(2,1)S(1)}, u32[]{:S(2)}, u32[]{:S(2)}) %collective-permute-start.12) | collective-permute-done | bytes 65568 | tf_op jit(solution)/shard_map/ppermute | solution.py:282
  65.2 2.0 %collective-permute-done.13.refs_7_ = bf16[16,2048]{1,0:T(8,128)(2,1)S(1)} collective-permute-done((bf16[16,2048]{1,0:T(8,128)(2,1)S(1)}, bf16[16,2048]{1,0:T(8,128)(2,1)S(1)}, u32[]{:S(2)}, u32[]{:S(2)}) %collective-permute-start.13) | collective-permute-done | bytes 65568 | tf_op jit(solution)/shard_map/ppermute | solution.py:282
  67.3 1.4 %collective-permute-start.23 = (bf16[32,2048]{1,0:T(8,128)(2,1)S(1)}, bf16[32,2048]{1,0:T(8,128)(2,1)S(1)}, u32[]{:S(2)}, u32[]{:S(2)}) collective-permute-start(bf16[32,2048]{1,0:T(8,128)(2,1)S(1)} %shard_map.64), channel_id=1, source_target_pairs={{0,2},{1,3},{2,0},{3,1},{4,6},{5,7},{6,4},{7,5},{8,10},{9,11},{10,... | collective-permute-start | bytes 393224 | tf_op jit(solution)/shard_map/ppermute | solution.py:282
  68.7 1.5 %collective-permute-done.8.refs_2_ = bf16[32,2048]{1,0:T(8,128)(2,1)S(1)} collective-permute-done((bf16[32,2048]{1,0:T(8,128)(2,1)S(1)}, bf16[32,2048]{1,0:T(8,128)(2,1)S(1)}, u32[]{:S(2)}, u32[]{:S(2)}) %collective-permute-start.8) | collective-permute-done | bytes 131104 | tf_op jit(solution)/shard_map/ppermute | solution.py:282
  70.2 2.8 %collective-permute-done.9.refs_3_ = bf16[32,2048]{1,0:T(8,128)(2,1)S(1)} collective-permute-done((bf16[32,2048]{1,0:T(8,128)(2,1)S(1)}, bf16[32,2048]{1,0:T(8,128)(2,1)S(1)}, u32[]{:S(2)}, u32[]{:S(2)}) %collective-permute-start.9) | collective-permute-done | bytes 131104 | tf_op jit(solution)/shard_map/ppermute | solution.py:282
  73.0 1.1 %shard_map.65 = bf16[128,2048]{1,0:T(8,128)(2,1)} custom-call(bf16[256,128]{1,0:T(8,128)(2,1)S(1)} %get-tuple-element.35.select_ref, bf16[32,2048]{1,0:T(8,128)(2,1)S(1)} %get-tuple-element.44.refs_0_, bf16[32,2048]{1,0:T(8,128)(2,1)S(1)} %collective-permute-done.7.refs_1_, bf16[32,2048]{1,0:T(8,128)(2,1)S(1)} %collective-permute-done.8.refs_2_, ...), custom_call_target="tpu_custom_call" | custom-call | flops 134217728 | bytes 1048576 | tf_op jit(solution)/shard_map/pallas_call | solution.py:265
  74.2 1.1 %shard_map.66 = f32[512,512]{1,0:T(8,128)} custom-call(f32[1,512,256]{2,1,0:T(8,128)S(1)} %get-tuple-element.71.refs_0_, bf16[1,512,256]{2,1,0:T(8,128)(2,1)S(1)} %collective-permute-done.25.refs_1_, f32[1,512,256]{2,1,0:T(8,128)S(1)} %get-tuple-element.69.refs_2_, bf16[1,512,256]{2,1,0:T(8,128)(2,1)S(1)} %collective-permute-done.27.refs_3_), custom_call_target="tpu_custom_call" | custom-call | flops 524288 | bytes 2621440 | tf_op jit(solution)/shard_map/pallas_call | solution.py:265
  (36 shorter events, 7.8 us)
Async XLA Ops:
  2.2 15.6 %collective-permute-start.14 = (bf16[32,2432]{1,0:T(8,128)(2,1)S(1)}, bf16[32,2432]{1,0:T(8,128)(2,1)S(1)}, u32[]{:S(2)}, u32[]{:S(2)}) collective-permute-start(bf16[32,2432]{1,0:T(8,128)(2,1)S(1)} %get-tuple-element.55), channel_id=1, source_target_pairs={{0,2},{1,3},{2,0},{3,1},{4,6},{5,7},{6,4},{7,5},{8,10},{9,11},{10,... | collective-permute-start | bytes 466952 | tf_op jit(solution)/shard_map/ppermute | solution.py:282
  5.3 6.5 %collective-permute-start.3 = (bf16[16,2304]{1,0:T(8,128)(2,1)S(1)}, bf16[16,2304]{1,0:T(8,128)(2,1)S(1)}, u32[]{:S(2)}, u32[]{:S(2)}) collective-permute-start(bf16[16,2304]{1,0:T(8,128)(2,1)S(1)} %get-tuple-element.40), channel_id=1, source_target_pairs={{0,16},{4,20},{8,24},{12,28},{16,0},{20,4},{24,8},{28,12},{1,17},{... | collective-permute-start | bytes 221192 | tf_op jit(solution)/shard_map/ppermute | solution.py:282
  7.9 7.1 %collective-permute-start.4 = (bf16[16,2304]{1,0:T(8,128)(2,1)S(1)}, bf16[16,2304]{1,0:T(8,128)(2,1)S(1)}, u32[]{:S(2)}, u32[]{:S(2)}) collective-permute-start(bf16[16,2304]{1,0:T(8,128)(2,1)S(1)} %get-tuple-element.41), channel_id=1, source_target_pairs={{0,20},{4,16},{8,28},{12,24},{16,4},{20,0},{24,12},{28,8},{1,21},{... | collective-permute-start | bytes 221192 | tf_op jit(solution)/shard_map/ppermute | solution.py:282
  7.9 17.6 %collective-permute-start = (bf16[32,2304]{1,0:T(8,128)(2,1)S(1)}, bf16[32,2304]{1,0:T(8,128)(2,1)S(1)}, u32[]{:S(2)}, u32[]{:S(2)}) collective-permute-start(bf16[32,2304]{1,0:T(8,128)(2,1)S(1)} %get-tuple-element.37), channel_id=1, source_target_pairs={{0,4},{4,0},{8,12},{12,8},{16,20},{20,16},{24,28},{28,24},{1,5},{5... | collective-permute-start | bytes 442376 | tf_op jit(solution)/shard_map/ppermute | solution.py:282
  8.3 19.1 %collective-permute-start.1 = (bf16[32,2304]{1,0:T(8,128)(2,1)S(1)}, bf16[32,2304]{1,0:T(8,128)(2,1)S(1)}, u32[]{:S(2)}, u32[]{:S(2)}) collective-permute-start(bf16[32,2304]{1,0:T(8,128)(2,1)S(1)} %get-tuple-element.38), channel_id=1, source_target_pairs={{0,8},{4,12},{8,0},{12,4},{16,24},{20,28},{24,16},{28,20},{1,9},{5... | collective-permute-start | bytes 442376 | tf_op jit(solution)/shard_map/ppermute | solution.py:282
  11.8 17.6 %collective-permute-start.2 = (bf16[32,2304]{1,0:T(8,128)(2,1)S(1)}, bf16[32,2304]{1,0:T(8,128)(2,1)S(1)}, u32[]{:S(2)}, u32[]{:S(2)}) collective-permute-start(bf16[32,2304]{1,0:T(8,128)(2,1)S(1)} %get-tuple-element.39), channel_id=1, source_target_pairs={{0,12},{4,8},{8,4},{12,0},{16,28},{20,24},{24,20},{28,16},{1,13},{... | collective-permute-start | bytes 442376 | tf_op jit(solution)/shard_map/ppermute | solution.py:282
  15.0 6.9 %collective-permute-start.5 = (bf16[16,2304]{1,0:T(8,128)(2,1)S(1)}, bf16[16,2304]{1,0:T(8,128)(2,1)S(1)}, u32[]{:S(2)}, u32[]{:S(2)}) collective-permute-start(bf16[16,2304]{1,0:T(8,128)(2,1)S(1)} %get-tuple-element.42), channel_id=1, source_target_pairs={{0,24},{4,28},{8,16},{12,20},{16,8},{20,12},{24,0},{28,4},{1,25},{... | collective-permute-start | bytes 221192 | tf_op jit(solution)/shard_map/ppermute | solution.py:282
  17.9 6.4 %collective-permute-start.6 = (bf16[16,2304]{1,0:T(8,128)(2,1)S(1)}, bf16[16,2304]{1,0:T(8,128)(2,1)S(1)}, u32[]{:S(2)}, u32[]{:S(2)}) collective-permute-start(bf16[16,2304]{1,0:T(8,128)(2,1)S(1)} %get-tuple-element.43), channel_id=1, source_target_pairs={{0,28},{4,24},{8,20},{12,16},{16,12},{20,8},{24,4},{28,0},{1,29},{... | collective-permute-start | bytes 221192 | tf_op jit(solution)/shard_map/ppermute | solution.py:282
  21.8 8.9 %collective-permute-start.15 = (bf16[8,2304]{1,0:T(8,128)(2,1)S(1)}, bf16[8,2304]{1,0:T(8,128)(2,1)S(1)}, u32[]{:S(2)}, u32[]{:S(2)}) collective-permute-start(bf16[8,2304]{1,0:T(8,128)(2,1)S(1)} %get-tuple-element.56), channel_id=1, source_target_pairs={{0,16},{4,20},{8,24},{12,28},{16,0},{20,4},{24,8},{28,12},{1,17},{... | collective-permute-start | bytes 110600 | tf_op jit(solution)/shard_map/ppermute | solution.py:282
  24.2 6.5 %collective-permute-start.16 = (bf16[8,2304]{1,0:T(8,128)(2,1)S(1)}, bf16[8,2304]{1,0:T(8,128)(2,1)S(1)}, u32[]{:S(2)}, u32[]{:S(2)}) collective-permute-start(bf16[8,2304]{1,0:T(8,128)(2,1)S(1)} %get-tuple-element.57), channel_id=1, source_target_pairs={{0,20},{4,16},{8,28},{12,24},{16,4},{20,0},{24,12},{28,8},{1,21},{... | collective-permute-start | bytes 110600 | tf_op jit(solution)/shard_map/ppermute | solution.py:282
  25.4 6.1 %collective-permute-start.17 = (bf16[8,2304]{1,0:T(8,128)(2,1)S(1)}, bf16[8,2304]{1,0:T(8,128)(2,1)S(1)}, u32[]{:S(2)}, u32[]{:S(2)}) collective-permute-start(bf16[8,2304]{1,0:T(8,128)(2,1)S(1)} %get-tuple-element.58), channel_id=1, source_target_pairs={{0,24},{4,28},{8,16},{12,20},{16,8},{20,12},{24,0},{28,4},{1,25},{... | collective-permute-start | bytes 110600 | tf_op jit(solution)/shard_map/ppermute | solution.py:282
  27.4 5.4 %collective-permute-start.18 = (bf16[8,2304]{1,0:T(8,128)(2,1)S(1)}, bf16[8,2304]{1,0:T(8,128)(2,1)S(1)}, u32[]{:S(2)}, u32[]{:S(2)}) collective-permute-start(bf16[8,2304]{1,0:T(8,128)(2,1)S(1)} %get-tuple-element.59), channel_id=1, source_target_pairs={{0,28},{4,24},{8,20},{12,16},{16,12},{20,8},{24,4},{28,0},{1,29},{... | collective-permute-start | bytes 110600 | tf_op jit(solution)/shard_map/ppermute | solution.py:282
  34.6 14.0 %collective-permute-start.24 = (bf16[2,512,256]{2,1,0:T(8,128)(2,1)S(1)}, bf16[2,512,256]{2,1,0:T(8,128)(2,1)S(1)}, u32[]{:S(2)}, u32[]{:S(2)}) collective-permute-start(bf16[2,512,256]{2,1,0:T(8,128)(2,1)S(1)} %get-tuple-element.65), channel_id=1, source_target_pairs={{0,1},{1,0},{2,3},{3,2},{4,5},{5,4},{6,7},{7,6},{8,9},{9,8},{10,11... | collective-permute-start | bytes 1572872 | tf_op jit(solution)/shard_map/ppermute | solution.py:282
  36.2 13.7 %collective-permute-start.26 = (bf16[2,512,256]{2,1,0:T(8,128)(2,1)S(1)}, bf16[2,512,256]{2,1,0:T(8,128)(2,1)S(1)}, u32[]{:S(2)}, u32[]{:S(2)}) collective-permute-start(bf16[2,512,256]{2,1,0:T(8,128)(2,1)S(1)} %get-tuple-element.67), channel_id=1, source_target_pairs={{0,2},{1,3},{2,0},{3,1},{4,6},{5,7},{6,4},{7,5},{8,10},{9,11},{10,... | collective-permute-start | bytes 1572872 | tf_op jit(solution)/shard_map/ppermute | solution.py:282
  36.7 14.1 %collective-permute-start.10 = (bf16[16,2048]{1,0:T(8,128)(2,1)S(1)}, bf16[16,2048]{1,0:T(8,128)(2,1)S(1)}, u32[]{:S(2)}, u32[]{:S(2)}) collective-permute-start(bf16[16,2048]{1,0:T(8,128)(2,1)S(1)} %get-tuple-element.48), channel_id=1, source_target_pairs={{0,16},{4,20},{8,24},{12,28},{16,0},{20,4},{24,8},{28,12},{1,17},{... | collective-permute-start | bytes 196616 | tf_op jit(solution)/shard_map/ppermute | solution.py:282
  36.7 15.1 %collective-permute-start.11 = (bf16[16,2048]{1,0:T(8,128)(2,1)S(1)}, bf16[16,2048]{1,0:T(8,128)(2,1)S(1)}, u32[]{:S(2)}, u32[]{:S(2)}) collective-permute-start(bf16[16,2048]{1,0:T(8,128)(2,1)S(1)} %get-tuple-element.49), channel_id=1, source_target_pairs={{0,20},{4,16},{8,28},{12,24},{16,4},{20,0},{24,12},{28,8},{1,21},{... | collective-permute-start | bytes 196616 | tf_op jit(solution)/shard_map/ppermute | solution.py:282
  38.5 28.8 %collective-permute-start.7 = (bf16[32,2048]{1,0:T(8,128)(2,1)S(1)}, bf16[32,2048]{1,0:T(8,128)(2,1)S(1)}, u32[]{:S(2)}, u32[]{:S(2)}) collective-permute-start(bf16[32,2048]{1,0:T(8,128)(2,1)S(1)} %get-tuple-element.45), channel_id=1, source_target_pairs={{0,4},{4,0},{8,12},{12,8},{16,20},{20,16},{24,28},{28,24},{1,5},{5... | collective-permute-start | bytes 393224 | tf_op jit(solution)/shard_map/ppermute | solution.py:282
  48.6 4.8 %collective-permute-start.19 = (bf16[8,2048]{1,0:T(8,128)(2,1)S(1)}, bf16[8,2048]{1,0:T(8,128)(2,1)S(1)}, u32[]{:S(2)}, u32[]{:S(2)}) collective-permute-start(bf16[8,2048]{1,0:T(8,128)(2,1)S(1)} %get-tuple-element.60), channel_id=1, source_target_pairs={{0,16},{4,20},{8,24},{12,28},{16,0},{20,4},{24,8},{28,12},{1,17},{... | collective-permute-start | bytes 98312 | tf_op jit(solution)/shard_map/ppermute | solution.py:282
  49.9 5.6 %collective-permute-start.20 = (bf16[8,2048]{1,0:T(8,128)(2,1)S(1)}, bf16[8,2048]{1,0:T(8,128)(2,1)S(1)}, u32[]{:S(2)}, u32[]{:S(2)}) collective-permute-start(bf16[8,2048]{1,0:T(8,128)(2,1)S(1)} %get-tuple-element.61), channel_id=1, source_target_pairs={{0,20},{4,16},{8,28},{12,24},{16,4},{20,0},{24,12},{28,8},{1,21},{... | collective-permute-start | bytes 98312 | tf_op jit(solution)/shard_map/ppermute | solution.py:282
  50.8 23.3 %collective-permute-start.25 = (bf16[1,512,256]{2,1,0:T(8,128)(2,1)S(1)}, bf16[1,512,256]{2,1,0:T(8,128)(2,1)S(1)}, u32[]{:S(2)}, u32[]{:S(2)}) collective-permute-start(bf16[1,512,256]{2,1,0:T(8,128)(2,1)S(1)} %get-tuple-element.70), channel_id=1, source_target_pairs={{0,2},{1,3},{2,0},{3,1},{4,6},{5,7},{6,4},{7,5},{8,10},{9,11},{10,... | collective-permute-start | bytes 786440 | tf_op jit(solution)/shard_map/ppermute | solution.py:282
  51.9 22.3 %collective-permute-start.27 = (bf16[1,512,256]{2,1,0:T(8,128)(2,1)S(1)}, bf16[1,512,256]{2,1,0:T(8,128)(2,1)S(1)}, u32[]{:S(2)}, u32[]{:S(2)}) collective-permute-start(bf16[1,512,256]{2,1,0:T(8,128)(2,1)S(1)} %get-tuple-element.68), channel_id=1, source_target_pairs={{0,1},{1,0},{2,3},{3,2},{4,5},{5,4},{6,7},{7,6},{8,9},{9,8},{10,11... | collective-permute-start | bytes 786440 | tf_op jit(solution)/shard_map/ppermute | solution.py:282
  53.5 5.7 %collective-permute-start.21 = (bf16[8,2048]{1,0:T(8,128)(2,1)S(1)}, bf16[8,2048]{1,0:T(8,128)(2,1)S(1)}, u32[]{:S(2)}, u32[]{:S(2)}) collective-permute-start(bf16[8,2048]{1,0:T(8,128)(2,1)S(1)} %get-tuple-element.62), channel_id=1, source_target_pairs={{0,24},{4,28},{8,16},{12,20},{16,8},{20,12},{24,0},{28,4},{1,25},{... | collective-permute-start | bytes 98312 | tf_op jit(solution)/shard_map/ppermute | solution.py:282
  55.5 5.7 %collective-permute-start.22 = (bf16[8,2048]{1,0:T(8,128)(2,1)S(1)}, bf16[8,2048]{1,0:T(8,128)(2,1)S(1)}, u32[]{:S(2)}, u32[]{:S(2)}) collective-permute-start(bf16[8,2048]{1,0:T(8,128)(2,1)S(1)} %get-tuple-element.63), channel_id=1, source_target_pairs={{0,28},{4,24},{8,20},{12,16},{16,12},{20,8},{24,4},{28,0},{1,29},{... | collective-permute-start | bytes 98312 | tf_op jit(solution)/shard_map/ppermute | solution.py:282
  59.2 6.1 %collective-permute-start.12 = (bf16[16,2048]{1,0:T(8,128)(2,1)S(1)}, bf16[16,2048]{1,0:T(8,128)(2,1)S(1)}, u32[]{:S(2)}, u32[]{:S(2)}) collective-permute-start(bf16[16,2048]{1,0:T(8,128)(2,1)S(1)} %get-tuple-element.50), channel_id=1, source_target_pairs={{0,24},{4,28},{8,16},{12,20},{16,8},{20,12},{24,0},{28,4},{1,25},{... | collective-permute-start | bytes 196616 | tf_op jit(solution)/shard_map/ppermute | solution.py:282
  61.2 6.1 %collective-permute-start.13 = (bf16[16,2048]{1,0:T(8,128)(2,1)S(1)}, bf16[16,2048]{1,0:T(8,128)(2,1)S(1)}, u32[]{:S(2)}, u32[]{:S(2)}) collective-permute-start(bf16[16,2048]{1,0:T(8,128)(2,1)S(1)} %get-tuple-element.51), channel_id=1, source_target_pairs={{0,28},{4,24},{8,20},{12,16},{16,12},{20,8},{24,4},{28,0},{1,29},{... | collective-permute-start | bytes 196616 | tf_op jit(solution)/shard_map/ppermute | solution.py:282
  65.2 5.0 %collective-permute-start.8 = (bf16[32,2048]{1,0:T(8,128)(2,1)S(1)}, bf16[32,2048]{1,0:T(8,128)(2,1)S(1)}, u32[]{:S(2)}, u32[]{:S(2)}) collective-permute-start(bf16[32,2048]{1,0:T(8,128)(2,1)S(1)} %get-tuple-element.46), channel_id=1, source_target_pairs={{0,8},{4,12},{8,0},{12,4},{16,24},{20,28},{24,16},{28,20},{1,9},{5... | collective-permute-start | bytes 393224 | tf_op jit(solution)/shard_map/ppermute | solution.py:282
  67.3 5.8 %collective-permute-start.9 = (bf16[32,2048]{1,0:T(8,128)(2,1)S(1)}, bf16[32,2048]{1,0:T(8,128)(2,1)S(1)}, u32[]{:S(2)}, u32[]{:S(2)}) collective-permute-start(bf16[32,2048]{1,0:T(8,128)(2,1)S(1)} %get-tuple-element.47), channel_id=1, source_target_pairs={{0,12},{4,8},{8,4},{12,0},{16,28},{20,24},{24,20},{28,16},{1,13},{... | collective-permute-start | bytes 393224 | tf_op jit(solution)/shard_map/ppermute | solution.py:282
  67.3 5.8 %collective-permute-start.23 = (bf16[32,2048]{1,0:T(8,128)(2,1)S(1)}, bf16[32,2048]{1,0:T(8,128)(2,1)S(1)}, u32[]{:S(2)}, u32[]{:S(2)}) collective-permute-start(bf16[32,2048]{1,0:T(8,128)(2,1)S(1)} %shard_map.64), channel_id=1, source_target_pairs={{0,2},{1,3},{2,0},{3,1},{4,6},{5,7},{6,4},{7,5},{8,10},{9,11},{10,... | collective-permute-start | bytes 393224 | tf_op jit(solution)/shard_map/ppermute | solution.py:282

commit v4 on v3

--- a/solution.py
+++ b/solution.py
@@ -10,8 +10,8 @@
 
 BF16 = jnp.bfloat16
 F32 = jnp.float32
-LATE = ("up0", "up1", "up2", "up3")
-PARTS = 1
+MERGE = 20000
+LATE = ("low2", "low3", "up0", "up1", "up2", "up3")
 VMEM = pl.BlockSpec(memory_space=pltpu.VMEM)
 HBM = pl.BlockSpec(memory_space=pltpu.HBM)
 
@@ -77,6 +77,14 @@
     for copy in copies:
         copy.start()
     return copies
+
+
+def input_scratch(rows, width, hidden):
+    return [
+        pltpu.VMEM((1, rows), jnp.int32),
+        pltpu.VMEM((rows, width + hidden), BF16),
+        pltpu.SemaphoreType.DMA((3,)),
+    ]
 
 
 def dispatch_kernel(experts, *refs):
@@ -118,7 +126,7 @@
     ).astype(BF16)
     copies[1].wait()
     copies[2].wait()
-    for at, size in chunks(joined, 256):
+    for at, size in chunks(joined_ref.shape[1], 256):
         columns = slice(at, at + size)
         placed = dot(select, joined_ref[:, columns])
         unstack(placed, [*near, *low, own_ref, spill_ref], columns)
@@ -162,13 +170,7 @@
         unstack(dot_nt(pre_grad, weights_ref[columns, :]), pieces, columns)
 
 
-def load_kernel(source, target, sem):
-    copy = pltpu.make_async_copy(source, target, sem)
-    copy.start()
-    copy.wait()
-
-
-def rows_grads(pieces, weights_ref, inputs_ref, pre_ref, grads):
+def rows_hidden(pieces, weights_ref, inputs_ref, pre_ref):
     width = weights_ref.shape[0]
     start = 0
     for run in runs(pieces):
@@ -179,7 +181,6 @@
         [stack(run, slice(width, None)).astype(F32) for run in runs(pieces)], axis=0
     )
     pre_ref[...] = hidden_grads(inputs_ref[...], cotangent, weights_ref)
-    input_grads(pre_ref[...], weights_ref, grads)
 
 
 def early_kernel(count, *refs):
@@ -188,21 +189,27 @@
         refs[count : count + 3],
         refs[count + 3 :],
     )
-    rows_grads(pieces, weights_ref, inputs_ref, pre_ref, grads)
-
-
-def late_kernel(groups, parts, count, *refs):
+    rows_hidden(pieces, weights_ref, inputs_ref, pre_ref)
+    input_grads(pre_ref[...], weights_ref, grads)
+
+
+def late_kernel(groups, count, *refs):
     early_inputs_ref, early_pre_ref, weights_ref = refs[:3]
-    pieces, rest = refs[3 : count + 3], refs[count + 3 :]
-    grads, terms, (inputs_ref, pre_ref) = rest[:count], rest[count:-2], rest[-2:]
+    pieces, (late_pre_ref, *terms) = refs[3 : count + 3], refs[count + 3 : -2]
+    inputs_ref, pre_ref = refs[-2:]
     split = early_pre_ref.shape[0]
     inputs_ref[:split, :] = early_inputs_ref[...]
     pre_ref[:split, :] = early_pre_ref[...]
-    rows_grads(pieces, weights_ref, inputs_ref.at[split:, :], pre_ref.at[split:, :], grads)
-    weight_terms(groups, parts, inputs_ref, pre_ref, terms)
-
-
-def weight_terms(groups, parts, inputs_ref, pre_ref, terms):
+    rows_hidden(pieces, weights_ref, inputs_ref.at[split:, :], late_pre_ref)
+    pre_ref[split:, :] = late_pre_ref[...]
+    weight_terms(groups, inputs_ref, pre_ref, *terms)
+
+
+def grads_kernel(pre_ref, weights_ref, *grads):
+    input_grads(pre_ref[...], weights_ref, grads)
+
+
+def weight_terms(groups, inputs_ref, pre_ref, send_a, keep_a, send_b, keep_b):
     me = lax.axis_index("group").astype(jnp.int32)
     part = inputs_ref.shape[1] // groups
     hidden = pre_ref.shape[1] // 2
@@ -210,18 +217,14 @@
     for k in range(groups):
         columns = pl.ds(pl.multiple_of((me ^ k) * part, part), part)
         term = dot_t(inputs_ref[:, columns], pre_grad)
-        for chunk in range(parts):
-            send_a, keep_a, send_b, keep_b = terms[4 * chunk : 4 * chunk + 4]
-            size = part // parts
-            rows = slice(chunk * size, (chunk + 1) * size)
-            if k % 2:
-                send_a[k // 2] = term[rows, :hidden].astype(BF16)
-            else:
-                keep_a[k // 2] = term[rows, :hidden]
-            if k >= groups // 2:
-                send_b[k - groups // 2] = term[rows, hidden:].astype(BF16)
-            else:
-                keep_b[k] = term[rows, hidden:]
+        if k % 2:
+            send_a[k // 2] = term[:, :hidden].astype(BF16)
+        else:
+            keep_a[k // 2] = term[:, :hidden]
+        if k >= groups // 2:
+            send_b[k - groups // 2] = term[:, hidden:].astype(BF16)
+        else:
+            keep_b[k] = term[:, hidden:]
 
 
 def runs(pieces):
@@ -234,29 +237,38 @@
     return found
 
 
-def combine_kernel(select_ref, *refs):
-    *pieces, out_ref, stacked_ref = refs
+def last_kernel(count, *refs):
+    select_ref, pieces, terms = refs[0], refs[1 : count + 1], refs[count + 1 : count + 5]
+    tokens_hbm, weights_hbm, stacked_ref, tokens_ref, weights_ref, sems = refs[count + 5 :]
+    copies = []
+
+    def send(source, target, columns):
+        copy = pltpu.make_async_copy(
+            source.at[:, columns], target.at[:, columns], sems.at[len(copies)]
+        )
+        copy.start()
+        copies.append(copy)
+
     start = 0
     for run in runs(pieces):
         end = start + sum(piece.shape[0] for piece in run)
         stacked_ref[start:end, :] = stack(run)
         start = end
+    hidden = weights_ref.shape[1] // 2
+    for at, keep, got in ((0, *terms[:2]), (hidden, *terms[2:])):
+        columns = slice(at, at + hidden)
+        weights_ref[:, columns] = keep[0] + got[0].astype(F32)
+        send(weights_ref, weights_hbm, columns)
     select = select_ref[...]
-    for at, size in chunks(out_ref.shape[1], 512):
-        out_ref[:, at : at + size] = dot_t(select, stacked_ref[:, at : at + size]).astype(BF16)
-
-
-def finish_kernel(parts, *refs):
-    *terms, out_ref = refs
-    size, hidden = out_ref.shape[0] // parts, out_ref.shape[1] // 2
-    for chunk in range(parts):
-        keep_a, got_a, keep_b, got_b = terms[4 * chunk : 4 * chunk + 4]
-        rows = slice(chunk * size, (chunk + 1) * size)
-        out_ref[rows, :hidden] = keep_a[0] + got_a[0].astype(F32)
-        out_ref[rows, hidden:] = keep_b[0] + got_b[0].astype(F32)
-
-
-def call(kernel, out_shapes, scratch, flops, moved, args, specs=None, vmem=24 << 20):
+    for at, size in chunks(tokens_ref.shape[1], 512):
+        columns = slice(at, at + size)
+        tokens_ref[:, columns] = dot_t(select, stacked_ref[:, columns]).astype(BF16)
+        send(tokens_ref, tokens_hbm, columns)
+    for copy in copies:
+        copy.wait()
+
+
+def call(kernel, out_shapes, scratch, flops, moved, args, specs=None, outs=VMEM, vmem=24 << 20):
     if specs is not None:
         args = [
             pltpu.with_memory_space_constraint(arg, pltpu.HBM) if spec is HBM else arg
@@ -266,7 +278,7 @@
         kernel,
         out_shape=out_shapes,
         in_specs=specs or [VMEM] * len(args),
-        out_specs=jax.tree.map(lambda _: VMEM, out_shapes),
+        out_specs=jax.tree.map(lambda _: outs, out_shapes),
         scratch_shapes=scratch,
         compiler_params=pltpu.CompilerParams(vmem_limit_bytes=vmem),
         cost_estimate=pl.CostEstimate(flops=flops, bytes_accessed=moved, transcendentals=0),
@@ -282,37 +294,43 @@
     return lax.ppermute(value, axis, [(i, i ^ mask) for i in range(size)])
 
 
-def sum_over_groups(terms, groups, parts):
+def sum_over_groups(send_a, keep_a, send_b, keep_b, groups):
     bits = groups.bit_length() - 1
-    last = []
-    for chunk in range(parts):
-        send_a, keep_a, send_b, keep_b = terms[4 * chunk : 4 * chunk + 4]
-        for step in range(bits):
-            got_a = flip(send_a, "group", 1 << step)
-            got_b = flip(send_b, "group", 1 << (bits - 1 - step))
-            if step == bits - 1:
-                last += [keep_a, got_a, keep_b, got_b]
-                break
+    for step in range(bits):
+        got_a = flip(send_a, "group", 1 << step)
+        got_b = flip(send_b, "group", 1 << (bits - 1 - step))
+        if step < bits - 1:
             got_a, got_b = got_a.astype(F32), got_b.astype(F32)
             half = keep_a.shape[0] // 2
             send_a = (keep_a[1::2] + got_a[1::2]).astype(BF16)
             keep_a = keep_a[0::2] + got_a[0::2]
             send_b = (keep_b[half:] + got_b[half:]).astype(BF16)
             keep_b = keep_b[:half] + got_b[:half]
-    rows, columns = parts * last[0].shape[1], 2 * last[0].shape[2]
+    return keep_a, got_a, keep_b, got_b
+
+
+def last(select, pieces, terms, width):
+    slots, rows = select.shape
+    part, columns = terms[0].shape[1], 2 * terms[0].shape[2]
     return call(
-        functools.partial(finish_kernel, parts),
-        shape((rows, columns), F32),
-        [],
-        2 * rows * columns,
-        10 * rows * columns,
-        last,
-    )
-
-
-def term_shapes(groups, width, hidden, parts):
-    block = (groups // 2, width // groups // parts, hidden)
-    return [shape(block), shape(block, F32), shape(block), shape(block, F32)] * parts
+        functools.partial(last_kernel, len(pieces)),
+        [shape((rows, width)), shape((part, columns), F32)],
+        [
+            pltpu.VMEM((slots, width), BF16),
+            pltpu.VMEM((rows, width), BF16),
+            pltpu.VMEM((part, columns), F32),
+            pltpu.SemaphoreType.DMA((2 + len(chunks(width, 512)),)),
+        ],
+        2 * slots * rows * width,
+        2 * slots * width,
+        (select, *pieces, *terms),
+        outs=HBM,
+    )
+
+
+def term_shapes(groups, width, hidden):
+    block = (groups // 2, width // groups, hidden)
+    return [shape(block), shape(block, F32), shape(block), shape(block, F32)]
 
 
 def paired(tokens_in, hidden_grad, routing, weights):
@@ -332,11 +350,7 @@
         [shape((slots, rows)), shape((spill, joined + lane)), shape((half * up_rows, joined))]
         + [shape((full, joined))] * half
         + [shape((low_rows, joined))] * half,
-        [
-            pltpu.VMEM((1, rows), jnp.int32),
-            pltpu.VMEM((rows, joined), BF16),
-            pltpu.SemaphoreType.DMA((3,)),
-        ],
+        input_scratch(rows, width, hidden),
         2 * slots * rows * joined,
         2 * slots * joined,
         (routing.reshape(1, rows), tokens_in, hidden_grad),
@@ -350,21 +364,12 @@
         merge_kernel,
         [shape((up_rows, joined))] * half,
         [],
-        2 * spill * lane * joined,
+        MERGE * weights.size,
         4 * half * up_rows * joined,
         (own, landed),
     )
     up = [flip(up[k], "expert", half + k) for k in range(half)]
 
-    weights = call(
-        load_kernel,
-        shape(weights.shape),
-        [pltpu.SemaphoreType.DMA],
-        0,
-        weights.size * 2,
-        (weights,),
-        specs=[HBM],
-    )
     names = [f"near{k}" for k in range(half)]
     names += [f"low{k}" for k in range(half)] + [f"up{k}" for k in range(half)]
     arrived = dict(zip(names, [*near, *low, *up]))
@@ -384,17 +389,25 @@
         4 * early_rows * joined,
         (*(arrived[name] for name in early), weights),
     )
-    out = call(
-        functools.partial(late_kernel, groups, PARTS, len(late)),
-        grad_shapes(late) + term_shapes(groups, width, hidden, PARTS),
+    late_rows = all_rows - early_rows
+    late_pre, *terms = call(
+        functools.partial(late_kernel, groups, len(late)),
+        [shape((late_rows, 2 * hidden))] + term_shapes(groups, width, hidden),
         [pltpu.VMEM((all_rows, width), BF16), pltpu.VMEM((all_rows, 2 * hidden), BF16)],
-        4 * (all_rows + 2 * (all_rows - early_rows)) * width * hidden,
+        4 * (all_rows + late_rows) * width * hidden,
         4 * all_rows * joined,
         (early_inputs, early_pre, weights, *(arrived[name] for name in late)),
         vmem=32 << 20,
     )
-    terms = out[len(late) :]
-    grads = dict(zip(early + late, [*early_grads, *out[: len(late)]]))
+    late_grads = call(
+        grads_kernel,
+        grad_shapes(late),
+        [],
+        4 * late_rows * width * hidden,
+        4 * late_rows * width,
+        (late_pre, weights),
+    )
+    grads = dict(zip(early + late, [*early_grads, *late_grads]))
     for k in range(half):
         if k:
             grads[f"near{k}"] = flip(grads[f"near{k}"], "expert", k)
@@ -409,16 +422,8 @@
         (landed, *(grads[f"up{k}"] for k in range(half))),
     )
     spilled_grad = flip(spilled_grad, "group", groups // 2)
-    weight_grad = sum_over_groups(terms, groups, PARTS)
-    tokens_grad = call(
-        combine_kernel,
-        shape((rows, width)),
-        [pltpu.VMEM((slots, width), BF16)],
-        2 * slots * rows * width,
-        2 * slots * width,
-        (select, *(grads[name] for name in names), spilled_grad),
-    )
-    return tokens_grad, weight_grad
+    pieces = (*(grads[name] for name in names), spilled_grad)
+    return last(select, pieces, sum_over_groups(*terms, groups), width)
 
 
 def whole_dispatch_kernel(experts, routing_hbm, tokens_hbm, hidden_hbm, select_ref, out_ref, *rest):
@@ -431,15 +436,16 @@
     select_ref[...] = select
     copies[1].wait()
     copies[2].wait()
-    for at, size in chunks(out_ref.shape[1], 256):
+    for at, size in chunks(joined_ref.shape[1], 256):
         columns = slice(at, at + size)
         out_ref[:, columns] = dot(select, joined_ref[:, columns]).astype(BF16)
 
 
 def whole_expert_kernel(groups, rows_ref, weights_ref, grad_ref, *refs):
     *terms, inputs_ref, pre_ref = refs
-    rows_grads([rows_ref], weights_ref, inputs_ref, pre_ref, [grad_ref])
-    weight_terms(groups, 1, inputs_ref, pre_ref, terms)
+    rows_hidden([rows_ref], weights_ref, inputs_ref, pre_ref)
+    input_grads(pre_ref[...], weights_ref, [grad_ref])
+    weight_terms(groups, inputs_ref, pre_ref, *terms)
 
 
 def unpaired(tokens_in, hidden_grad, routing, weights):
@@ -459,11 +465,7 @@
     select, outgoing = call(
         functools.partial(whole_dispatch_kernel, experts),
         [shape((slots, rows)), shape((slots, joined))],
-        [
-            pltpu.VMEM((1, rows), jnp.int32),
-            pltpu.VMEM((rows, joined), BF16),
-            pltpu.SemaphoreType.DMA((3,)),
-        ],
+        input_scratch(rows, width, hidden),
         2 * slots * rows * joined,
         2 * slots * joined,
         (routing.reshape(1, rows), tokens_in, hidden_grad),
@@ -471,23 +473,14 @@
     )
     grad, *terms = call(
         functools.partial(whole_expert_kernel, groups),
-        [shape((slots, width))] + term_shapes(groups, width, hidden, 1),
+        [shape((slots, width))] + term_shapes(groups, width, hidden),
         [pltpu.VMEM((slots, width), BF16), pltpu.VMEM((slots, 2 * hidden), BF16)],
         12 * slots * width * hidden,
         4 * slots * joined,
         (exchange(outgoing), weights),
         vmem=32 << 20,
     )
-    weight_grad = sum_over_groups(terms, groups, 1)
-    tokens_grad = call(
-        combine_kernel,
-        shape((rows, width)),
-        [pltpu.VMEM((slots, width), BF16)],
-        2 * slots * rows * width,
-        2 * slots * width,
-        (select, exchange(grad)),
-    )
-    return tokens_grad, weight_grad
+    return last(select, (exchange(grad),), sum_over_groups(*terms, groups), width)
 
 
 def can_pair(mesh, rows):

time: 75.4 us -> 73.2 us (0.971)
  waiting for transfers between devices: 32.6 us -> 30.3 us
  Pallas kernels: 8.98 us -> 6.75 us
  starting transfers between devices: 32.4 us -> 34.6 us
    ppermute x28, starting transfers between devices: 32.4 us -> 34.6 us  [flip(): return lax.ppermute(value, axis, [(i, i ^ mask) for i in range(size)])]
    ppermute x28, waiting for transfers between devices: 32.6 us -> 30.3 us  [flip(): return lax.ppermute(value, axis, [(i, i ^ mask) for i in range(size)])]
    pallas_call x8 -> x7, Pallas kernels: 8.98 us -> 6.75 us  [call(): pl.pallas_call(kernel, out_shape=out_shapes, in_specs=specs or [VMEM] * l...]
  transfers between devices with their start and end apart: 28 -> 28, of which waited for: 14 -> 11; matrix products, arithmetic and copies ran while one was open for 1% -> 1% of each run, Pallas kernels for 6% -> 3%
where the time goes in v4:
time: 73.2 us; the launch traced here: 73 us
  starting transfers between devices  34.6 us (47%)
  waiting for transfers between devices  30.3 us (41%)
  Pallas kernels  6.75 us (9%)
  between operations  0.75 us (1%)
    ppermute x28, starting transfers between devices, flip(): return lax.ppermute(value, axis, [(i, i ^ mask) for i in range(size)])  34.6 us
    ppermute x28, waiting for transfers between devices, flip(): return lax.ppermute(value, axis, [(i, i ^ mask) for i in range(size)])  30.3 us
    pallas_call x7, Pallas kernels, call(): pl.pallas_call(kernel, out_shape=out_shapes, in_specs=specs or [VMEM] * l...  6.75 us
  transfers between devices with their start and end apart: 28, of which 11 were waited for; matrix products, arithmetic and copies ran while one was open for 1% of the time, Pallas kernels for 3%

profile of v4, /device:TPU:0, one launch (start us, length us, event | category | flops | bytes accessed | tf_op | source)
XLA Modules:
  0.0 73.0 jit_solution(15494868866085671880)
XLA Ops:
  0.6 1.6 %shard_map.59 = (bf16[256,128]{1,0:T(8,128)(2,1)S(1)}, bf16[32,2432]{1,0:T(8,128)(2,1)S(1)}, bf16[32,2304]{1,0:T(8,128)(2,1)S(1)}, bf16[32,2304]{1,0:T(8,128)(2,...) custom-call(s32[1,128]{1,0:T(1,128)} %bitcast.6, ...), custom_call_target="tpu_custom_call" | custom-call | flops 150994944 | bytes 1179648 | tf_op jit(solution)/shard_map/pallas_call | solution.py:277
  2.2 3.1 %collective-permute-start.12 = (bf16[32,2432]{1,0:T(8,128)(2,1)S(1)}, bf16[32,2432]{1,0:T(8,128)(2,1)S(1)}, u32[]{:S(2)}, u32[]{:S(2)}) collective-permute-start(bf16[32,2432]{1,0:T(8,128)(2,1)S(1)} %get-tuple-element.56), channel_id=1, source_target_pairs={{0,2},{1,3},{2,0},{3,1},{4,6},{5,7},{6,4},{7,5},{8,10},{9,11},{10,... | collective-permute-start | bytes 466952 | tf_op jit(solution)/shard_map/ppermute | solution.py:294
  5.3 2.6 %collective-permute-start.3 = (bf16[16,2304]{1,0:T(8,128)(2,1)S(1)}, bf16[16,2304]{1,0:T(8,128)(2,1)S(1)}, u32[]{:S(2)}, u32[]{:S(2)}) collective-permute-start(bf16[16,2304]{1,0:T(8,128)(2,1)S(1)} %get-tuple-element.43), channel_id=1, source_target_pairs={{0,16},{4,20},{8,24},{12,28},{16,0},{20,4},{24,8},{28,12},{1,17},{... | collective-permute-start | bytes 221192 | tf_op jit(solution)/shard_map/ppermute | solution.py:294
  8.3 1.6 %collective-permute-start.1 = (bf16[32,2304]{1,0:T(8,128)(2,1)S(1)}, bf16[32,2304]{1,0:T(8,128)(2,1)S(1)}, u32[]{:S(2)}, u32[]{:S(2)}) collective-permute-start(bf16[32,2304]{1,0:T(8,128)(2,1)S(1)} %get-tuple-element.41), channel_id=1, source_target_pairs={{0,8},{4,12},{8,0},{12,4},{16,24},{20,28},{24,16},{28,20},{1,9},{5... | collective-permute-start | bytes 442376 | tf_op jit(solution)/shard_map/ppermute | solution.py:294
  9.9 1.9 %collective-permute-done.3.refs_4_ = bf16[16,2304]{1,0:T(8,128)(2,1)S(1)} collective-permute-done((bf16[16,2304]{1,0:T(8,128)(2,1)S(1)}, bf16[16,2304]{1,0:T(8,128)(2,1)S(1)}, u32[]{:S(2)}, u32[]{:S(2)}) %collective-permute-start.3) | collective-permute-done | bytes 73760 | tf_op jit(solution)/shard_map/ppermute | solution.py:294
  12.4 2.6 %collective-permute-done.4.refs_5_ = bf16[16,2304]{1,0:T(8,128)(2,1)S(1)} collective-permute-done((bf16[16,2304]{1,0:T(8,128)(2,1)S(1)}, bf16[16,2304]{1,0:T(8,128)(2,1)S(1)}, u32[]{:S(2)}, u32[]{:S(2)}) %collective-permute-start.4) | collective-permute-done | bytes 73760 | tf_op jit(solution)/shard_map/ppermute | solution.py:294
  15.0 2.9 %collective-permute-start.10 = (bf16[16,2304]{1,0:T(8,128)(2,1)S(1)}, bf16[16,2304]{1,0:T(8,128)(2,1)S(1)}, u32[]{:S(2)}, u32[]{:S(2)}) collective-permute-start(bf16[16,2304]{1,0:T(8,128)(2,1)S(1)} %get-tuple-element.53), channel_id=1, source_target_pairs={{0,24},{4,28},{8,16},{12,20},{16,8},{20,12},{24,0},{28,4},{1,25},{... | collective-permute-start | bytes 221192 | tf_op jit(solution)/shard_map/ppermute | solution.py:294
  18.4 3.4 %collective-permute-done.10.refs_3_ = bf16[16,2304]{1,0:T(8,128)(2,1)S(1)} collective-permute-done((bf16[16,2304]{1,0:T(8,128)(2,1)S(1)}, bf16[16,2304]{1,0:T(8,128)(2,1)S(1)}, u32[]{:S(2)}, u32[]{:S(2)}) %collective-permute-start.10) | collective-permute-done | bytes 73760 | tf_op jit(solution)/shard_map/ppermute | solution.py:294
  21.9 2.5 %collective-permute-start.14 = (bf16[8,2304]{1,0:T(8,128)(2,1)S(1)}, bf16[8,2304]{1,0:T(8,128)(2,1)S(1)}, u32[]{:S(2)}, u32[]{:S(2)}) collective-permute-start(bf16[8,2304]{1,0:T(8,128)(2,1)S(1)} %get-tuple-element.58), channel_id=1, source_target_pairs={{0,20},{4,16},{8,28},{12,24},{16,4},{20,0},{24,12},{28,8},{1,21},{... | collective-permute-start | bytes 110600 | tf_op jit(solution)/shard_map/ppermute | solution.py:294
  24.4 1.3 %collective-permute-start.15 = (bf16[8,2304]{1,0:T(8,128)(2,1)S(1)}, bf16[8,2304]{1,0:T(8,128)(2,1)S(1)}, u32[]{:S(2)}, u32[]{:S(2)}) collective-permute-start(bf16[8,2304]{1,0:T(8,128)(2,1)S(1)} %get-tuple-element.59), channel_id=1, source_target_pairs={{0,24},{4,28},{8,16},{12,20},{16,8},{20,12},{24,0},{28,4},{1,25},{... | collective-permute-start | bytes 110600 | tf_op jit(solution)/shard_map/ppermute | solution.py:294
  25.6 2.4 %collective-permute-start.16 = (bf16[8,2304]{1,0:T(8,128)(2,1)S(1)}, bf16[8,2304]{1,0:T(8,128)(2,1)S(1)}, u32[]{:S(2)}, u32[]{:S(2)}) collective-permute-start(bf16[8,2304]{1,0:T(8,128)(2,1)S(1)} %get-tuple-element.60), channel_id=1, source_target_pairs={{0,28},{4,24},{8,20},{12,16},{16,12},{20,8},{24,4},{28,0},{1,29},{... | collective-permute-start | bytes 110600 | tf_op jit(solution)/shard_map/ppermute | solution.py:294
  28.1 1.3 %shard_map.60 = (bf16[160,2048]{1,0:T(8,128)(2,1)S(1)}, bf16[160,512]{1,0:T(8,128)(2,1)S(1)}, bf16[32,2048]{1,0:T(8,128)(2,1)S(1)}, bf16[32,2048]{1,0:T(8,128)(2...) custom-call(bf16[32,2304]{1,0:T(8,128)(2,1)S(1)} %get-tuple-element., ...), custom_call_target="tpu_custom_call" | custom-call | flops 671088640 | bytes 1474560 | tf_op jit(solution)/shard_map/pallas_call | solution.py:277
  29.4 0.8 %collective-permute-done.15.refs_7_ = bf16[8,2304]{1,0:T(8,128)(2,1)S(1)} collective-permute-done((bf16[8,2304]{1,0:T(8,128)(2,1)S(1)}, bf16[8,2304]{1,0:T(8,128)(2,1)S(1)}, u32[]{:S(2)}, u32[]{:S(2)}) %collective-permute-start.15) | collective-permute-done | bytes 36896 | tf_op jit(solution)/shard_map/ppermute | solution.py:294
  30.8 1.2 %shard_map.62 = (bf16[64,512]{1,0:T(8,128)(2,1)S(1)}, bf16[2,512,256]{2,1,0:T(8,128)(2,1)S(1)}, f32[2,512,256]{2,1,0:T(8,128)S(1)}, bf16[2,512,256]{2,1,0:T(8,128)(2,1)S(1)}, f32[2,512,256]{2,1,0:T(8,128)S(1)}) custom-call(bf16[160,2048]{1,0:T(8,128)(2,1)S(1)} %get-tuple-element.51.refs_0_, bf16[160,512]{1,0:T(8,128)(2,1)S(1)} %get-tuple-element.52.refs_1_, ...), custom_call_target="tpu_custom_call" | custom-call | flops 603979776 | bytes 2064384 | tf_op jit(solution)/shard_map/pallas_call | solution.py:277
  32.1 1.0 %collective-permute-start.26 = (bf16[2,512,256]{2,1,0:T(8,128)(2,1)S(1)}, bf16[2,512,256]{2,1,0:T(8,128)(2,1)S(1)}, u32[]{:S(2)}, u32[]{:S(2)}) collective-permute-start(bf16[2,512,256]{2,1,0:T(8,128)(2,1)S(1)} %get-tuple-element.71), channel_id=1, source_target_pairs={{0,2},{1,3},{2,0},{3,1},{4,6},{5,7},{6,4},{7,5},{8,10},{9,11},{10,... | collective-permute-start | bytes 1572872 | tf_op jit(solution)/shard_map/ppermute | solution.py:294
  33.1 1.0 %collective-permute-start.24 = (bf16[2,512,256]{2,1,0:T(8,128)(2,1)S(1)}, bf16[2,512,256]{2,1,0:T(8,128)(2,1)S(1)}, u32[]{:S(2)}, u32[]{:S(2)}) collective-permute-start(bf16[2,512,256]{2,1,0:T(8,128)(2,1)S(1)} %get-tuple-element.69), channel_id=1, source_target_pairs={{0,1},{1,0},{2,3},{3,2},{4,5},{5,4},{6,7},{7,6},{8,9},{9,8},{10,11... | collective-permute-start | bytes 1572872 | tf_op jit(solution)/shard_map/ppermute | solution.py:294
  34.1 1.2 %collective-permute-start.5 = (bf16[32,2048]{1,0:T(8,128)(2,1)S(1)}, bf16[32,2048]{1,0:T(8,128)(2,1)S(1)}, u32[]{:S(2)}, u32[]{:S(2)}) collective-permute-start(bf16[32,2048]{1,0:T(8,128)(2,1)S(1)} %get-tuple-element.46), channel_id=1, source_target_pairs={{0,4},{4,0},{8,12},{12,8},{16,20},{20,16},{24,28},{28,24},{1,5},{5... | collective-permute-start | bytes 393224 | tf_op jit(solution)/shard_map/ppermute | solution.py:294
  35.7 1.9 %collective-permute-start.9 = (bf16[16,2048]{1,0:T(8,128)(2,1)S(1)}, bf16[16,2048]{1,0:T(8,128)(2,1)S(1)}, u32[]{:S(2)}, u32[]{:S(2)}) collective-permute-start(bf16[16,2048]{1,0:T(8,128)(2,1)S(1)} %get-tuple-element.50), channel_id=1, source_target_pairs={{0,20},{4,16},{8,28},{12,24},{16,4},{20,0},{24,12},{28,8},{1,21},{... | collective-permute-start | bytes 196616 | tf_op jit(solution)/shard_map/ppermute | solution.py:294
  37.6 0.7 %shard_map.63 = (bf16[16,2048]{1,0:T(8,128)(2,1)S(1)}, bf16[16,2048]{1,0:T(8,128)(2,1)S(1)}, bf16[8,2048]{1,0:T(8,128)(2,1)S(1)}, bf16[8,2048]{1,0:T(8,128)(2,1)...) custom-call(bf16[64,512]{1,0:T(8,128)(2,1)S(1)} %get-tuple-element.61.pre_ref, bf16[2048,512]{1,0:T(8,128)(2,1)S(1)} %bitcast.5), custom_call_target="tpu_custom_call" | custom-call | flops 134217728 | bytes 524288 | tf_op jit(solution)/shard_map/pallas_call | solution.py:277
  38.3 7.8 %collective-permute-done.26 = bf16[2,512,256]{2,1,0:T(8,128)(2,1)S(1)} collective-permute-done((bf16[2,512,256]{2,1,0:T(8,128)(2,1)S(1)}, bf16[2,512,256]{2,1,0:T(8,128)(2,1)S(1)}, u32[]{:S(2)}, u32[]{:S(2)}) %collective-permute-start.26) | collective-permute-done | bytes 524320 | tf_op jit(solution)/shard_map/ppermute | solution.py:294
  46.1 1.9 %collective-permute-start.19 = (bf16[8,2048]{1,0:T(8,128)(2,1)S(1)}, bf16[8,2048]{1,0:T(8,128)(2,1)S(1)}, u32[]{:S(2)}, u32[]{:S(2)}) collective-permute-start(bf16[8,2048]{1,0:T(8,128)(2,1)S(1)} %get-tuple-element.64), channel_id=1, source_target_pairs={{0,16},{4,20},{8,24},{12,28},{16,0},{20,4},{24,8},{28,12},{1,17},{... | collective-permute-start | bytes 98312 | tf_op jit(solution)/shard_map/ppermute | solution.py:294
  48.3 1.3 %collective-permute-start.20 = (bf16[8,2048]{1,0:T(8,128)(2,1)S(1)}, bf16[8,2048]{1,0:T(8,128)(2,1)S(1)}, u32[]{:S(2)}, u32[]{:S(2)}) collective-permute-start(bf16[8,2048]{1,0:T(8,128)(2,1)S(1)} %get-tuple-element.65), channel_id=1, source_target_pairs={{0,20},{4,16},{8,28},{12,24},{16,4},{20,0},{24,12},{28,8},{1,21},{... | collective-permute-start | bytes 98312 | tf_op jit(solution)/shard_map/ppermute | solution.py:294
  50.0 1.6 %collective-permute-start.27 = (bf16[1,512,256]{2,1,0:T(8,128)(2,1)S(1)}, bf16[1,512,256]{2,1,0:T(8,128)(2,1)S(1)}, u32[]{:S(2)}, u32[]{:S(2)}) collective-permute-start(bf16[1,512,256]{2,1,0:T(8,128)(2,1)S(1)} %get-tuple-element.74), channel_id=1, source_target_pairs={{0,1},{1,0},{2,3},{3,2},{4,5},{5,4},{6,7},{7,6},{8,9},{9,8},{10,11... | collective-permute-start | bytes 786440 | tf_op jit(solution)/shard_map/ppermute | solution.py:294
  52.0 2.0 %collective-permute-start.21 = (bf16[8,2048]{1,0:T(8,128)(2,1)S(1)}, bf16[8,2048]{1,0:T(8,128)(2,1)S(1)}, u32[]{:S(2)}, u32[]{:S(2)}) collective-permute-start(bf16[8,2048]{1,0:T(8,128)(2,1)S(1)} %get-tuple-element.66), channel_id=1, source_target_pairs={{0,24},{4,28},{8,16},{12,20},{16,8},{20,12},{24,0},{28,4},{1,25},{... | collective-permute-start | bytes 98312 | tf_op jit(solution)/shard_map/ppermute | solution.py:294
  54.6 3.2 %collective-permute-done.21.refs_2_.refs_11_ = bf16[8,2048]{1,0:T(8,128)(2,1)S(1)} collective-permute-done((bf16[8,2048]{1,0:T(8,128)(2,1)S(1)}, bf16[8,2048]{1,0:T(8,128)(2,1)S(1)}, u32[]{:S(2)}, u32[]{:S(2)}) %collective-permute-start.21) | collective-permute-done | bytes 32800 | tf_op jit(solution)/shard_map/ppermute | solution.py:294
  57.7 2.0 %collective-permute-start.17 = (bf16[16,2048]{1,0:T(8,128)(2,1)S(1)}, bf16[16,2048]{1,0:T(8,128)(2,1)S(1)}, u32[]{:S(2)}, u32[]{:S(2)}) collective-permute-start(bf16[16,2048]{1,0:T(8,128)(2,1)S(1)} %get-tuple-element.62), channel_id=1, source_target_pairs={{0,24},{4,28},{8,16},{12,20},{16,8},{20,12},{24,0},{28,4},{1,25},{... | collective-permute-start | bytes 196616 | tf_op jit(solution)/shard_map/ppermute | solution.py:294
  59.9 3.9 %collective-permute-done.17.refs_7_ = bf16[16,2048]{1,0:T(8,128)(2,1)S(1)} collective-permute-done((bf16[16,2048]{1,0:T(8,128)(2,1)S(1)}, bf16[16,2048]{1,0:T(8,128)(2,1)S(1)}, u32[]{:S(2)}, u32[]{:S(2)}) %collective-permute-start.17) | collective-permute-done | bytes 65568 | tf_op jit(solution)/shard_map/ppermute | solution.py:294
  63.8 2.2 %collective-permute-done.18.refs_8_ = bf16[16,2048]{1,0:T(8,128)(2,1)S(1)} collective-permute-done((bf16[16,2048]{1,0:T(8,128)(2,1)S(1)}, bf16[16,2048]{1,0:T(8,128)(2,1)S(1)}, u32[]{:S(2)}, u32[]{:S(2)}) %collective-permute-start.18) | collective-permute-done | bytes 65568 | tf_op jit(solution)/shard_map/ppermute | solution.py:294
  66.0 1.8 %collective-permute-start.23 = (bf16[32,2048]{1,0:T(8,128)(2,1)S(1)}, bf16[32,2048]{1,0:T(8,128)(2,1)S(1)}, u32[]{:S(2)}, u32[]{:S(2)}) collective-permute-start(bf16[32,2048]{1,0:T(8,128)(2,1)S(1)} %shard_map.64), channel_id=1, source_target_pairs={{0,2},{1,3},{2,0},{3,1},{4,6},{5,7},{6,4},{7,5},{8,10},{9,11},{10,... | collective-permute-start | bytes 393224 | tf_op jit(solution)/shard_map/ppermute | solution.py:294
  67.8 1.0 %collective-permute-done.6.refs_3_ = bf16[32,2048]{1,0:T(8,128)(2,1)S(1)} collective-permute-done((bf16[32,2048]{1,0:T(8,128)(2,1)S(1)}, bf16[32,2048]{1,0:T(8,128)(2,1)S(1)}, u32[]{:S(2)}, u32[]{:S(2)}) %collective-permute-start.6) | collective-permute-done | bytes 131104 | tf_op jit(solution)/shard_map/ppermute | solution.py:294
  68.8 2.8 %collective-permute-done.7.refs_4_ = bf16[32,2048]{1,0:T(8,128)(2,1)S(1)} collective-permute-done((bf16[32,2048]{1,0:T(8,128)(2,1)S(1)}, bf16[32,2048]{1,0:T(8,128)(2,1)S(1)}, u32[]{:S(2)}, u32[]{:S(2)}) %collective-permute-start.7) | collective-permute-done | bytes 131104 | tf_op jit(solution)/shard_map/ppermute | solution.py:294
  71.6 1.4 %shard_map.65 = (bf16[128,2048]{1,0:T(8,128)(2,1)}, f32[512,512]{1,0:T(8,128)}) custom-call(bf16[256,128]{1,0:T(8,128)(2,1)S(1)} %get-tuple-element.38.refs_0_, bf16[32,2048]{1,0:T(8,128)(2,1)S(1)} %get-tuple-element.45.refs_1_, bf16[32,2048]{1,0:T(8,128)(2,1)S(1)} %collective-permute-done.5.refs_2_, bf16[32,2048]{1,0:T(8,128)(2,1)S(1)} %collective-permute-done.6.refs_3_, ...), custom_call_target="tpu_custom_call" | custom-call | flops 134217728 | bytes 1048576 | tf_op jit(solution)/shard_map/pallas_call | solution.py:277
  (37 shorter events, 4.5 us)
Async XLA Ops:
  2.2 15.6 %collective-permute-start.12 = (bf16[32,2432]{1,0:T(8,128)(2,1)S(1)}, bf16[32,2432]{1,0:T(8,128)(2,1)S(1)}, u32[]{:S(2)}, u32[]{:S(2)}) collective-permute-start(bf16[32,2432]{1,0:T(8,128)(2,1)S(1)} %get-tuple-element.56), channel_id=1, source_target_pairs={{0,2},{1,3},{2,0},{3,1},{4,6},{5,7},{6,4},{7,5},{8,10},{9,11},{10,... | collective-permute-start | bytes 466952 | tf_op jit(solution)/shard_map/ppermute | solution.py:294
  5.3 6.5 %collective-permute-start.3 = (bf16[16,2304]{1,0:T(8,128)(2,1)S(1)}, bf16[16,2304]{1,0:T(8,128)(2,1)S(1)}, u32[]{:S(2)}, u32[]{:S(2)}) collective-permute-start(bf16[16,2304]{1,0:T(8,128)(2,1)S(1)} %get-tuple-element.43), channel_id=1, source_target_pairs={{0,16},{4,20},{8,24},{12,28},{16,0},{20,4},{24,8},{28,12},{1,17},{... | collective-permute-start | bytes 221192 | tf_op jit(solution)/shard_map/ppermute | solution.py:294
  7.9 7.1 %collective-permute-start.4 = (bf16[16,2304]{1,0:T(8,128)(2,1)S(1)}, bf16[16,2304]{1,0:T(8,128)(2,1)S(1)}, u32[]{:S(2)}, u32[]{:S(2)}) collective-permute-start(bf16[16,2304]{1,0:T(8,128)(2,1)S(1)} %get-tuple-element.44), channel_id=1, source_target_pairs={{0,20},{4,16},{8,28},{12,24},{16,4},{20,0},{24,12},{28,8},{1,21},{... | collective-permute-start | bytes 221192 | tf_op jit(solution)/shard_map/ppermute | solution.py:294
  7.9 14.0 %collective-permute-start = (bf16[32,2304]{1,0:T(8,128)(2,1)S(1)}, bf16[32,2304]{1,0:T(8,128)(2,1)S(1)}, u32[]{:S(2)}, u32[]{:S(2)}) collective-permute-start(bf16[32,2304]{1,0:T(8,128)(2,1)S(1)} %get-tuple-element.40), channel_id=1, source_target_pairs={{0,4},{4,0},{8,12},{12,8},{16,20},{20,16},{24,28},{28,24},{1,5},{5... | collective-permute-start | bytes 442376 | tf_op jit(solution)/shard_map/ppermute | solution.py:294
  8.3 16.1 %collective-permute-start.1 = (bf16[32,2304]{1,0:T(8,128)(2,1)S(1)}, bf16[32,2304]{1,0:T(8,128)(2,1)S(1)}, u32[]{:S(2)}, u32[]{:S(2)}) collective-permute-start(bf16[32,2304]{1,0:T(8,128)(2,1)S(1)} %get-tuple-element.41), channel_id=1, source_target_pairs={{0,8},{4,12},{8,0},{12,4},{16,24},{20,28},{24,16},{28,20},{1,9},{5... | collective-permute-start | bytes 442376 | tf_op jit(solution)/shard_map/ppermute | solution.py:294
  11.8 13.8 %collective-permute-start.2 = (bf16[32,2304]{1,0:T(8,128)(2,1)S(1)}, bf16[32,2304]{1,0:T(8,128)(2,1)S(1)}, u32[]{:S(2)}, u32[]{:S(2)}) collective-permute-start(bf16[32,2304]{1,0:T(8,128)(2,1)S(1)} %get-tuple-element.42), channel_id=1, source_target_pairs={{0,12},{4,8},{8,4},{12,0},{16,28},{20,24},{24,20},{28,16},{1,13},{... | collective-permute-start | bytes 442376 | tf_op jit(solution)/shard_map/ppermute | solution.py:294
  15.0 6.9 %collective-permute-start.10 = (bf16[16,2304]{1,0:T(8,128)(2,1)S(1)}, bf16[16,2304]{1,0:T(8,128)(2,1)S(1)}, u32[]{:S(2)}, u32[]{:S(2)}) collective-permute-start(bf16[16,2304]{1,0:T(8,128)(2,1)S(1)} %get-tuple-element.53), channel_id=1, source_target_pairs={{0,24},{4,28},{8,16},{12,20},{16,8},{20,12},{24,0},{28,4},{1,25},{... | collective-permute-start | bytes 221192 | tf_op jit(solution)/shard_map/ppermute | solution.py:294
  17.9 11.5 %collective-permute-start.11 = (bf16[16,2304]{1,0:T(8,128)(2,1)S(1)}, bf16[16,2304]{1,0:T(8,128)(2,1)S(1)}, u32[]{:S(2)}, u32[]{:S(2)}) collective-permute-start(bf16[16,2304]{1,0:T(8,128)(2,1)S(1)} %get-tuple-element.54), channel_id=1, source_target_pairs={{0,28},{4,24},{8,20},{12,16},{16,12},{20,8},{24,4},{28,0},{1,29},{... | collective-permute-start | bytes 221192 | tf_op jit(solution)/shard_map/ppermute | solution.py:294
  18.1 10.0 %copy-start = (bf16[1,2048,512]{2,1,0:T(8,128)(2,1)S(1)}, bf16[1,2048,512]{2,1,0:T(8,128)(2,1)}, u32[]{:S(2)}) copy-start(bf16[1,2048,512]{2,1,0:T(8,128)(2,1)} %param.7) | copy-start | bytes 6291460
  21.8 7.5 %collective-permute-start.13 = (bf16[8,2304]{1,0:T(8,128)(2,1)S(1)}, bf16[8,2304]{1,0:T(8,128)(2,1)S(1)}, u32[]{:S(2)}, u32[]{:S(2)}) collective-permute-start(bf16[8,2304]{1,0:T(8,128)(2,1)S(1)} %get-tuple-element.57), channel_id=1, source_target_pairs={{0,16},{4,20},{8,24},{12,28},{16,0},{20,4},{24,8},{28,12},{1,17},{... | collective-permute-start | bytes 110600 | tf_op jit(solution)/shard_map/ppermute | solution.py:294
  21.9 7.5 %collective-permute-start.14 = (bf16[8,2304]{1,0:T(8,128)(2,1)S(1)}, bf16[8,2304]{1,0:T(8,128)(2,1)S(1)}, u32[]{:S(2)}, u32[]{:S(2)}) collective-permute-start(bf16[8,2304]{1,0:T(8,128)(2,1)S(1)} %get-tuple-element.58), channel_id=1, source_target_pairs={{0,20},{4,16},{8,28},{12,24},{16,4},{20,0},{24,12},{28,8},{1,21},{... | collective-permute-start | bytes 110600 | tf_op jit(solution)/shard_map/ppermute | solution.py:294
  24.4 5.8 %collective-permute-start.15 = (bf16[8,2304]{1,0:T(8,128)(2,1)S(1)}, bf16[8,2304]{1,0:T(8,128)(2,1)S(1)}, u32[]{:S(2)}, u32[]{:S(2)}) collective-permute-start(bf16[8,2304]{1,0:T(8,128)(2,1)S(1)} %get-tuple-element.59), channel_id=1, source_target_pairs={{0,24},{4,28},{8,16},{12,20},{16,8},{20,12},{24,0},{28,4},{1,25},{... | collective-permute-start | bytes 110600 | tf_op jit(solution)/shard_map/ppermute | solution.py:294
  25.6 5.2 %collective-permute-start.16 = (bf16[8,2304]{1,0:T(8,128)(2,1)S(1)}, bf16[8,2304]{1,0:T(8,128)(2,1)S(1)}, u32[]{:S(2)}, u32[]{:S(2)}) collective-permute-start(bf16[8,2304]{1,0:T(8,128)(2,1)S(1)} %get-tuple-element.60), channel_id=1, source_target_pairs={{0,28},{4,24},{8,20},{12,16},{16,12},{20,8},{24,4},{28,0},{1,29},{... | collective-permute-start | bytes 110600 | tf_op jit(solution)/shard_map/ppermute | solution.py:294
  32.1 14.1 %collective-permute-start.26 = (bf16[2,512,256]{2,1,0:T(8,128)(2,1)S(1)}, bf16[2,512,256]{2,1,0:T(8,128)(2,1)S(1)}, u32[]{:S(2)}, u32[]{:S(2)}) collective-permute-start(bf16[2,512,256]{2,1,0:T(8,128)(2,1)S(1)} %get-tuple-element.71), channel_id=1, source_target_pairs={{0,2},{1,3},{2,0},{3,1},{4,6},{5,7},{6,4},{7,5},{8,10},{9,11},{10,... | collective-permute-start | bytes 1572872 | tf_op jit(solution)/shard_map/ppermute | solution.py:294
  33.1 15.2 %collective-permute-start.24 = (bf16[2,512,256]{2,1,0:T(8,128)(2,1)S(1)}, bf16[2,512,256]{2,1,0:T(8,128)(2,1)S(1)}, u32[]{:S(2)}, u32[]{:S(2)}) collective-permute-start(bf16[2,512,256]{2,1,0:T(8,128)(2,1)S(1)} %get-tuple-element.69), channel_id=1, source_target_pairs={{0,1},{1,0},{2,3},{3,2},{4,5},{5,4},{6,7},{7,6},{8,9},{9,8},{10,11... | collective-permute-start | bytes 1572872 | tf_op jit(solution)/shard_map/ppermute | solution.py:294
  34.1 31.9 %collective-permute-start.5 = (bf16[32,2048]{1,0:T(8,128)(2,1)S(1)}, bf16[32,2048]{1,0:T(8,128)(2,1)S(1)}, u32[]{:S(2)}, u32[]{:S(2)}) collective-permute-start(bf16[32,2048]{1,0:T(8,128)(2,1)S(1)} %get-tuple-element.46), channel_id=1, source_target_pairs={{0,4},{4,0},{8,12},{12,8},{16,20},{20,16},{24,28},{28,24},{1,5},{5... | collective-permute-start | bytes 393224 | tf_op jit(solution)/shard_map/ppermute | solution.py:294
  35.3 14.6 %collective-permute-start.8 = (bf16[16,2048]{1,0:T(8,128)(2,1)S(1)}, bf16[16,2048]{1,0:T(8,128)(2,1)S(1)}, u32[]{:S(2)}, u32[]{:S(2)}) collective-permute-start(bf16[16,2048]{1,0:T(8,128)(2,1)S(1)} %get-tuple-element.49), channel_id=1, source_target_pairs={{0,16},{4,20},{8,24},{12,28},{16,0},{20,4},{24,8},{28,12},{1,17},{... | collective-permute-start | bytes 196616 | tf_op jit(solution)/shard_map/ppermute | solution.py:294
  35.7 15.8 %collective-permute-start.9 = (bf16[16,2048]{1,0:T(8,128)(2,1)S(1)}, bf16[16,2048]{1,0:T(8,128)(2,1)S(1)}, u32[]{:S(2)}, u32[]{:S(2)}) collective-permute-start(bf16[16,2048]{1,0:T(8,128)(2,1)S(1)} %get-tuple-element.50), channel_id=1, source_target_pairs={{0,20},{4,16},{8,28},{12,24},{16,4},{20,0},{24,12},{28,8},{1,21},{... | collective-permute-start | bytes 196616 | tf_op jit(solution)/shard_map/ppermute | solution.py:294
  46.1 5.9 %collective-permute-start.19 = (bf16[8,2048]{1,0:T(8,128)(2,1)S(1)}, bf16[8,2048]{1,0:T(8,128)(2,1)S(1)}, u32[]{:S(2)}, u32[]{:S(2)}) collective-permute-start(bf16[8,2048]{1,0:T(8,128)(2,1)S(1)} %get-tuple-element.64), channel_id=1, source_target_pairs={{0,16},{4,20},{8,24},{12,28},{16,0},{20,4},{24,8},{28,12},{1,17},{... | collective-permute-start | bytes 98312 | tf_op jit(solution)/shard_map/ppermute | solution.py:294
  48.3 5.7 %collective-permute-start.20 = (bf16[8,2048]{1,0:T(8,128)(2,1)S(1)}, bf16[8,2048]{1,0:T(8,128)(2,1)S(1)}, u32[]{:S(2)}, u32[]{:S(2)}) collective-permute-start(bf16[8,2048]{1,0:T(8,128)(2,1)S(1)} %get-tuple-element.65), channel_id=1, source_target_pairs={{0,20},{4,16},{8,28},{12,24},{16,4},{20,0},{24,12},{28,8},{1,21},{... | collective-permute-start | bytes 98312 | tf_op jit(solution)/shard_map/ppermute | solution.py:294
  50.0 21.6 %collective-permute-start.27 = (bf16[1,512,256]{2,1,0:T(8,128)(2,1)S(1)}, bf16[1,512,256]{2,1,0:T(8,128)(2,1)S(1)}, u32[]{:S(2)}, u32[]{:S(2)}) collective-permute-start(bf16[1,512,256]{2,1,0:T(8,128)(2,1)S(1)} %get-tuple-element.74), channel_id=1, source_target_pairs={{0,1},{1,0},{2,3},{3,2},{4,5},{5,4},{6,7},{7,6},{8,9},{9,8},{10,11... | collective-permute-start | bytes 786440 | tf_op jit(solution)/shard_map/ppermute | solution.py:294
  51.5 20.1 %collective-permute-start.25 = (bf16[1,512,256]{2,1,0:T(8,128)(2,1)S(1)}, bf16[1,512,256]{2,1,0:T(8,128)(2,1)S(1)}, u32[]{:S(2)}, u32[]{:S(2)}) collective-permute-start(bf16[1,512,256]{2,1,0:T(8,128)(2,1)S(1)} %get-tuple-element.76), channel_id=1, source_target_pairs={{0,2},{1,3},{2,0},{3,1},{4,6},{5,7},{6,4},{7,5},{8,10},{9,11},{10,... | collective-permute-start | bytes 786440 | tf_op jit(solution)/shard_map/ppermute | solution.py:294
  52.0 5.7 %collective-permute-start.21 = (bf16[8,2048]{1,0:T(8,128)(2,1)S(1)}, bf16[8,2048]{1,0:T(8,128)(2,1)S(1)}, u32[]{:S(2)}, u32[]{:S(2)}) collective-permute-start(bf16[8,2048]{1,0:T(8,128)(2,1)S(1)} %get-tuple-element.66), channel_id=1, source_target_pairs={{0,24},{4,28},{8,16},{12,20},{16,8},{20,12},{24,0},{28,4},{1,25},{... | collective-permute-start | bytes 98312 | tf_op jit(solution)/shard_map/ppermute | solution.py:294
  54.0 5.7 %collective-permute-start.22 = (bf16[8,2048]{1,0:T(8,128)(2,1)S(1)}, bf16[8,2048]{1,0:T(8,128)(2,1)S(1)}, u32[]{:S(2)}, u32[]{:S(2)}) collective-permute-start(bf16[8,2048]{1,0:T(8,128)(2,1)S(1)} %get-tuple-element.67), channel_id=1, source_target_pairs={{0,28},{4,24},{8,20},{12,16},{16,12},{20,8},{24,4},{28,0},{1,29},{... | collective-permute-start | bytes 98312 | tf_op jit(solution)/shard_map/ppermute | solution.py:294
  57.7 6.1 %collective-permute-start.17 = (bf16[16,2048]{1,0:T(8,128)(2,1)S(1)}, bf16[16,2048]{1,0:T(8,128)(2,1)S(1)}, u32[]{:S(2)}, u32[]{:S(2)}) collective-permute-start(bf16[16,2048]{1,0:T(8,128)(2,1)S(1)} %get-tuple-element.62), channel_id=1, source_target_pairs={{0,24},{4,28},{8,16},{12,20},{16,8},{20,12},{24,0},{28,4},{1,25},{... | collective-permute-start | bytes 196616 | tf_op jit(solution)/shard_map/ppermute | solution.py:294
  59.7 6.3 %collective-permute-start.18 = (bf16[16,2048]{1,0:T(8,128)(2,1)S(1)}, bf16[16,2048]{1,0:T(8,128)(2,1)S(1)}, u32[]{:S(2)}, u32[]{:S(2)}) collective-permute-start(bf16[16,2048]{1,0:T(8,128)(2,1)S(1)} %get-tuple-element.63), channel_id=1, source_target_pairs={{0,28},{4,24},{8,20},{12,16},{16,12},{20,8},{24,4},{28,0},{1,29},{... | collective-permute-start | bytes 196616 | tf_op jit(solution)/shard_map/ppermute | solution.py:294
  63.8 5.0 %collective-permute-start.6 = (bf16[32,2048]{1,0:T(8,128)(2,1)S(1)}, bf16[32,2048]{1,0:T(8,128)(2,1)S(1)}, u32[]{:S(2)}, u32[]{:S(2)}) collective-permute-start(bf16[32,2048]{1,0:T(8,128)(2,1)S(1)} %get-tuple-element.47), channel_id=1, source_target_pairs={{0,8},{4,12},{8,0},{12,4},{16,24},{20,28},{24,16},{28,20},{1,9},{5... | collective-permute-start | bytes 393224 | tf_op jit(solution)/shard_map/ppermute | solution.py:294
  66.0 5.6 %collective-permute-start.7 = (bf16[32,2048]{1,0:T(8,128)(2,1)S(1)}, bf16[32,2048]{1,0:T(8,128)(2,1)S(1)}, u32[]{:S(2)}, u32[]{:S(2)}) collective-permute-start(bf16[32,2048]{1,0:T(8,128)(2,1)S(1)} %get-tuple-element.48), channel_id=1, source_target_pairs={{0,12},{4,8},{8,4},{12,0},{16,28},{20,24},{24,20},{28,16},{1,13},{... | collective-permute-start | bytes 393224 | tf_op jit(solution)/shard_map/ppermute | solution.py:294
  66.0 5.6 %collective-permute-start.23 = (bf16[32,2048]{1,0:T(8,128)(2,1)S(1)}, bf16[32,2048]{1,0:T(8,128)(2,1)S(1)}, u32[]{:S(2)}, u32[]{:S(2)}) collective-permute-start(bf16[32,2048]{1,0:T(8,128)(2,1)S(1)} %shard_map.64), channel_id=1, source_target_pairs={{0,2},{1,3},{2,0},{3,1},{4,6},{5,7},{6,4},{7,5},{8,10},{9,11},{10,... | collective-permute-start | bytes 393224 | tf_op jit(solution)/shard_map/ppermute | solution.py:294
